TPU v7x, 32 devices: a whole 2x2x4 slice. The times are simulated.
32 devices in a mesh: section: 4 (over x, core), ctx: 8 (over z, y).
Axes of the slice: x: 2, y: 2, z: 4, core: 2. Of those that a mesh axis runs over, the one named last changes fastest.
Arguments:
- block_order: int32 [8], replicated, may hold values from 0 to 7, each once
- queries: bfloat16 [4, 64, 2560], P('section', 'ctx'), may hold values from -400 to 400
- cache_keys: bfloat16 [1024, 2560], P('ctx', 'section'), may hold values from -6 to 6
- cache_values: bfloat16 [1024, 2560], P('ctx', 'section'), may hold values from -6 to 6
- attention_out: bfloat16 [4, 64, 2560], P('section', 'ctx'), may hold values from -6 to 6
- output_grad: bfloat16 [4, 64, 2560], P('section', 'ctx'), may hold values from -192 to 192
Outputs:
- grad_queries: bfloat16 [4, 64, 2560], P('section', 'ctx')
- grad_keys: bfloat16 [1024, 2560], P('ctx', 'section')
- grad_values: bfloat16 [1024, 2560], P('ctx', 'section')
Inputs may be any that keep to these rules, and one draw needn't show every extreme that they name: `block_order`: every block number once.
All inputs are finite; a program needn't handle non-finite values.
Results may differ from a plain program's by a relative error of at most 0.012.
Values may be sent and summed in bfloat16 or wider, within the bound.
No kernel may reach another device: no remote copies, remote signals or barrier semaphores. Data moves between devices by JAX's collectives and lax.ppermute only.
A program may use at most 64 MiB of HBM per device.

v0:
```python
import jax
import jax.numpy as jnp
from jax import lax
from jax.sharding import PartitionSpec as P

HEADS = 20
HEAD_DIM = 128


masked_score = -1e30


def local(block_order, queries, cache_keys, cache_values, attention_out, output_grad):
    ctx_count = lax.axis_size("ctx")
    rows_here = queries.shape[1]
    key_count = cache_keys.shape[0]
    key_total = key_count * ctx_count
    query_count = rows_here * ctx_count
    scaling = HEAD_DIM ** (-0.5)
    product = output_grad.astype(jnp.float32) * attention_out.astype(jnp.float32)
    delta_terms = jnp.sum(product.reshape(1, rows_here, HEADS, HEAD_DIM), axis=3)
    query_part, grad_part, delta_part = (queries, output_grad, delta_terms)
    key_block, value_block = (
        lax.all_gather(cache_keys, "section", axis=1, tiled=True),
        lax.all_gather(cache_values, "section", axis=1, tiled=True),
    )
    group_heads = HEADS
    layers = query_part.shape[0]
    pair_count = layers * group_heads
    query_all, grad_all = (
        lax.all_gather(query_part, "ctx", axis=1, tiled=True),
        lax.all_gather(grad_part, "ctx", axis=1, tiled=True),
    )
    delta_all = lax.all_gather(delta_part, "ctx", axis=1, tiled=True)

    def split_heads(values):
        return (
            values.reshape(layers, query_count, group_heads, HEAD_DIM)
            .transpose(0, 2, 1, 3)
            .reshape(pair_count, query_count, HEAD_DIM)
        )

    query_heads = split_heads(query_all)
    grad_heads = split_heads(grad_all)
    delta_heads = delta_all.transpose(0, 2, 1).reshape(pair_count, query_count)
    key_heads = key_block.reshape(key_count, group_heads, HEAD_DIM).transpose(1, 0, 2)
    value_heads = value_block.reshape(key_count, group_heads, HEAD_DIM).transpose(1, 0, 2)
    head_ids = jnp.arange(pair_count, dtype=jnp.int32) % group_heads
    ctx_index = lax.axis_index("ctx")
    key_pos = block_order[ctx_index] * key_count + jnp.arange(key_count, dtype=jnp.int32)
    query_pos = key_total - query_count + jnp.arange(query_count, dtype=jnp.int32)
    visible = key_pos[None, :] <= query_pos[:, None]

    def masked_scores(query_head, head_index):
        scores = (
            jnp.dot(query_head, key_heads[head_index].T, preferred_element_type=jnp.float32)
            * scaling
        )
        return jnp.where(visible, scores, masked_score)

    def local_stats(packed):
        query_head, head_index = packed
        scores = masked_scores(query_head, head_index)
        row_max = jnp.max(scores, axis=1)
        row_sum = jnp.sum(jnp.where(visible, jnp.exp(scores - row_max[:, None]), 0.0), axis=1)
        return (row_max, row_sum)

    row_max, row_sum = lax.map(local_stats, (query_heads, head_ids))
    peak_max = lax.pmax(row_max.astype(jnp.bfloat16), "ctx").astype(row_max.dtype)
    row_sum = lax.psum(row_sum * jnp.exp(row_max - peak_max), "ctx")
    row_max = peak_max
    log_total = row_max + jnp.log(row_sum)

    def gradients(packed):
        query_head, grad_head, delta_head, total_head, head_index = packed
        scores = masked_scores(query_head, head_index)
        prob = jnp.where(visible, jnp.exp(scores - total_head[:, None]), 0.0)
        prob_b = prob.astype(jnp.bfloat16)
        value_grad = jnp.dot(prob_b.T, grad_head, preferred_element_type=jnp.float32)
        prob_grad = jnp.dot(
            grad_head, value_heads[head_index].T, preferred_element_type=jnp.float32
        )
        score_grad = (prob * (prob_grad - delta_head[:, None]) * scaling).astype(jnp.bfloat16)
        query_grad = jnp.dot(score_grad, key_heads[head_index], preferred_element_type=jnp.float32)
        key_grad = jnp.dot(score_grad.T, query_head, preferred_element_type=jnp.float32)
        return (query_grad, key_grad, value_grad)

    query_grad, key_grad, value_grad = lax.map(
        gradients, (query_heads, grad_heads, delta_heads, log_total, head_ids)
    )
    query_layout = (
        query_grad.reshape(layers, group_heads, query_count, HEAD_DIM)
        .transpose(0, 2, 1, 3)
        .reshape(layers, query_count, group_heads * HEAD_DIM)
    )
    query_rows_sum = lax.psum_scatter(query_layout, "ctx", scatter_dimension=1, tiled=True)
    key_sum = (
        key_grad.reshape(layers, group_heads, key_count, HEAD_DIM)
        .sum(axis=0)
        .transpose(1, 0, 2)
        .reshape(key_count, group_heads * HEAD_DIM)
    )
    value_sum = (
        value_grad.reshape(layers, group_heads, key_count, HEAD_DIM)
        .sum(axis=0)
        .transpose(1, 0, 2)
        .reshape(key_count, group_heads * HEAD_DIM)
    )
    grad_queries = query_rows_sum.astype(jnp.bfloat16)
    key_part, value_part = (
        lax.psum_scatter(
            key_sum.astype(jnp.bfloat16), "section", scatter_dimension=1, tiled=True
        ).astype(jnp.float32),
        lax.psum_scatter(
            value_sum.astype(jnp.bfloat16), "section", scatter_dimension=1, tiled=True
        ).astype(jnp.float32),
    )
    grad_keys = key_part.astype(jnp.bfloat16)
    grad_values = value_part.astype(jnp.bfloat16)
    return (grad_queries, grad_keys, grad_values)


def solution(mesh):
    in_specs = (
        P(),
        P("section", "ctx", None),
        P("ctx", "section"),
        P("ctx", "section"),
        P("section", "ctx", None),
        P("section", "ctx", None),
    )
    out_specs = (P("section", "ctx", None), P("ctx", "section"), P("ctx", "section"))
    return jax.shard_map(local, mesh=mesh, in_specs=in_specs, out_specs=out_specs, check_vma=False)
```

profile of v0, /device:TPU:0, one launch (start us, length us, event | category | flops | bytes accessed | tf_op | source)
XLA Modules:
  0.0 449.6 jit_solution(16274756989076429292)
XLA Ops:
  9.2 33.0 %all_gather.17 = bf16[1,64,2560]{2,1,0:T(8,128)(2,1)S(1)} all-gather(bf16[1,8,2560]{2,1,0:T(8,128)(2,1)} %param.15), channel_id=1, replica_groups=mesh['section'=4,'ctx'=8] {'ctx'}, dimensions={1}, use_global_device_ids=true | all-gather | bytes 368640 | tf_op jit(solution)/shard_map/all_gather | solution.py:32
  42.4 30.6 %all-gather = f32[64,20]{1,0:T(8,128)S(1)} all-gather(f32[8,20]{1,0:T(8,128)S(1)} %copy.43), channel_id=2, replica_groups=mesh['section'=4,'ctx'=8] {'ctx'}, dimensions={0}, use_global_device_ids=true | all-gather | bytes 5760 | tf_op jit(solution)/shard_map/all_gather | solution.py:34
  74.8 30.8 %all_gather.15 = bf16[1,64,2560]{2,1,0:T(8,128)(2,1)S(1)} all-gather(bf16[1,8,2560]{2,1,0:T(8,128)(2,1)S(1)} %copy-done.4), channel_id=1, replica_groups=mesh['section'=4,'ctx'=8] {'ctx'}, dimensions={1}, use_global_device_ids=true | all-gather | bytes 368640 | tf_op jit(solution)/shard_map/all_gather | solution.py:31
  106.2 7.9 %all_gather.18 = bf16[128,2560]{0,1:T(8,128)(2,1)S(1)} all-gather(bf16[128,640]{0,1:T(8,128)(2,1)S(1)} %copy.42), channel_id=1, replica_groups=mesh['section'=4,'ctx'=8] {'section'}, dimensions={1}, use_global_device_ids=true | all-gather | bytes 819200 | tf_op jit(solution)/shard_map/all_gather | solution.py:25
  114.1 8.0 %all_gather.16 = bf16[128,2560]{0,1:T(8,128)(2,1)S(1)} all-gather(bf16[128,640]{0,1:T(8,128)(2,1)S(1)} %copy.39), channel_id=1, replica_groups=mesh['section'=4,'ctx'=8] {'section'}, dimensions={1}, use_global_device_ids=true | all-gather | bytes 819200 | tf_op jit(solution)/shard_map/all_gather | solution.py:24
  122.4 61.5 %while.28 = (s32[]{:T(128)}, f32[20,64]{1,0:T(8,128)S(1)}, f32[20,64]{1,0:T(8,128)S(1)}, bf16[20,64,128]{2,1,0:T(8,128)(2,1)S(1)}, s32[20]{0:T(128)S(1)}, /*inde...) while((s32[]{:T(128)}, f32[20,64]{1,0:T(8,128)S(1)}, ...), condition=%wide.region_4.5_spmd.clone, body=%wide.region_1.4_spmd.clone.sunk | while | flops 2162565 | bytes 118451 | solution.py:68
  184.0 21.7 %pmax.7 = bf16[20,64]{1,0:T(8,128)(2,1)S(1)} all-reduce(bf16[20,64]{1,0:T(8,128)(2,1)S(1)} %convert_element_type.43), channel_id=1, replica_groups=mesh['section'=4,'ctx'=8] {'ctx'}, use_global_device_ids=true, to_apply=%region_5.6 | all-reduce | flops 1280 | bytes 5120 | tf_op jit(solution)/shard_map/pmax | solution.py:69
  205.7 33.0 %psum.7 = f32[20,64]{1,0:T(8,128)S(1)} all-reduce(f32[20,64]{1,0:T(8,128)S(1)} %fusion.44), channel_id=1, replica_groups=mesh['section'=4,'ctx'=8] {'ctx'}, use_global_device_ids=true, to_apply=%region_6.7 | all-reduce | flops 1280 | bytes 10240 | tf_op jit(solution)/shard_map/psum | solution.py:70
  238.7 92.9 %while.29 = (s32[]{:T(128)}, f32[20,64,128]{2,1,0:T(8,128)S(1)}, bf16[20,128,128]{1,2,0:T(8,128)(2,1)}, bf16[20,128,128]{1,2,0:T(8,128)(2,1)}, bf16[20,64,128]{2...) while((s32[]{:T(128)}, f32[20,64,128]{2,1,0:T(8,128)S(1)}, ...), condition=%wide.region_8.9_spmd.clone, body=%wide.region_7.8_spmd.clone.sunk | while | flops 10567685 | bytes 480487 | solution.py:88
  246.2 0.9 fusion.84
  255.4 0.9 fusion.84
  264.7 0.9 fusion.84
  274.0 0.9 fusion.84
  287.9 0.9 fusion.84
  292.6 0.9 fusion.84
  311.2 0.9 fusion.84
  329.7 0.9 fusion.84
  332.4 0.9 copy_bitcast_fusion
  333.3 17.2 %reduce-scatter.8.cloned.1.call-done = bf16[128,640]{0,1:T(8,128)(2,1)} async-done(((bf16[128,2560]{0,1:T(8,128)(2,1)}), bf16[128,640]{0,1:T(8,128)(2,1)}) %reduce-scatter.8.cloned.1.call-update) | async-done | bytes 163856 | tf_op jit(solution)/shard_map/reduce_scatter | solution.py:114
  350.5 1.7 copy.53
  352.2 23.3 %reduce-scatter.6.cloned.1.call-done = bf16[128,640]{0,1:T(8,128)(2,1)} async-done(((bf16[128,2560]{0,1:T(8,128)(2,1)}), bf16[128,640]{0,1:T(8,128)(2,1)}) %reduce-scatter.6.cloned.1.call-update) | async-done | bytes 163856 | tf_op jit(solution)/shard_map/reduce_scatter | solution.py:111
  375.5 1.7 copy.52
  377.2 64.4 %reduce-scatter.4.cloned.1.call-done = f32[1,8,2560]{2,1,0:T(8,128)} async-done(((f32[1,64,2560]{2,1,0:T(8,128)}), f32[1,8,2560]{2,1,0:T(8,128)}) %reduce-scatter.4.cloned.1.call-update) | async-done | bytes 81936 | tf_op jit(solution)/shard_map/reduce_scatter | solution.py:96
  441.6 1.5 convert_element_type.47
  (273 shorter events, 73.8 us)
Async XLA Ops:
  7.2 343.3 %reduce-scatter.8.cloned.1.call-start = ((), (), s32[]{:S(2)}) async-start(), calls=%async_computation.5 | async-start | bytes 819200 | tf_op jit(solution)/shard_map/reduce_scatter | solution.py:114
  7.3 0.7 copy-start.5
  9.2 33.0 %copy-start.2 = (bf16[1,8,2560]{2,1,0:T(8,128)(2,1)S(1)}, bf16[1,8,2560]{2,1,0:T(8,128)(2,1)}, u32[]{:S(2)}) copy-start(bf16[1,8,2560]{2,1,0:T(8,128)(2,1)} %param.15) | copy-start | bytes 122884
  9.2 33.0 %copy-start.3 = (bf16[1,8,2560]{2,1,0:T(8,128)(2,1)S(1)}, bf16[1,8,2560]{2,1,0:T(8,128)(2,1)}, u32[]{:S(2)}) copy-start(bf16[1,8,2560]{2,1,0:T(8,128)(2,1)} %param.14) | copy-start | bytes 122884
  42.2 30.9 %copy-start = (bf16[128,640]{1,0:T(8,128)(2,1)S(1)}, bf16[128,640]{1,0:T(8,128)(2,1)}, u32[]{:S(2)}) copy-start(bf16[128,640]{1,0:T(8,128)(2,1)} %param.12) | copy-start | bytes 491524
  73.1 0.9 copy-start.1
  74.0 0.8 copy-start.4
  331.6 43.9 %reduce-scatter.6.cloned.1.call-start = ((), (), s32[]{:S(2)}) async-start(), calls=%async_computation.4 | async-start | bytes 819200 | tf_op jit(solution)/shard_map/reduce_scatter | solution.py:111
  332.4 109.2 %reduce-scatter.4.cloned.1.call-start = ((), (), s32[]{:S(2)}) async-start(), calls=%async_computation.3 | async-start | bytes 737280 | tf_op jit(solution)/shard_map/reduce_scatter | solution.py:96
Sparse Core Ops, SparseCore 0:
  331.7 18.7 reduce-scatter.7
  353.0 22.4 reduce-scatter.5
  378.8 62.7 reduce-scatter.3
where the time goes:
time: 451 us; the launch traced here: 450 us
  blocking collectives  165 us (37%)
  waiting for transfers between devices  106 us (24%)
  loops' own time  78.6 us (17%)
  matrix products  46.9 us (10%)
  local copies, waits for them, and re-layouts  33.4 us (7%)
  between operations  14.6 us (3%)
  other arithmetic  5.47 us (1%)
    reduce_scatter x1, waiting for transfers between devices, local(): lax.psum_scatter(query_layout, 'ctx', scatter_dimension=1, tiled=True)  64.4 us
    another operation x1, loops' own time, local(): row_max, row_sum = lax.map(local_stats, (query_heads, head_ids))  39.3 us
    another operation x1, loops' own time, local(): lax.map(gradients, (query_heads, grad_heads, delta_heads, log_total, head...  39.3 us
    all_gather x1, blocking collectives, local(): lax.all_gather(grad_part, 'ctx', axis=1, tiled=True)  33 us
    psum x1, blocking collectives, local(): row_sum = lax.psum(row_sum * jnp.exp(row_max - peak_max), 'ctx')  33 us
    all_gather x1, blocking collectives, local(): lax.all_gather(query_part, 'ctx', axis=1, tiled=True)  30.8 us
    all_gather x1, blocking collectives, local(): delta_all = lax.all_gather(delta_part, 'ctx', axis=1, tiled=True)  30.6 us
    dynamic_slice x40, local copies, waits for them, and re-layouts, local(): row_max, row_sum = lax.map(local_stats, (query_heads, head_ids))  23.4 us
  transfers between devices with their start and end apart: 3, of which 3 were waited for; matrix products, arithmetic and copies ran while one was open for 1% of the time, Pallas kernels for 0%

commit v1 on v0

v1 whole, which is shorter than its diff:
```python
import jax
import jax.numpy as jnp
from jax import lax
from jax.experimental import pallas as pl
from jax.experimental.pallas import tpu as pltpu
from jax.sharding import PartitionSpec as P

HEAD_DIM = 128
LANES = 128
masked_score = -1e30
BF = jnp.bfloat16
F32 = jnp.float32


def nt(a, b):
    return lax.dot_general(a, b, (((1,), (1,)), ((), ())), preferred_element_type=F32)


def nn(a, b):
    return lax.dot_general(a, b, (((1,), (0,)), ((), ())), preferred_element_type=F32)


def tn(a, b):
    return lax.dot_general(a, b, (((0,), (0,)), ((), ())), preferred_element_type=F32)


def split3(x):
    hi = x.astype(BF)
    rest = x - hi.astype(F32)
    mid = rest.astype(BF)
    low = (rest - mid.astype(F32)).astype(BF)
    return hi, mid, low


def pack(queries, grads, outs, sections, copies):
    rows, features = queries.shape
    here = features // sections
    heads = here // HEAD_DIM
    width = 2 * here + LANES

    def body(q_ref, g_ref, o_ref, out_ref):
        lane = lax.broadcasted_iota(jnp.int32, (rows, LANES), 1)
        for s in range(sections):
            extra = jnp.zeros((rows, LANES), F32)
            for h in range(heads):
                at = pl.ds(s * here + h * HEAD_DIM, HEAD_DIM)
                terms = g_ref[:, at].astype(F32) * o_ref[:, at].astype(F32)
                delta = jnp.sum(terms, axis=1, keepdims=True)
                for part, value in enumerate(split3(delta)):
                    extra = jnp.where(lane == part * heads + h, value.astype(F32), extra)
            q = q_ref[:, pl.ds(s * here, here)]
            g = g_ref[:, pl.ds(s * here, here)]
            e = extra.astype(BF)

            @pl.loop(0, copies)
            def _(c):
                out_ref[s, c, :, pl.ds(0, here)] = q
                out_ref[s, c, :, pl.ds(here, here)] = g
                out_ref[s, c, :, pl.ds(2 * here, LANES)] = e

    return pl.pallas_call(
        body,
        out_shape=jax.ShapeDtypeStruct((sections, copies, rows, width), BF),
        name="pack",
    )(queries, grads, outs)


def visible_of(start_ref, shape, row_count, key_total):
    key_pos = start_ref[0] + lax.broadcasted_iota(jnp.int32, shape, 0)
    row = lax.broadcasted_iota(jnp.int32, shape, 1) % row_count
    return key_pos <= key_total - row_count + row


def stats_kernel(start, packed, keys, row_count, key_total, heads):
    m = packed.shape[0]
    key_count = keys.shape[0]
    scaling = HEAD_DIM ** (-0.5)

    def body(start_ref, q_ref, k_ref, out_ref):
        h = pl.program_id(0)
        shape = (key_count, m)
        visible = visible_of(start_ref, shape, row_count, key_total)
        s = jnp.where(visible, nt(k_ref[...], q_ref[...]) * scaling, masked_score)
        top = jnp.max(s, axis=0, keepdims=True)
        total = jnp.sum(jnp.where(visible, jnp.exp(s - top), 0.0), axis=0, keepdims=True)

        @pl.when(h == 0)
        def _():
            out_ref[...] = jnp.ones_like(out_ref)

        out_ref[0, pl.ds(h, 1), :] = top
        out_ref[1, pl.ds(h, 1), :] = total

    return pl.pallas_call(
        body,
        grid_spec=pltpu.PrefetchScalarGridSpec(
            num_scalar_prefetch=1,
            grid=(heads,),
            in_specs=[
                pl.BlockSpec((m, HEAD_DIM), lambda h, s: (0, h)),
                pl.BlockSpec((key_count, HEAD_DIM), lambda h, s: (0, h)),
            ],
            out_specs=pl.BlockSpec((2, 8, m), lambda h, s: (0, 0, 0)),
        ),
        out_shape=jax.ShapeDtypeStruct((2, 8, m), F32),
        name="stats",
    )(start, packed, keys)


def gradient_kernel(start, packed, keys, values, log_total, row_count, key_total, heads):
    m = packed.shape[0]
    key_count, here = keys.shape
    scaling = HEAD_DIM ** (-0.5)

    def body(start_ref, q_ref, g_ref, e_ref, k_ref, v_ref, l_ref, u_ref, dk_ref, dv_ref):
        h = pl.program_id(0)
        shape = (key_count, m)
        visible = visible_of(start_ref, shape, row_count, key_total)
        q, g, k, v = q_ref[...], g_ref[...], k_ref[...], v_ref[...]
        lane = lax.broadcasted_iota(jnp.int32, (8, LANES), 1)
        pick = (lane == h) | (lane == heads + h) | (lane == 2 * heads + h)
        delta = nt(jnp.where(pick, 1.0, 0.0).astype(BF), e_ref[...])[0:1, :]
        s = nt(k, q) * scaling
        prob = jnp.where(visible, jnp.exp(s - l_ref[pl.ds(h, 1), :]), 0.0)
        ds = (prob * (nt(v, g) - delta) * scaling).astype(BF)
        dv_ref[...] = nn(prob.astype(BF), g).astype(BF)
        dk_ref[...] = nn(ds, q).astype(BF)
        u_ref[...] = tn(ds, k).astype(BF)

    return pl.pallas_call(
        body,
        grid_spec=pltpu.PrefetchScalarGridSpec(
            num_scalar_prefetch=1,
            grid=(heads,),
            in_specs=[
                pl.BlockSpec((m, HEAD_DIM), lambda h, s: (0, h)),
                pl.BlockSpec((m, HEAD_DIM), lambda h, s: (0, heads + h)),
                pl.BlockSpec((m, LANES), lambda h, s: (0, 2 * heads)),
                pl.BlockSpec((key_count, HEAD_DIM), lambda h, s: (0, h)),
                pl.BlockSpec((key_count, HEAD_DIM), lambda h, s: (0, h)),
                pl.BlockSpec((8, m), lambda h, s: (0, 0)),
            ],
            out_specs=[
                pl.BlockSpec((m, HEAD_DIM), lambda h, s: (0, h)),
                pl.BlockSpec((key_count, HEAD_DIM), lambda h, s: (0, h)),
                pl.BlockSpec((key_count, HEAD_DIM), lambda h, s: (0, h)),
            ],
        ),
        out_shape=[
            jax.ShapeDtypeStruct((m, here), BF),
            jax.ShapeDtypeStruct((key_count, here), BF),
            jax.ShapeDtypeStruct((key_count, here), BF),
        ],
        name="gradients",
    )(start, packed, packed, packed, keys, values, log_total)


def merge_stats(stats, axis, count):
    step = count // 2
    while step:
        other = lax.ppermute(stats, axis, [(i, i ^ step) for i in range(count)])
        top = jnp.maximum(stats[0], other[0])
        total = stats[1] * jnp.exp(stats[0] - top) + other[1] * jnp.exp(other[0] - top)
        stats = jnp.stack([top, total])
        step //= 2
    return stats


def local(block_order, queries, cache_keys, cache_values, attention_out, output_grad):
    sections = lax.axis_size("section")
    ctx_count = lax.axis_size("ctx")
    assert ctx_count & (ctx_count - 1) == 0
    layers, rows, features = queries.shape
    assert layers == 1
    key_count, here = cache_keys.shape
    heads = here // HEAD_DIM
    row_count = rows * ctx_count
    key_total = key_count * ctx_count
    start = (block_order[lax.axis_index("ctx")] * key_count).reshape(1)

    sent = pack(queries[0], output_grad[0], attention_out[0], sections, ctx_count)
    width = sent.shape[-1]
    sent = sent.reshape(sections * ctx_count, rows, width)
    packed = lax.all_to_all(sent, ("section", "ctx"), 0, 0, tiled=True)
    packed = packed.reshape(sections * row_count, width)

    stats = stats_kernel(start, packed, cache_keys, row_count, key_total, heads)
    stats = merge_stats(stats, "ctx", ctx_count)
    log_total = stats[0] + jnp.log(stats[1])
    part, grad_keys, grad_values = gradient_kernel(
        start, packed, cache_keys, cache_values, log_total, row_count, key_total, heads
    )
    part = part.reshape(sections * ctx_count, rows, here)
    part = lax.all_to_all(part, ("section", "ctx"), 0, 0, tiled=True)
    part = part.reshape(sections, ctx_count, rows, here).astype(F32).sum(axis=1)
    grad_queries = part.transpose(1, 0, 2).reshape(1, rows, features).astype(BF)
    return (grad_queries, grad_keys, grad_values)


def solution(mesh):
    in_specs = (
        P(),
        P("section", "ctx", None),
        P("ctx", "section"),
        P("ctx", "section"),
        P("section", "ctx", None),
        P("section", "ctx", None),
    )
    out_specs = (P("section", "ctx", None), P("ctx", "section"), P("ctx", "section"))
    return jax.shard_map(local, mesh=mesh, in_specs=in_specs, out_specs=out_specs, check_vma=False)
```

time: 451 us -> 70 us (0.16)
  blocking collectives: 165 us -> 14.6 us
  loops' own time: 78.6 us -> 0 us
  waiting for transfers between devices: 106 us -> 29.3 us
  matrix products: 46.9 us -> 0 us
  local copies, waits for them, and re-layouts: 33.4 us -> 2.1 us
  between operations: 14.6 us -> 1.34 us
  Pallas kernels: 0 us -> 10.8 us
  starting transfers between devices: 0.12 us -> 9.04 us
    all_gather x5 -> x0, blocking collectives: 110 us -> none  [the longest x1 33 us: local(): lax.all_gather(grad_part, 'ctx', axis=1, tiled=True)]
    reduce_scatter x3 -> x0, waiting for transfers between devices: 105 us -> none  [the longest x1 64.4 us: local(): lax.psum_scatter(query_layout, 'ctx', scatter_dimension=1, tiled=True)]
    another operation x2 -> x0, loops' own time: 78.6 us -> none  [the longest x1 39.3 us: local(): row_max, row_sum = lax.map(local_stats, (query_heads, head_ids))]
    dot_general x120 -> x0, matrix products: 46.9 us -> none  [the longest x20 17.5 us: gradients(): jnp.dot(prob_b.T, grad_head, preferred_element_type=jnp.float32)]
    psum x1 -> x0, blocking collectives: 33 us -> none  [local(): row_sum = lax.psum(row_sum * jnp.exp(row_max - peak_max), 'ctx')]
    dynamic_slice x41 -> x1, local copies, waits for them, and re-layouts: 24 us -> 0.58 us  [local(): start = (block_order[lax.axis_index('ctx')] * key_count).reshape(1)]
    pmax x1 -> x0, blocking collectives: 21.7 us -> none  [local(): lax.pmax(row_max.astype(jnp.bfloat16), 'ctx').astype(row_max.dtype)]
    all_to_all x0 -> x1, waiting for transfers between devices: none -> 18.6 us  [local(): packed = lax.all_to_all(sent, ('section', 'ctx'), 0, 0, tiled=True)]
  transfers between devices with their start and end apart: 3 -> 4, of which waited for: 3 -> 4; matrix products, arithmetic and copies ran while one was open for 1% -> 1% of each run, Pallas kernels for 0% -> 0%
where the time goes in v1:
time: 70 us; the launch traced here: 69.2 us
  waiting for transfers between devices  29.3 us (42%)
  blocking collectives  14.6 us (21%)
  Pallas kernels  10.8 us (15%)
  starting transfers between devices  9.04 us (13%)
  local copies, waits for them, and re-layouts  2.1 us (3%)
  other arithmetic  2.03 us (3%)
  between operations  1.34 us (2%)
    all_to_all x1, waiting for transfers between devices, local(): packed = lax.all_to_all(sent, ('section', 'ctx'), 0, 0, tiled=True)  18.6 us
    all_to_all x1, blocking collectives, local(): part = lax.all_to_all(part, ('section', 'ctx'), 0, 0, tiled=True)  14.6 us
    ppermute x3, waiting for transfers between devices, merge_stats(): other = lax.ppermute(stats, axis, [(i, i ^ step) for i in range(count)])  10.8 us
    all_to_all x1, starting transfers between devices, local(): packed = lax.all_to_all(sent, ('section', 'ctx'), 0, 0, tiled=True)  7.33 us
    pallas_call x1, Pallas kernels, gradient_kernel(): pl.pallas_call(body, grid_spec=pltpu.PrefetchScalarGridSpec(num_scalar_pr...  4.77 us
    pallas_call x1, Pallas kernels, stats_kernel(): pl.pallas_call(body, grid_spec=pltpu.PrefetchScalarGridSpec(num_scalar_pr...  3.81 us
    pallas_call x1, Pallas kernels, pack(): pl.pallas_call(body, out_shape=jax.ShapeDtypeStruct((sections, copies, ro...  2.21 us
    ppermute x3, starting transfers between devices, merge_stats(): other = lax.ppermute(stats, axis, [(i, i ^ step) for i in range(count)])  1.71 us
  transfers between devices with their start and end apart: 4, of which 4 were waited for; matrix products, arithmetic and copies ran while one was open for 1% of the time, Pallas kernels for 0%

profile of v1, /device:TPU:0, one launch (start us, length us, event | category | flops | bytes accessed | tf_op | source)
XLA Modules:
  0.0 69.2 jit_solution(10295435346357470006)
XLA Ops:
  0.6 2.2 %pack.1 = bf16[4,8,8,1408]{3,2,1,0:T(8,128)(2,1)} custom-call(bf16[8,2560]{1,0:T(8,128)(2,1)} %bitcast.102, bf16[8,2560]{1,0:T(8,128)(2,1)} %bitcast.103, bf16[8,2560]{1,0:T(8,128)(2,1)} %bitcast.104), custom_call_target="tpu_custom_call" | custom-call | tf_op jit(solution)/shard_map/pack/pallas_call | solution.py:61
  2.8 7.3 %all-to-all-start = ((bf16[32,8,1408]{2,1,0:T(8,128)(2,1)}), bf16[32,8,1408]{2,1,0:T(8,128)(2,1)S(1)}, u32[]{:S(2)}, u32[]{:S(2)}) async-start(bf16[32,8,1408]{2,1,0:T(8,128)(2,1)} %bitcast.100), calls=%async_computation | async-start | bytes 1441792 | tf_op jit(solution)/shard_map/all_to_all | solution.py:184
  10.2 0.0 copy-start.2
  10.2 0.6 copy-done.2
  10.8 0.6 dynamic_slice.3
  12.1 18.6 %all-to-all-done = bf16[32,8,1408]{2,1,0:T(8,128)(2,1)S(1)} async-done(((bf16[32,8,1408]{2,1,0:T(8,128)(2,1)}), bf16[32,8,1408]{2,1,0:T(8,128)(2,1)S(1)}, u32[]{:S(2)}, u32[]{:S(2)}) %all-to-all-start) | async-done | bytes 720928 | tf_op jit(solution)/shard_map/all_to_all | solution.py:184
  30.6 0.0 copy-start
  30.6 0.9 %copy-done = bf16[32,8,1408]{2,1,0:T(8,128)(2,1)} copy-done((bf16[32,8,1408]{2,1,0:T(8,128)(2,1)}, bf16[32,8,1408]{2,1,0:T(8,128)(2,1)S(1)}, u32[]{:S(2)}) %copy-start) | copy-done | bytes 720920
  31.5 3.8 %stats.1 = f32[2,8,256]{2,1,0:T(8,128)} custom-call(s32[1]{0:T(128)S(6)} %mul.36.start_ref, bf16[256,1408]{1,0:T(8,128)(2,1)} %bitcast.96, bf16[128,640]{1,0:T(8,128)(2,1)} %k_ref.3), custom_call_target="tpu_custom_call" | custom-call | tf_op jit(solution)/shard_map/stats/pallas_call | solution.py:94
  35.3 0.0 collective-permute-start
  35.3 4.9 %collective-permute-done = f32[2,8,256]{2,1,0:T(8,128)S(1)} collective-permute-done((f32[2,8,256]{2,1,0:T(8,128)}, f32[2,8,256]{2,1,0:T(8,128)S(1)}, u32[]{:S(2)}, u32[]{:S(2)}) %collective-permute-start) | collective-permute-done | bytes 16416 | tf_op jit(solution)/shard_map/ppermute | solution.py:161
  40.2 0.7 %multiply_add_fusion.1 = (f32[1,8,256]{2,1,0:T(8,128)S(1)}, f32[1,8,256]{2,1,0:T(8,128)S(1)}) fusion(f32[2,8,256]{2,1,0:T(8,128)S(1)} %collective-permute-done, f32[2,8,256]{2,1,0:T(8,128)} %stats.1), kind=kLoop, calls=%fused_computation.29 | loop fusion | flops 12288 | bytes 49152 | tf_op jit(solution)/shard_map/add | solution.py:163
  40.9 0.8 %collective-permute-start.1 = (f32[2,8,256]{2,1,0:T(8,128)S(1)}, f32[2,8,256]{2,1,0:T(8,128)S(1)}, u32[]{:S(2)}, u32[]{:S(2)}) collective-permute-start(f32[2,8,256]{2,1,0:T(8,128)S(1)} %pad_maximum_fusion), channel_id=1, source_target_pairs={{0,2},{1,3},{2,0},{3,1},{4,6},{5,7},{6,4},{7,5},{8,10},{9,11},{10,... | collective-permute-start | bytes 49160 | tf_op jit(solution)/shard_map/ppermute | solution.py:161
  41.7 3.0 %collective-permute-done.1 = f32[2,8,256]{2,1,0:T(8,128)S(1)} collective-permute-done((f32[2,8,256]{2,1,0:T(8,128)S(1)}, f32[2,8,256]{2,1,0:T(8,128)S(1)}, u32[]{:S(2)}, u32[]{:S(2)}) %collective-permute-start.1) | collective-permute-done | bytes 16416 | tf_op jit(solution)/shard_map/ppermute | solution.py:161
  44.7 0.0 copy-start.1
  44.7 0.9 %collective-permute-start.2 = (f32[2,8,256]{2,1,0:T(8,128)S(1)}, f32[2,8,256]{2,1,0:T(8,128)S(1)}, u32[]{:S(2)}, u32[]{:S(2)}) collective-permute-start(f32[2,8,256]{2,1,0:T(8,128)S(1)} %pad_maximum_fusion.1), channel_id=1, source_target_pairs={{0,1},{1,0},{2,3},{3,2},{4,5},{5,4},{6,7},{7,6},{8,9},{9,8},{10,11... | collective-permute-start | bytes 49160 | tf_op jit(solution)/shard_map/ppermute | solution.py:161
  45.7 2.9 %collective-permute-done.2 = f32[2,8,256]{2,1,0:T(8,128)S(1)} collective-permute-done((f32[2,8,256]{2,1,0:T(8,128)S(1)}, f32[2,8,256]{2,1,0:T(8,128)S(1)}, u32[]{:S(2)}, u32[]{:S(2)}) %collective-permute-start.2) | collective-permute-done | bytes 16416 | tf_op jit(solution)/shard_map/ppermute | solution.py:161
  48.5 0.0 copy-done.1
  48.5 0.6 fusion.3.l_ref
  49.2 4.8 %gradients.1 = (bf16[256,640]{1,0:T(8,128)(2,1)}, bf16[128,640]{1,0:T(8,128)(2,1)}, bf16[128,640]{1,0:T(8,128)(2,1)}) custom-call(s32[1]{0:T(128)S(6)} %mul.36.start_ref, bf16[256,1408]{1,0:T(8,128)(2,1)} %bitcast.97, bf16[256,1408]{1,0:T(8,128)(2,1)} %bitcast.98, bf16[256,1408]{1,0:T(8,128)(2,1)} %bitcast.99, bf16[128,640]{1,0:T(8,128)(2,1)} %k_ref.3, ...), custom_call_target="tpu_custom_call" | custom-call | tf_op jit(solution)/shard_map/gradients/pallas_call | solution.py:130
  53.9 14.6 %all_to_all.10 = bf16[32,8,640]{2,1,0:T(8,128)(2,1)S(1)} all-to-all(bf16[32,8,640]{2,1,0:T(8,128)(2,1)} %bitcast.101), channel_id=1, replica_groups=mesh['section'=4,'ctx'=8] {'section','ctx'}, dimensions={0} | all-to-all | bytes 655360 | tf_op jit(solution)/shard_map/all_to_all | solution.py:194
  68.6 0.7 bitcast_reduce_fusion
  (3 shorter events, 0.0 us)
Async XLA Ops:
  2.8 27.8 %all-to-all-start = ((bf16[32,8,1408]{2,1,0:T(8,128)(2,1)}), bf16[32,8,1408]{2,1,0:T(8,128)(2,1)S(1)}, u32[]{:S(2)}, u32[]{:S(2)}) async-start(bf16[32,8,1408]{2,1,0:T(8,128)(2,1)} %bitcast.100), calls=%async_computation | async-start | bytes 1441792 | tf_op jit(solution)/shard_map/all_to_all | solution.py:184
  10.2 0.7 copy-start.2
  30.6 0.9 %copy-start = (bf16[32,8,1408]{2,1,0:T(8,128)(2,1)}, bf16[32,8,1408]{2,1,0:T(8,128)(2,1)S(1)}, u32[]{:S(2)}) copy-start(bf16[32,8,1408]{2,1,0:T(8,128)(2,1)S(1)} %all-to-all-done) | copy-start | bytes 2162692
  35.3 4.9 %collective-permute-start = (f32[2,8,256]{2,1,0:T(8,128)}, f32[2,8,256]{2,1,0:T(8,128)S(1)}, u32[]{:S(2)}, u32[]{:S(2)}) collective-permute-start(f32[2,8,256]{2,1,0:T(8,128)} %stats.1), channel_id=1, source_target_pairs={{0,4},{1,5},{2,6},{3,7},{4,0},{5,1},{6,2},{7,3},{8,12},{9,13},{10,... | collective-permute-start | bytes 49160 | tf_op jit(solution)/shard_map/ppermute | solution.py:161
  40.9 3.8 %collective-permute-start.1 = (f32[2,8,256]{2,1,0:T(8,128)S(1)}, f32[2,8,256]{2,1,0:T(8,128)S(1)}, u32[]{:S(2)}, u32[]{:S(2)}) collective-permute-start(f32[2,8,256]{2,1,0:T(8,128)S(1)} %pad_maximum_fusion), channel_id=1, source_target_pairs={{0,2},{1,3},{2,0},{3,1},{4,6},{5,7},{6,4},{7,5},{8,10},{9,11},{10,... | collective-permute-start | bytes 49160 | tf_op jit(solution)/shard_map/ppermute | solution.py:161
  44.7 3.8 %copy-start.1 = (f32[2,8,256]{2,1,0:T(8,128)S(1)}, f32[2,8,256]{2,1,0:T(8,128)}, u32[]{:S(2)}) copy-start(f32[2,8,256]{2,1,0:T(8,128)} %stats.1) | copy-start | bytes 49156
  44.7 3.8 %collective-permute-start.2 = (f32[2,8,256]{2,1,0:T(8,128)S(1)}, f32[2,8,256]{2,1,0:T(8,128)S(1)}, u32[]{:S(2)}, u32[]{:S(2)}) collective-permute-start(f32[2,8,256]{2,1,0:T(8,128)S(1)} %pad_maximum_fusion.1), channel_id=1, source_target_pairs={{0,1},{1,0},{2,3},{3,2},{4,5},{5,4},{6,7},{7,6},{8,9},{9,8},{10,11... | collective-permute-start | bytes 49160 | tf_op jit(solution)/shard_map/ppermute | solution.py:161

commit v2 on v1

v2 whole, which is shorter than its diff:
```python
import jax
import jax.numpy as jnp
from jax import lax
from jax.experimental import pallas as pl
from jax.experimental.pallas import tpu as pltpu
from jax.sharding import PartitionSpec as P


HEAD_DIM = 128
LANES = 128
masked_score = -1e30
BF = jnp.bfloat16
F32 = jnp.float32


def nt(a, b):
    return lax.dot_general(a, b, (((1,), (1,)), ((), ())), preferred_element_type=F32)


def nn(a, b):
    return lax.dot_general(a, b, (((1,), (0,)), ((), ())), preferred_element_type=F32)


def tn(a, b):
    return lax.dot_general(a, b, (((0,), (0,)), ((), ())), preferred_element_type=F32)


def split3(x):
    hi = x.astype(BF)
    rest = x - hi.astype(F32)
    mid = rest.astype(BF)
    low = (rest - mid.astype(F32)).astype(BF)
    return hi, mid, low


def in_vmem(count):
    return [pl.BlockSpec(memory_space=pltpu.VMEM) for _ in range(count)]


def in_smem():
    return pl.BlockSpec(memory_space=pltpu.SMEM)


def head_of(h):
    return pl.ds(h * HEAD_DIM, HEAD_DIM)


def pack_grads(grads, outs, sections):
    rows, features = grads.shape
    here = features // sections
    heads = here // HEAD_DIM

    def body(g_ref, o_ref, out_ref):
        lane = lax.broadcasted_iota(jnp.int32, (rows, LANES), 1)
        for s in range(sections):
            extra = jnp.zeros((rows, LANES), F32)
            for h in range(heads):
                at = head_of(s * heads + h)
                terms = g_ref[:, at].astype(F32) * o_ref[:, at].astype(F32)
                delta = jnp.sum(terms, axis=1, keepdims=True)
                for part, value in enumerate(split3(delta)):
                    extra = jnp.where(lane == part * heads + h, value.astype(F32), extra)
            out_ref[s, :, pl.ds(0, here)] = g_ref[:, pl.ds(s * here, here)]
            out_ref[s, :, pl.ds(here, LANES)] = extra.astype(BF)

    return pl.pallas_call(
        body,
        in_specs=in_vmem(2),
        out_specs=in_vmem(1)[0],
        out_shape=jax.ShapeDtypeStruct((sections, rows, here + LANES), BF),
        name="pack_grads",
    )(grads, outs)


def visible_of(start_ref, shape, row_count, key_total):
    key_pos = start_ref[0] + lax.broadcasted_iota(jnp.int32, shape, 0)
    row = lax.broadcasted_iota(jnp.int32, shape, 1) % row_count
    return key_pos <= key_total - row_count + row


def stats_kernel(start, queries, keys, row_count, key_total):
    m, here = queries.shape
    key_count = keys.shape[0]
    heads = here // HEAD_DIM
    slots = -(-heads // 8) * 8
    scaling = HEAD_DIM ** (-0.5)

    def body(start_ref, q_ref, k_ref, out_ref):
        visible = visible_of(start_ref, (key_count, m), row_count, key_total)
        out_ref[...] = jnp.ones_like(out_ref)
        for h in range(heads):
            at = head_of(h)
            s = jnp.where(visible, nt(k_ref[:, at], q_ref[:, at]) * scaling, masked_score)
            top = jnp.max(s, axis=0, keepdims=True)
            total = jnp.sum(jnp.where(visible, jnp.exp(s - top), 0.0), axis=0, keepdims=True)
            out_ref[0, pl.ds(h, 1), :] = top
            out_ref[1, pl.ds(h, 1), :] = total

    return pl.pallas_call(
        body,
        in_specs=[in_smem(), *in_vmem(2)],
        out_specs=in_vmem(1)[0],
        out_shape=jax.ShapeDtypeStruct((2, slots, m), F32),
        name="stats",
    )(start, queries, keys)


def query_kernel(start, queries, grads, keys, values, stats, row_count, key_total):
    m = queries.shape[0]
    key_count, here = keys.shape
    heads = here // HEAD_DIM
    scaling = HEAD_DIM ** (-0.5)

    def body(start_ref, q_ref, g_ref, k_ref, v_ref, l_ref, u_ref, p_ref, ds_ref):
        visible = visible_of(start_ref, (key_count, m), row_count, key_total)
        extra = g_ref[:, pl.ds(here, LANES)]
        slot = lax.broadcasted_iota(jnp.int32, (l_ref.shape[1], LANES), 0)
        lane = lax.broadcasted_iota(jnp.int32, (l_ref.shape[1], LANES), 1)
        pick = (lane % heads == slot) & (lane < 3 * heads)
        delta = nt(jnp.where(pick, 1.0, 0.0).astype(BF), extra)
        log_total = l_ref[0] + jnp.log(l_ref[1])
        for h in range(heads):
            at = head_of(h)
            k = k_ref[:, at]
            s = nt(k, q_ref[:, at]) * scaling
            prob = jnp.where(visible, jnp.exp(s - log_total[h : h + 1, :]), 0.0)
            ds = prob * (nt(v_ref[:, at], g_ref[:, at]) - delta[h : h + 1, :]) * scaling
            ds = ds.astype(BF)
            u_ref[:, at] = tn(ds, k).astype(BF)
            p_ref[h] = prob.astype(BF)
            ds_ref[h] = ds

    return pl.pallas_call(
        body,
        in_specs=[in_smem(), *in_vmem(5)],
        out_specs=in_vmem(3),
        out_shape=[
            jax.ShapeDtypeStruct((m, here), BF),
            jax.ShapeDtypeStruct((heads, key_count, m), BF),
            jax.ShapeDtypeStruct((heads, key_count, m), BF),
        ],
        name="query_gradients",
    )(start, queries, grads, keys, values, stats)


def cache_kernel(queries, grads, probs, score_grads):
    here = queries.shape[1]
    heads, key_count, _ = probs.shape

    def body(q_ref, g_ref, p_ref, ds_ref, dk_ref, dv_ref):
        for h in range(heads):
            at = head_of(h)
            dk_ref[:, at] = nn(ds_ref[h], q_ref[:, at]).astype(BF)
            dv_ref[:, at] = nn(p_ref[h], g_ref[:, at]).astype(BF)

    return pl.pallas_call(
        body,
        in_specs=in_vmem(4),
        out_specs=in_vmem(2),
        out_shape=[jax.ShapeDtypeStruct((key_count, here), BF)] * 2,
        name="cache_gradients",
    )(queries, grads, probs, score_grads)


def merge_stats(stats, axis, count):
    step = count // 2
    while step:
        other = lax.ppermute(stats, axis, [(i, i ^ step) for i in range(count)])
        top = jnp.maximum(stats[0], other[0])
        total = stats[1] * jnp.exp(stats[0] - top) + other[1] * jnp.exp(other[0] - top)
        stats = jnp.stack([top, total])
        step //= 2
    return stats


def flip(value, axis, bit):
    count = lax.axis_size(axis)
    return lax.ppermute(value, axis, [(i, i ^ bit) for i in range(count)])


def ordered(mine, other, upper, axis):
    first = jnp.where(upper, other, mine)
    second = jnp.where(upper, mine, other)
    return jnp.stack([first, second], axis)


def swap_blocks(blocks, axis):
    count = lax.axis_size(axis)
    bits = count.bit_length() - 1
    rest = blocks.shape[1:]
    blocks = blocks.reshape((2,) * bits + rest)
    for i in range(bits):
        upper = (lax.axis_index(axis) >> i) % 2 == 1
        first = lax.index_in_dim(blocks, 0, bits - 1, keepdims=False)
        second = lax.index_in_dim(blocks, 1, bits - 1, keepdims=False)
        mine = jnp.where(upper, second, first)
        other = flip(jnp.where(upper, first, second), axis, 1 << i)
        blocks = ordered(mine, other, upper, 0)
    return blocks.reshape((count,) + rest)


def spread_blocks(blocks, axis):
    count = lax.axis_size(axis)
    bits = count.bit_length() - 1
    lead, rest = blocks.shape[0], blocks.shape[1:]
    for i in range(bits):
        bit = count >> (i + 1)
        upper = lax.axis_index(axis) & bit != 0
        blocks = ordered(blocks, flip(blocks, axis, bit), upper, i + 1)
    return blocks.reshape((lead, count) + rest)


def exchange(blocks):
    return lax.all_to_all(blocks, ("section", "ctx"), 0, 0, tiled=True)


def compute(block_order, queries, cache_keys, cache_values, attention_out, output_grad):
    sections = lax.axis_size("section")
    ctx_count = lax.axis_size("ctx")
    assert ctx_count & (ctx_count - 1) == 0
    assert sections & (sections - 1) == 0
    layers, rows, features = queries.shape
    assert layers == 1
    key_count, here = cache_keys.shape
    row_count = rows * ctx_count
    key_total = key_count * ctx_count
    peers = sections * ctx_count
    start = (block_order[lax.axis_index("ctx")] * key_count).reshape(1)

    sent = queries.reshape(rows, sections, here).transpose(1, 0, 2)[:, None]
    sent = jnp.broadcast_to(sent, (sections, ctx_count, rows, here))
    query_all = exchange(sent.reshape(peers, rows, here)).reshape(-1, here)

    sent = pack_grads(output_grad[0], attention_out[0], sections)
    sent = spread_blocks(swap_blocks(sent, "section"), "ctx")
    grad_all = sent.reshape(peers * rows, -1)

    stats = stats_kernel(start, query_all, cache_keys, row_count, key_total)
    stats = merge_stats(stats, "ctx", ctx_count)
    part, probs, score_grads = query_kernel(
        start, query_all, grad_all, cache_keys, cache_values, stats, row_count, key_total
    )
    part = exchange(part.reshape(peers, rows, here))
    grad_keys, grad_values = cache_kernel(query_all, grad_all, probs, score_grads)
    part = part.reshape(sections, ctx_count, rows, here).astype(F32).sum(axis=1)
    grad_queries = part.transpose(1, 0, 2).reshape(1, rows, features).astype(BF)
    return (grad_queries, grad_keys, grad_values)


def solution(mesh):
    in_specs = (
        P(),
        P("section", "ctx", None),
        P("ctx", "section"),
        P("ctx", "section"),
        P("section", "ctx", None),
        P("section", "ctx", None),
    )
    out_specs = (P("section", "ctx", None), P("ctx", "section"), P("ctx", "section"))
    return jax.shard_map(compute, mesh=mesh, in_specs=in_specs, out_specs=out_specs, check_vma=False)
```

time: 70 us -> 64.2 us (0.917)
  blocking collectives: 14.6 us -> 0 us
  starting transfers between devices: 9.04 us -> 20 us
  waiting for transfers between devices: 29.3 us -> 27.4 us
  Pallas kernels: 10.8 us -> 9.15 us
  other arithmetic: 2.03 us -> 3.05 us
    all_to_all x1 -> x0, blocking collectives: 14.6 us -> none  [local(): part = lax.all_to_all(part, ('section', 'ctx'), 0, 0, tiled=True)]
    ppermute x0 -> x5, starting transfers between devices: none -> 9.96 us  [flip(): return lax.ppermute(value, axis, [(i, i ^ bit) for i in range(count)])]
    ppermute x0 -> x5, waiting for transfers between devices: none -> 9.31 us  [flip(): return lax.ppermute(value, axis, [(i, i ^ bit) for i in range(count)])]
    all_to_all x1 -> x2, waiting for transfers between devices: 18.6 us -> 12.4 us  [exchange(): return lax.all_to_all(blocks, ('section', 'ctx'), 0, 0, tiled=True)]
    ppermute x3, waiting for transfers between devices: 10.8 us -> 5.69 us  [merge_stats(): other = lax.ppermute(stats, axis, [(i, i ^ step) for i in range(count)])]
    pallas_call x3 -> x4, Pallas kernels: 10.8 us -> 9.15 us  [the longest x1 3.27 us: query_kernel(): pl.pallas_call(body, in_specs=[in_smem(), *in_vmem(5)], out_specs=in_vmem...]
    ppermute x3, starting transfers between devices: 1.71 us -> 3.07 us  [merge_stats(): other = lax.ppermute(stats, axis, [(i, i ^ step) for i in range(count)])]
    another operation x0 -> x9, other arithmetic: none -> 0.92 us  [ordered(): return jnp.stack([first, second], axis)]
  transfers between devices with their start and end apart: 4 -> 10, of which waited for: 4 -> 9; matrix products, arithmetic and copies ran while one was open for 1% -> 4% of each run, Pallas kernels for 0% -> 4%
where the time goes in v2:
time: 64.2 us; the launch traced here: 63.7 us
  waiting for transfers between devices  27.4 us (43%)
  starting transfers between devices  20 us (31%)
  Pallas kernels  9.15 us (14%)
  other arithmetic  3.05 us (5%)
  local copies, waits for them, and re-layouts  2.73 us (4%)
  between operations  1.42 us (2%)
    all_to_all x2, waiting for transfers between devices, exchange(): return lax.all_to_all(blocks, ('section', 'ctx'), 0, 0, tiled=True)  12.4 us
    ppermute x5, starting transfers between devices, flip(): return lax.ppermute(value, axis, [(i, i ^ bit) for i in range(count)])  9.96 us
    ppermute x5, waiting for transfers between devices, flip(): return lax.ppermute(value, axis, [(i, i ^ bit) for i in range(count)])  9.31 us
    all_to_all x2, starting transfers between devices, exchange(): return lax.all_to_all(blocks, ('section', 'ctx'), 0, 0, tiled=True)  6.93 us
    ppermute x3, waiting for transfers between devices, merge_stats(): other = lax.ppermute(stats, axis, [(i, i ^ step) for i in range(count)])  5.69 us
    pallas_call x1, Pallas kernels, query_kernel(): pl.pallas_call(body, in_specs=[in_smem(), *in_vmem(5)], out_specs=in_vmem...  3.27 us
    ppermute x3, starting transfers between devices, merge_stats(): other = lax.ppermute(stats, axis, [(i, i ^ step) for i in range(count)])  3.07 us
    pallas_call x1, Pallas kernels, cache_kernel(): pl.pallas_call(body, in_specs=in_vmem(4), out_specs=in_vmem(2), out_shape...  2.33 us
  transfers between devices with their start and end apart: 10, of which 9 were waited for; matrix products, arithmetic and copies ran while one was open for 4% of the time, Pallas kernels for 4%

profile of v2, /device:TPU:0, one launch (start us, length us, event | category | flops | bytes accessed | tf_op | source)
XLA Modules:
  0.0 63.7 jit_solution(12489311821997239893)
XLA Ops:
  0.6 1.5 %pack_grads.1 = bf16[4,8,768]{2,1,0:T(8,128)(2,1)} custom-call(bf16[8,2560]{1,0:T(8,128)(2,1)} %bitcast.101, bf16[8,2560]{1,0:T(8,128)(2,1)} %bitcast.102), custom_call_target="tpu_custom_call" | custom-call | tf_op jit(solution)/shard_map/pack_grads/pallas_call | solution.py:66
  2.2 0.8 %fusion.4 = bf16[2,8,768]{2,1,0:T(8,128)(2,1)S(1)} fusion(pred[]{:T(512)S(6)} %eq.10, bf16[2,2,8,768]{3,2,1,0:T(8,128)(2,1)} %bitcast.97), kind=kLoop, calls=%fused_computation.22 | loop fusion | flops 12288 | bytes 73729 | tf_op jit(solution)/shard_map/jit(_where)/select_n | solution.py:197
  3.5 0.8 %collective-permute-done = bf16[2,8,768]{2,1,0:T(8,128)(2,1)S(1)} collective-permute-done((bf16[2,8,768]{2,1,0:T(8,128)(2,1)S(1)}, bf16[2,8,768]{2,1,0:T(8,128)(2,1)S(1)}, u32[]{:S(2)}, u32[]{:S(2)}) %collective-permute-start) | collective-permute-done | bytes 24608 | tf_op jit(solution)/shard_map/ppermute | solution.py:178
  4.4 2.9 %collective-permute-start.1 = (bf16[2,8,768]{2,1,0:T(8,128)(2,1)S(1)}, bf16[2,8,768]{2,1,0:T(8,128)(2,1)S(1)}, u32[]{:S(2)}, u32[]{:S(2)}) collective-permute-start(bf16[2,8,768]{2,1,0:T(8,128)(2,1)S(1)} %fusion.3), channel_id=1, source_target_pairs={{0,16},{8,24},{16,0},{24,8},{1,17},{9,25},{17,1},{25,9},{2,18},{10... | collective-permute-start | bytes 73736 | tf_op jit(solution)/shard_map/ppermute | solution.py:178
  7.3 1.8 %collective-permute-done.1 = bf16[2,8,768]{2,1,0:T(8,128)(2,1)S(1)} collective-permute-done((bf16[2,8,768]{2,1,0:T(8,128)(2,1)S(1)}, bf16[2,8,768]{2,1,0:T(8,128)(2,1)S(1)}, u32[]{:S(2)}, u32[]{:S(2)}) %collective-permute-start.1) | collective-permute-done | bytes 24608 | tf_op jit(solution)/shard_map/ppermute | solution.py:178
  9.1 3.2 %collective-permute-start.2 = (bf16[4,8,768]{2,1,0:T(8,128)(2,1)S(1)}, bf16[4,8,768]{2,1,0:T(8,128)(2,1)S(1)}, u32[]{:S(2)}, u32[]{:S(2)}) collective-permute-start(bf16[4,8,768]{2,1,0:T(8,128)(2,1)S(1)} %bitcast.100), channel_id=1, source_target_pairs={{0,4},{1,5},{2,6},{3,7},{4,0},{5,1},{6,2},{7,3},{8,12},{9,13},{10,... | collective-permute-start | bytes 147464 | tf_op jit(solution)/shard_map/ppermute | solution.py:178
  13.0 3.9 %all-to-all-start = ((bf16[32,8,640]{2,1,0:T(8,128)(2,1)}), bf16[32,8,640]{2,1,0:T(8,128)(2,1)S(1)}, u32[]{:S(2)}, u32[]{:S(2)}) async-start(bf16[32,8,640]{2,1,0:T(8,128)(2,1)} %bitcast.2), calls=%async_computation | async-start | bytes 655360 | tf_op jit(solution)/shard_map/all_to_all | solution.py:214
  17.1 1.8 %collective-permute-start.3 = (bf16[4,2,8,768]{3,2,1,0:T(8,128)(2,1)S(1)}, bf16[4,2,8,768]{3,2,1,0:T(8,128)(2,1)S(1)}, u32[]{:S(2)}, u32[]{:S(2)}) collective-permute-start(bf16[4,2,8,768]{3,2,1,0:T(8,128)(2,1)S(1)} %pad_maximum_fusion.2), channel_id=1, source_target_pairs={{0,2},{1,3},{2,0},{3,1},{4,6},{5,7},{6,4},{7,5},{8,10},{9,11},{10,... | collective-permute-start | bytes 294920 | tf_op jit(solution)/shard_map/ppermute | solution.py:178
  20.8 5.4 %collective-permute-done.3 = bf16[4,2,8,768]{3,2,1,0:T(8,128)(2,1)S(1)} collective-permute-done((bf16[4,2,8,768]{3,2,1,0:T(8,128)(2,1)S(1)}, bf16[4,2,8,768]{3,2,1,0:T(8,128)(2,1)S(1)}, u32[]{:S(2)}, u32[]{:S(2)}) %collective-permute-start.3) | collective-permute-done | bytes 98336 | tf_op jit(solution)/shard_map/ppermute | solution.py:178
  26.2 2.7 %all-to-all-done = bf16[32,8,640]{2,1,0:T(8,128)(2,1)S(1)} async-done(((bf16[32,8,640]{2,1,0:T(8,128)(2,1)}), bf16[32,8,640]{2,1,0:T(8,128)(2,1)S(1)}, u32[]{:S(2)}, u32[]{:S(2)}) %all-to-all-start) | async-done | bytes 327712 | tf_op jit(solution)/shard_map/all_to_all | solution.py:214
  29.6 2.0 %stats.1 = f32[2,8,256]{2,1,0:T(8,128)} custom-call(s32[1]{0:T(128)S(6)} %mul.34.start_ref, bf16[256,640]{1,0:T(8,128)(2,1)} %bitcast.92, bf16[128,640]{1,0:T(8,128)(2,1)} %k_ref.3), custom_call_target="tpu_custom_call" | custom-call | tf_op jit(solution)/shard_map/stats/pallas_call | solution.py:99
  31.6 0.8 %collective-permute-start.5 = (f32[2,8,256]{2,1,0:T(8,128)}, f32[2,8,256]{2,1,0:T(8,128)S(1)}, u32[]{:S(2)}, u32[]{:S(2)}) collective-permute-start(f32[2,8,256]{2,1,0:T(8,128)} %stats.1), channel_id=1, source_target_pairs={{0,4},{1,5},{2,6},{3,7},{4,0},{5,1},{6,2},{7,3},{8,12},{9,13},{10,... | collective-permute-start | bytes 49160 | tf_op jit(solution)/shard_map/ppermute | solution.py:168
  32.4 1.6 %collective-permute-start.4 = (bf16[4,2,2,8,768]{4,3,2,1,0:T(8,128)(2,1)S(1)}, bf16[4,2,2,8,768]{4,3,2,1,0:T(8,128)(2,1)S(1)}, u32[]{:S(2)}, u32[]{:S(2)}) collective-permute-start(bf16[4,2,2,8,768]{4,3,2,1,0:T(8,128)(2,1)S(1)} %pad_maximum_fusion.1), channel_id=1, source_target_pairs={{0,1},{1,0},{2,3},{3,2},{4,5},{5,4},{6,7},{7,6},{8,9},{9,8},{10,11... | collective-permute-start | bytes 589832 | tf_op jit(solution)/shard_map/ppermute | solution.py:178
  34.0 2.5 %collective-permute-done.5 = f32[2,8,256]{2,1,0:T(8,128)S(1)} collective-permute-done((f32[2,8,256]{2,1,0:T(8,128)}, f32[2,8,256]{2,1,0:T(8,128)S(1)}, u32[]{:S(2)}, u32[]{:S(2)}) %collective-permute-start.5) | collective-permute-done | bytes 16416 | tf_op jit(solution)/shard_map/ppermute | solution.py:168
  36.5 1.1 %collective-permute-start.6 = (f32[2,8,256]{2,1,0:T(8,128)S(1)}, f32[2,8,256]{2,1,0:T(8,128)S(1)}, u32[]{:S(2)}, u32[]{:S(2)}) collective-permute-start(f32[2,8,256]{2,1,0:T(8,128)S(1)} %pad_maximum_fusion.5), channel_id=1, source_target_pairs={{0,2},{1,3},{2,0},{3,1},{4,6},{5,7},{6,4},{7,5},{8,10},{9,11},{10,... | collective-permute-start | bytes 49160 | tf_op jit(solution)/shard_map/ppermute | solution.py:168
  37.6 1.3 %collective-permute-done.4 = bf16[4,2,2,8,768]{4,3,2,1,0:T(8,128)(2,1)S(1)} collective-permute-done((bf16[4,2,2,8,768]{4,3,2,1,0:T(8,128)(2,1)S(1)}, bf16[4,2,2,8,768]{4,3,2,1,0:T(8,128)(2,1)S(1)}, u32[]{:S(2)}, u32[]{:S(2)}) %collective-permute-start.4) | collective-permute-done | bytes 196640 | tf_op jit(solution)/shard_map/ppermute | solution.py:178
  38.9 1.4 %collective-permute-done.6 = f32[2,8,256]{2,1,0:T(8,128)S(1)} collective-permute-done((f32[2,8,256]{2,1,0:T(8,128)S(1)}, f32[2,8,256]{2,1,0:T(8,128)S(1)}, u32[]{:S(2)}, u32[]{:S(2)}) %collective-permute-start.6) | collective-permute-done | bytes 16416 | tf_op jit(solution)/shard_map/ppermute | solution.py:168
  40.3 1.2 %collective-permute-start.7 = (f32[2,8,256]{2,1,0:T(8,128)S(1)}, f32[2,8,256]{2,1,0:T(8,128)S(1)}, u32[]{:S(2)}, u32[]{:S(2)}) collective-permute-start(f32[2,8,256]{2,1,0:T(8,128)S(1)} %pad_maximum_fusion.6), channel_id=1, source_target_pairs={{0,1},{1,0},{2,3},{3,2},{4,5},{5,4},{6,7},{7,6},{8,9},{9,8},{10,11... | collective-permute-start | bytes 49160 | tf_op jit(solution)/shard_map/ppermute | solution.py:168
  41.5 0.8 %pad_maximum_fusion = bf16[4,2,2,2,8,768]{5,4,3,2,1,0:T(8,128)(2,1)} fusion(bf16[4,2,2,1,8,768]{5,4,3,2,1,0:T(8,128)(2,1)S(1)} %get-tuple-element.18, bf16[4,2,2,1,8,768]{5,4,3,2,1,0:T(8,128)(2,1)S(1)} %get-tuple-element.17), kind=kLoop, calls=%fused_computation | loop fusion | flops 196608 | bytes 786432 | tf_op jit(solution)/shard_map/stack | solution.py:184
  42.3 1.8 %collective-permute-done.7 = f32[2,8,256]{2,1,0:T(8,128)S(1)} collective-permute-done((f32[2,8,256]{2,1,0:T(8,128)S(1)}, f32[2,8,256]{2,1,0:T(8,128)S(1)}, u32[]{:S(2)}, u32[]{:S(2)}) %collective-permute-start.7) | collective-permute-done | bytes 16416 | tf_op jit(solution)/shard_map/ppermute | solution.py:168
  44.8 3.3 %query_gradients.1 = (bf16[256,640]{1,0:T(8,128)(2,1)}, bf16[5,128,256]{2,1,0:T(8,128)(2,1)}, bf16[5,128,256]{2,1,0:T(8,128)(2,1)}) custom-call(s32[1]{0:T(128)S(6)} %mul.34.start_ref, bf16[256,640]{1,0:T(8,128)(2,1)} %bitcast.93, bf16[256,768]{1,0:T(8,128)(2,1)} %bitcast.95, bf16[128,640]{1,0:T(8,128)(2,1)} %k_ref.3, bf16[128,640]{1,0:T(8,128)(2,1)} %v_ref.1, ...), custom_call_target="tpu_custom_call" | custom-call | tf_op jit(solution)/shard_map/query_gradients/pallas_call | solution.py:133
  48.0 3.0 %all-to-all-start.1 = ((bf16[32,8,640]{2,1,0:T(8,128)(2,1)}), bf16[32,8,640]{2,1,0:T(8,128)(2,1)S(1)}, u32[]{:S(2)}, u32[]{:S(2)}) async-start(bf16[32,8,640]{2,1,0:T(8,128)(2,1)} %bitcast.99), calls=%async_computation.1 | async-start | bytes 655360 | tf_op jit(solution)/shard_map/all_to_all | solution.py:214
  51.0 2.3 %cache_gradients.1 = (bf16[128,640]{1,0:T(8,128)(2,1)}, bf16[128,640]{1,0:T(8,128)(2,1)}) custom-call(bf16[256,640]{1,0:T(8,128)(2,1)} %bitcast.94, bf16[256,768]{1,0:T(8,128)(2,1)} %bitcast.96, bf16[5,128,256]{2,1,0:T(8,128)(2,1)} %get-tuple-element.9.p_ref, bf16[5,128,256]{2,1,0:T(8,128)(2,1)} %get-tuple-element.10.ds_ref), custom_call_target="tpu_custom_call" | custom-call | tf_op jit(solution)/shard_map/cache_gradients/pallas_call | solution.py:156
  53.4 9.7 %all-to-all-done.1 = bf16[32,8,640]{2,1,0:T(8,128)(2,1)S(1)} async-done(((bf16[32,8,640]{2,1,0:T(8,128)(2,1)}), bf16[32,8,640]{2,1,0:T(8,128)(2,1)S(1)}, u32[]{:S(2)}, u32[]{:S(2)}) %all-to-all-start.1) | async-done | bytes 327712 | tf_op jit(solution)/shard_map/all_to_all | solution.py:214
  (30 shorter events, 4.7 us)
Async XLA Ops:
  2.2 2.2 %copy-start.1 = (bf16[4,8,768]{2,1,0:T(8,128)(2,1)S(1)}, bf16[4,8,768]{2,1,0:T(8,128)(2,1)}, u32[]{:S(2)}) copy-start(bf16[4,8,768]{2,1,0:T(8,128)(2,1)} %pack_grads.1) | copy-start | bytes 147460
  3.0 1.3 %collective-permute-start = (bf16[2,8,768]{2,1,0:T(8,128)(2,1)S(1)}, bf16[2,8,768]{2,1,0:T(8,128)(2,1)S(1)}, u32[]{:S(2)}, u32[]{:S(2)}) collective-permute-start(bf16[2,8,768]{2,1,0:T(8,128)(2,1)S(1)} %fusion.4), channel_id=1, source_target_pairs={{0,8},{8,0},{16,24},{24,16},{1,9},{9,1},{17,25},{25,17},{2,10},{10... | collective-permute-start | bytes 73736 | tf_op jit(solution)/shard_map/ppermute | solution.py:178
  4.4 4.7 %collective-permute-start.1 = (bf16[2,8,768]{2,1,0:T(8,128)(2,1)S(1)}, bf16[2,8,768]{2,1,0:T(8,128)(2,1)S(1)}, u32[]{:S(2)}, u32[]{:S(2)}) collective-permute-start(bf16[2,8,768]{2,1,0:T(8,128)(2,1)S(1)} %fusion.3), channel_id=1, source_target_pairs={{0,16},{8,24},{16,0},{24,8},{1,17},{9,25},{17,1},{25,9},{2,18},{10... | collective-permute-start | bytes 73736 | tf_op jit(solution)/shard_map/ppermute | solution.py:178
  9.1 3.2 %copy-start.3 = (bf16[1,8,2560]{2,1,0:T(8,128)(2,1)S(1)}, bf16[1,8,2560]{2,1,0:T(8,128)(2,1)}, u32[]{:S(2)}) copy-start(bf16[1,8,2560]{2,1,0:T(8,128)(2,1)} %param.7) | copy-start | bytes 122884
  9.1 7.9 %collective-permute-start.2 = (bf16[4,8,768]{2,1,0:T(8,128)(2,1)S(1)}, bf16[4,8,768]{2,1,0:T(8,128)(2,1)S(1)}, u32[]{:S(2)}, u32[]{:S(2)}) collective-permute-start(bf16[4,8,768]{2,1,0:T(8,128)(2,1)S(1)} %bitcast.100), channel_id=1, source_target_pairs={{0,4},{1,5},{2,6},{3,7},{4,0},{5,1},{6,2},{7,3},{8,12},{9,13},{10,... | collective-permute-start | bytes 147464 | tf_op jit(solution)/shard_map/ppermute | solution.py:178
  13.0 15.8 %all-to-all-start = ((bf16[32,8,640]{2,1,0:T(8,128)(2,1)}), bf16[32,8,640]{2,1,0:T(8,128)(2,1)S(1)}, u32[]{:S(2)}, u32[]{:S(2)}) async-start(bf16[32,8,640]{2,1,0:T(8,128)(2,1)} %bitcast.2), calls=%async_computation | async-start | bytes 655360 | tf_op jit(solution)/shard_map/all_to_all | solution.py:214
  17.1 9.1 %collective-permute-start.3 = (bf16[4,2,8,768]{3,2,1,0:T(8,128)(2,1)S(1)}, bf16[4,2,8,768]{3,2,1,0:T(8,128)(2,1)S(1)}, u32[]{:S(2)}, u32[]{:S(2)}) collective-permute-start(bf16[4,2,8,768]{3,2,1,0:T(8,128)(2,1)S(1)} %pad_maximum_fusion.2), channel_id=1, source_target_pairs={{0,2},{1,3},{2,0},{3,1},{4,6},{5,7},{6,4},{7,5},{8,10},{9,11},{10,... | collective-permute-start | bytes 294920 | tf_op jit(solution)/shard_map/ppermute | solution.py:178
  18.9 0.7 %copy-start.4 = (s32[8]{0:T(128)S(1)}, s32[8]{0:T(128)}, u32[]{:S(2)}) copy-start(s32[8]{0:T(128)} %param.6) | copy-start | bytes 100
  28.9 0.7 %copy-start = (bf16[32,8,640]{2,1,0:T(8,128)(2,1)}, bf16[32,8,640]{2,1,0:T(8,128)(2,1)S(1)}, u32[]{:S(2)}) copy-start(bf16[32,8,640]{2,1,0:T(8,128)(2,1)S(1)} %all-to-all-done) | copy-start | bytes 983044
  31.6 4.8 %collective-permute-start.5 = (f32[2,8,256]{2,1,0:T(8,128)}, f32[2,8,256]{2,1,0:T(8,128)S(1)}, u32[]{:S(2)}, u32[]{:S(2)}) collective-permute-start(f32[2,8,256]{2,1,0:T(8,128)} %stats.1), channel_id=1, source_target_pairs={{0,4},{1,5},{2,6},{3,7},{4,0},{5,1},{6,2},{7,3},{8,12},{9,13},{10,... | collective-permute-start | bytes 49160 | tf_op jit(solution)/shard_map/ppermute | solution.py:168
  32.4 4.1 %copy-start.2 = (f32[2,8,256]{2,1,0:T(8,128)S(1)}, f32[2,8,256]{2,1,0:T(8,128)}, u32[]{:S(2)}) copy-start(f32[2,8,256]{2,1,0:T(8,128)} %stats.1) | copy-start | bytes 49156
  32.4 6.5 %collective-permute-start.4 = (bf16[4,2,2,8,768]{4,3,2,1,0:T(8,128)(2,1)S(1)}, bf16[4,2,2,8,768]{4,3,2,1,0:T(8,128)(2,1)S(1)}, u32[]{:S(2)}, u32[]{:S(2)}) collective-permute-start(bf16[4,2,2,8,768]{4,3,2,1,0:T(8,128)(2,1)S(1)} %pad_maximum_fusion.1), channel_id=1, source_target_pairs={{0,1},{1,0},{2,3},{3,2},{4,5},{5,4},{6,7},{7,6},{8,9},{9,8},{10,11... | collective-permute-start | bytes 589832 | tf_op jit(solution)/shard_map/ppermute | solution.py:178
  36.5 3.8 %collective-permute-start.6 = (f32[2,8,256]{2,1,0:T(8,128)S(1)}, f32[2,8,256]{2,1,0:T(8,128)S(1)}, u32[]{:S(2)}, u32[]{:S(2)}) collective-permute-start(f32[2,8,256]{2,1,0:T(8,128)S(1)} %pad_maximum_fusion.5), channel_id=1, source_target_pairs={{0,2},{1,3},{2,0},{3,1},{4,6},{5,7},{6,4},{7,5},{8,10},{9,11},{10,... | collective-permute-start | bytes 49160 | tf_op jit(solution)/shard_map/ppermute | solution.py:168
  40.3 3.8 %collective-permute-start.7 = (f32[2,8,256]{2,1,0:T(8,128)S(1)}, f32[2,8,256]{2,1,0:T(8,128)S(1)}, u32[]{:S(2)}, u32[]{:S(2)}) collective-permute-start(f32[2,8,256]{2,1,0:T(8,128)S(1)} %pad_maximum_fusion.6), channel_id=1, source_target_pairs={{0,1},{1,0},{2,3},{3,2},{4,5},{5,4},{6,7},{7,6},{8,9},{9,8},{10,11... | collective-permute-start | bytes 49160 | tf_op jit(solution)/shard_map/ppermute | solution.py:168
  48.0 15.0 %all-to-all-start.1 = ((bf16[32,8,640]{2,1,0:T(8,128)(2,1)}), bf16[32,8,640]{2,1,0:T(8,128)(2,1)S(1)}, u32[]{:S(2)}, u32[]{:S(2)}) async-start(bf16[32,8,640]{2,1,0:T(8,128)(2,1)} %bitcast.99), calls=%async_computation.1 | async-start | bytes 655360 | tf_op jit(solution)/shard_map/all_to_all | solution.py:214

commit v3 on v2

--- a/solution.py
+++ b/solution.py
@@ -1,3 +1,5 @@
+import math
+
 import jax
 import jax.numpy as jnp
 from jax import lax
@@ -8,6 +10,7 @@
 
 HEAD_DIM = 128
 LANES = 128
+ON_CHIP_BYTES = 1 << 20
 masked_score = -1e30
 BF = jnp.bfloat16
 F32 = jnp.float32
@@ -37,6 +40,22 @@
     return [pl.BlockSpec(memory_space=pltpu.VMEM) for _ in range(count)]
 
 
+def small(shape, dtype):
+    return math.prod(shape) * jnp.dtype(dtype).itemsize <= ON_CHIP_BYTES
+
+
+def vmem(value):
+    if small(value.shape, value.dtype):
+        return pltpu.with_memory_space_constraint(value, pltpu.VMEM)
+    return value
+
+
+def held(shape, dtype):
+    if small(shape, dtype):
+        return pltpu.VMEM(shape, dtype)
+    return jax.ShapeDtypeStruct(shape, dtype)
+
+
 def in_smem():
     return pl.BlockSpec(memory_space=pltpu.SMEM)
 
@@ -45,12 +64,19 @@
     return pl.ds(h * HEAD_DIM, HEAD_DIM)
 
 
-def pack_grads(grads, outs, sections):
-    rows, features = grads.shape
+def pack(queries, grads, outs, sections, copies):
+    rows, features = queries.shape
     here = features // sections
     heads = here // HEAD_DIM
 
-    def body(g_ref, o_ref, out_ref):
+    def body(q_ref, g_ref, o_ref, sent_ref, out_ref):
+        for s in range(sections):
+            q = q_ref[:, pl.ds(s * here, here)]
+
+            @pl.loop(0, copies, unroll=copies <= 8)
+            def _(c):
+                sent_ref[s, c] = q
+
         lane = lax.broadcasted_iota(jnp.int32, (rows, LANES), 1)
         for s in range(sections):
             extra = jnp.zeros((rows, LANES), F32)
@@ -65,11 +91,14 @@
 
     return pl.pallas_call(
         body,
-        in_specs=in_vmem(2),
-        out_specs=in_vmem(1)[0],
-        out_shape=jax.ShapeDtypeStruct((sections, rows, here + LANES), BF),
-        name="pack_grads",
-    )(grads, outs)
+        in_specs=in_vmem(3),
+        out_specs=in_vmem(2),
+        out_shape=[
+            jax.ShapeDtypeStruct((sections, copies, rows, here), BF),
+            held((sections, rows, here + LANES), BF),
+        ],
+        name="pack",
+    )(queries, grads, outs)
 
 
 def visible_of(start_ref, shape, row_count, key_total):
@@ -100,9 +129,9 @@
         body,
         in_specs=[in_smem(), *in_vmem(2)],
         out_specs=in_vmem(1)[0],
-        out_shape=jax.ShapeDtypeStruct((2, slots, m), F32),
+        out_shape=held((2, slots, m), F32),
         name="stats",
-    )(start, queries, keys)
+    )(start, vmem(queries), vmem(keys))
 
 
 def query_kernel(start, queries, grads, keys, values, stats, row_count, key_total):
@@ -136,11 +165,11 @@
         out_specs=in_vmem(3),
         out_shape=[
             jax.ShapeDtypeStruct((m, here), BF),
-            jax.ShapeDtypeStruct((heads, key_count, m), BF),
-            jax.ShapeDtypeStruct((heads, key_count, m), BF),
+            held((heads, key_count, m), BF),
+            held((heads, key_count, m), BF),
         ],
         name="query_gradients",
-    )(start, queries, grads, keys, values, stats)
+    )(start, vmem(queries), vmem(grads), vmem(keys), vmem(values), vmem(stats))
 
 
 def cache_kernel(queries, grads, probs, score_grads):
@@ -159,17 +188,15 @@
         out_specs=in_vmem(2),
         out_shape=[jax.ShapeDtypeStruct((key_count, here), BF)] * 2,
         name="cache_gradients",
-    )(queries, grads, probs, score_grads)
+    )(vmem(queries), vmem(grads), vmem(probs), vmem(score_grads))
 
 
 def merge_stats(stats, axis, count):
-    step = count // 2
-    while step:
-        other = lax.ppermute(stats, axis, [(i, i ^ step) for i in range(count)])
+    for i in range(count.bit_length() - 1):
+        other = flip(stats, axis, count >> (i + 1))
         top = jnp.maximum(stats[0], other[0])
         total = stats[1] * jnp.exp(stats[0] - top) + other[1] * jnp.exp(other[0] - top)
         stats = jnp.stack([top, total])
-        step //= 2
     return stats
 
 
@@ -206,7 +233,8 @@
     for i in range(bits):
         bit = count >> (i + 1)
         upper = lax.axis_index(axis) & bit != 0
-        blocks = ordered(blocks, flip(blocks, axis, bit), upper, i + 1)
+        other = flip(blocks, axis, bit)
+        blocks = ordered(blocks, other, upper, i + 1)
     return blocks.reshape((lead, count) + rest)
 
 
@@ -227,13 +255,10 @@
     peers = sections * ctx_count
     start = (block_order[lax.axis_index("ctx")] * key_count).reshape(1)
 
-    sent = queries.reshape(rows, sections, here).transpose(1, 0, 2)[:, None]
-    sent = jnp.broadcast_to(sent, (sections, ctx_count, rows, here))
+    sent, own = pack(queries[0], output_grad[0], attention_out[0], sections, ctx_count)
     query_all = exchange(sent.reshape(peers, rows, here)).reshape(-1, here)
-
-    sent = pack_grads(output_grad[0], attention_out[0], sections)
-    sent = spread_blocks(swap_blocks(sent, "section"), "ctx")
-    grad_all = sent.reshape(peers * rows, -1)
+    own = spread_blocks(swap_blocks(own, "section"), "ctx")
+    grad_all = own.reshape(peers * rows, -1)
 
     stats = stats_kernel(start, query_all, cache_keys, row_count, key_total)
     stats = merge_stats(stats, "ctx", ctx_count)

time: 64.2 us -> 58.1 us (0.905)
  Pallas kernels: 9.15 us -> 5.04 us
  other arithmetic: 3.05 us -> 0.89 us
  waiting for transfers between devices: 27.4 us -> 29.2 us
  local copies, waits for them, and re-layouts: 2.73 us -> 1.25 us
    ppermute x5 -> x8, waiting for transfers between devices: 9.31 us -> 15.5 us  [flip(): return lax.ppermute(value, axis, [(i, i ^ bit) for i in range(count)])]
    ppermute x3 -> x0, waiting for transfers between devices: 5.69 us -> none  [merge_stats(): other = lax.ppermute(stats, axis, [(i, i ^ step) for i in range(count)])]
    ppermute x5 -> x8, starting transfers between devices: 9.96 us -> 13.1 us  [flip(): return lax.ppermute(value, axis, [(i, i ^ bit) for i in range(count)])]
    ppermute x3 -> x0, starting transfers between devices: 3.07 us -> none  [merge_stats(): other = lax.ppermute(stats, axis, [(i, i ^ step) for i in range(count)])]
    pallas_call x1, Pallas kernels: 2.03 us -> 0.4 us  [stats_kernel(): pl.pallas_call(body, in_specs=[in_smem(), *in_vmem(2)], out_specs=in_vmem...]
    all_to_all x2, waiting for transfers between devices: 12.4 us -> 13.7 us  [exchange(): return lax.all_to_all(blocks, ('section', 'ctx'), 0, 0, tiled=True)]
    pallas_call x1, Pallas kernels: 2.33 us -> 1.04 us  [cache_kernel(): pl.pallas_call(body, in_specs=in_vmem(4), out_specs=in_vmem(2), out_shape...]
    pallas_call x1, Pallas kernels: 3.27 us -> 2.02 us  [query_kernel(): pl.pallas_call(body, in_specs=[in_smem(), *in_vmem(5)], out_specs=in_vmem...]
  transfers between devices with their start and end apart: 10 -> 10, of which waited for: 9 -> 9; matrix products, arithmetic and copies ran while one was open for 4% -> 1% of each run, Pallas kernels for 4% -> 2%
where the time goes in v3:
time: 58.1 us; the launch traced here: 57.7 us
  waiting for transfers between devices  29.2 us (50%)
  starting transfers between devices  19.9 us (34%)
  Pallas kernels  5.04 us (9%)
  between operations  1.43 us (2%)
  local copies, waits for them, and re-layouts  1.25 us (2%)
  other arithmetic  0.89 us (2%)
    ppermute x8, waiting for transfers between devices, flip(): return lax.ppermute(value, axis, [(i, i ^ bit) for i in range(count)])  15.5 us
    all_to_all x2, waiting for transfers between devices, exchange(): return lax.all_to_all(blocks, ('section', 'ctx'), 0, 0, tiled=True)  13.7 us
    ppermute x8, starting transfers between devices, flip(): return lax.ppermute(value, axis, [(i, i ^ bit) for i in range(count)])  13.1 us
    all_to_all x2, starting transfers between devices, exchange(): return lax.all_to_all(blocks, ('section', 'ctx'), 0, 0, tiled=True)  6.82 us
    pallas_call x1, Pallas kernels, query_kernel(): pl.pallas_call(body, in_specs=[in_smem(), *in_vmem(5)], out_specs=in_vmem...  2.02 us
    pallas_call x1, Pallas kernels, pack(): pl.pallas_call(body, in_specs=in_vmem(3), out_specs=in_vmem(2), out_shape...  1.57 us
  transfers between devices with their start and end apart: 10, of which 9 were waited for; matrix products, arithmetic and copies ran while one was open for 1% of the time, Pallas kernels for 2%

profile of v3, /device:TPU:0, one launch (start us, length us, event | category | flops | bytes accessed | tf_op | source)
XLA Modules:
  0.0 57.7 jit_solution(8598626988627661373)
XLA Ops:
  0.6 1.6 %pack.1 = (bf16[4,8,8,640]{3,2,1,0:T(8,128)(2,1)}, bf16[4,8,768]{2,1,0:T(8,128)(2,1)S(1)}) custom-call(bf16[8,2560]{1,0:T(8,128)(2,1)} %bitcast.99, bf16[8,2560]{1,0:T(8,128)(2,1)} %bitcast.100, bf16[8,2560]{1,0:T(8,128)(2,1)} %bitcast.101), custom_call_target="tpu_custom_call" | custom-call | tf_op jit(solution)/shard_map/pack/pallas_call | solution.py:92
  2.7 0.8 %collective-permute-done = bf16[2,8,768]{2,1,0:T(8,128)(2,1)S(1)} collective-permute-done((bf16[2,8,768]{2,1,0:T(8,128)(2,1)S(1)}, bf16[2,8,768]{2,1,0:T(8,128)(2,1)S(1)}, u32[]{:S(2)}, u32[]{:S(2)}) %collective-permute-start) | collective-permute-done | bytes 24608 | tf_op jit(solution)/shard_map/ppermute | solution.py:205
  3.6 2.9 %collective-permute-start.1 = (bf16[2,8,768]{2,1,0:T(8,128)(2,1)S(1)}, bf16[2,8,768]{2,1,0:T(8,128)(2,1)S(1)}, u32[]{:S(2)}, u32[]{:S(2)}) collective-permute-start(bf16[2,8,768]{2,1,0:T(8,128)(2,1)S(1)} %fusion.3), channel_id=1, source_target_pairs={{0,16},{8,24},{16,0},{24,8},{1,17},{9,25},{17,1},{25,9},{2,18},{10... | collective-permute-start | bytes 73736 | tf_op jit(solution)/shard_map/ppermute | solution.py:205
  6.5 1.8 %collective-permute-done.1 = bf16[2,8,768]{2,1,0:T(8,128)(2,1)S(1)} collective-permute-done((bf16[2,8,768]{2,1,0:T(8,128)(2,1)S(1)}, bf16[2,8,768]{2,1,0:T(8,128)(2,1)S(1)}, u32[]{:S(2)}, u32[]{:S(2)}) %collective-permute-start.1) | collective-permute-done | bytes 24608 | tf_op jit(solution)/shard_map/ppermute | solution.py:205
  8.3 3.2 %collective-permute-start.2 = (bf16[4,8,768]{2,1,0:T(8,128)(2,1)S(1)}, bf16[4,8,768]{2,1,0:T(8,128)(2,1)S(1)}, u32[]{:S(2)}, u32[]{:S(2)}) collective-permute-start(bf16[4,8,768]{2,1,0:T(8,128)(2,1)S(1)} %bitcast.98), channel_id=1, source_target_pairs={{0,4},{1,5},{2,6},{3,7},{4,0},{5,1},{6,2},{7,3},{8,12},{9,13},{10,... | collective-permute-start | bytes 147464 | tf_op jit(solution)/shard_map/ppermute | solution.py:205
  11.5 3.8 %all-to-all-start = ((bf16[32,8,640]{2,1,0:T(8,128)(2,1)}), bf16[32,8,640]{2,1,0:T(8,128)(2,1)S(1)}, u32[]{:S(2)}, u32[]{:S(2)}) async-start(bf16[32,8,640]{2,1,0:T(8,128)(2,1)} %bitcast.3), calls=%async_computation | async-start | bytes 655360 | tf_op jit(solution)/shard_map/all_to_all | solution.py:242
  15.4 1.8 %collective-permute-start.3 = (bf16[4,2,8,768]{3,2,1,0:T(8,128)(2,1)S(1)}, bf16[4,2,8,768]{3,2,1,0:T(8,128)(2,1)S(1)}, u32[]{:S(2)}, u32[]{:S(2)}) collective-permute-start(bf16[4,2,8,768]{3,2,1,0:T(8,128)(2,1)S(1)} %pad_maximum_fusion.2), channel_id=1, source_target_pairs={{0,2},{1,3},{2,0},{3,1},{4,6},{5,7},{6,4},{7,5},{8,10},{9,11},{10,... | collective-permute-start | bytes 294920 | tf_op jit(solution)/shard_map/ppermute | solution.py:205
  17.2 0.7 %copy-done.2 = s32[8]{0:T(128)S(1)} copy-done((s32[8]{0:T(128)S(1)}, s32[8]{0:T(128)}, u32[]{:S(2)}) %copy-start.2) | copy-done | bytes 56
  17.9 0.6 %dynamic_slice.3 = s32[1]{0:T(128)} dynamic-slice(s32[8]{0:T(128)S(1)} %copy-done.2, s32[]{:T(128)S(6)} %select_n.104), dynamic_slice_sizes={1} | dynamic-slice | bytes 12 | tf_op jit(solution)/shard_map/dynamic_slice | solution.py:256
  19.1 5.4 %collective-permute-done.3 = bf16[4,2,8,768]{3,2,1,0:T(8,128)(2,1)S(1)} collective-permute-done((bf16[4,2,8,768]{3,2,1,0:T(8,128)(2,1)S(1)}, bf16[4,2,8,768]{3,2,1,0:T(8,128)(2,1)S(1)}, u32[]{:S(2)}, u32[]{:S(2)}) %collective-permute-start.3) | collective-permute-done | bytes 98336 | tf_op jit(solution)/shard_map/ppermute | solution.py:205
  24.5 2.7 %all-to-all-done = bf16[32,8,640]{2,1,0:T(8,128)(2,1)S(1)} async-done(((bf16[32,8,640]{2,1,0:T(8,128)(2,1)}), bf16[32,8,640]{2,1,0:T(8,128)(2,1)S(1)}, u32[]{:S(2)}, u32[]{:S(2)}) %all-to-all-start) | async-done | bytes 327712 | tf_op jit(solution)/shard_map/all_to_all | solution.py:242
  27.6 0.8 %collective-permute-start.5 = (f32[2,8,256]{2,1,0:T(8,128)S(1)}, f32[2,8,256]{2,1,0:T(8,128)S(1)}, u32[]{:S(2)}, u32[]{:S(2)}) collective-permute-start(f32[2,8,256]{2,1,0:T(8,128)S(1)} %stats.1), channel_id=1, source_target_pairs={{0,4},{1,5},{2,6},{3,7},{4,0},{5,1},{6,2},{7,3},{8,12},{9,13},{10,... | collective-permute-start | bytes 49160 | tf_op jit(solution)/shard_map/ppermute | solution.py:205
  28.5 1.6 %collective-permute-start.4 = (bf16[4,2,2,8,768]{4,3,2,1,0:T(8,128)(2,1)S(1)}, bf16[4,2,2,8,768]{4,3,2,1,0:T(8,128)(2,1)S(1)}, u32[]{:S(2)}, u32[]{:S(2)}) collective-permute-start(bf16[4,2,2,8,768]{4,3,2,1,0:T(8,128)(2,1)S(1)} %pad_maximum_fusion.1), channel_id=1, source_target_pairs={{0,1},{1,0},{2,3},{3,2},{4,5},{5,4},{6,7},{7,6},{8,9},{9,8},{10,11... | collective-permute-start | bytes 589832 | tf_op jit(solution)/shard_map/ppermute | solution.py:205
  30.1 2.3 %collective-permute-done.5 = f32[2,8,256]{2,1,0:T(8,128)S(1)} collective-permute-done((f32[2,8,256]{2,1,0:T(8,128)S(1)}, f32[2,8,256]{2,1,0:T(8,128)S(1)}, u32[]{:S(2)}, u32[]{:S(2)}) %collective-permute-start.5) | collective-permute-done | bytes 16416 | tf_op jit(solution)/shard_map/ppermute | solution.py:205
  32.3 1.1 %collective-permute-start.6 = (f32[2,8,256]{2,1,0:T(8,128)S(1)}, f32[2,8,256]{2,1,0:T(8,128)S(1)}, u32[]{:S(2)}, u32[]{:S(2)}) collective-permute-start(f32[2,8,256]{2,1,0:T(8,128)S(1)} %pad_maximum_fusion.5), channel_id=1, source_target_pairs={{0,2},{1,3},{2,0},{3,1},{4,6},{5,7},{6,4},{7,5},{8,10},{9,11},{10,... | collective-permute-start | bytes 49160 | tf_op jit(solution)/shard_map/ppermute | solution.py:205
  33.5 1.5 %collective-permute-done.4 = bf16[4,2,2,8,768]{4,3,2,1,0:T(8,128)(2,1)S(1)} collective-permute-done((bf16[4,2,2,8,768]{4,3,2,1,0:T(8,128)(2,1)S(1)}, bf16[4,2,2,8,768]{4,3,2,1,0:T(8,128)(2,1)S(1)}, u32[]{:S(2)}, u32[]{:S(2)}) %collective-permute-start.4) | collective-permute-done | bytes 196640 | tf_op jit(solution)/shard_map/ppermute | solution.py:205
  35.0 1.2 %collective-permute-done.6 = f32[2,8,256]{2,1,0:T(8,128)S(1)} collective-permute-done((f32[2,8,256]{2,1,0:T(8,128)S(1)}, f32[2,8,256]{2,1,0:T(8,128)S(1)}, u32[]{:S(2)}, u32[]{:S(2)}) %collective-permute-start.6) | collective-permute-done | bytes 16416 | tf_op jit(solution)/shard_map/ppermute | solution.py:205
  36.2 1.2 %collective-permute-start.7 = (f32[2,8,256]{2,1,0:T(8,128)S(1)}, f32[2,8,256]{2,1,0:T(8,128)S(1)}, u32[]{:S(2)}, u32[]{:S(2)}) collective-permute-start(f32[2,8,256]{2,1,0:T(8,128)S(1)} %pad_maximum_fusion.6), channel_id=1, source_target_pairs={{0,1},{1,0},{2,3},{3,2},{4,5},{5,4},{6,7},{7,6},{8,9},{9,8},{10,11... | collective-permute-start | bytes 49160 | tf_op jit(solution)/shard_map/ppermute | solution.py:205
  37.4 2.6 %collective-permute-done.7 = f32[2,8,256]{2,1,0:T(8,128)S(1)} collective-permute-done((f32[2,8,256]{2,1,0:T(8,128)S(1)}, f32[2,8,256]{2,1,0:T(8,128)S(1)}, u32[]{:S(2)}, u32[]{:S(2)}) %collective-permute-start.7) | collective-permute-done | bytes 16416 | tf_op jit(solution)/shard_map/ppermute | solution.py:205
  40.0 2.0 %query_gradients.1 = (bf16[256,640]{1,0:T(8,128)(2,1)}, bf16[5,128,256]{2,1,0:T(8,128)(2,1)S(1)}, bf16[5,128,256]{2,1,0:T(8,128)(2,1)S(1)}) custom-call(s32[1]{0:T(128)S(6)} %mul.34.start_ref, bf16[256,640]{1,0:T(8,128)(2,1)S(1)} %bitcast.91, bf16[256,768]{1,0:T(8,128)(2,1)S(1)} %bitcast.93, bf16[128,640]{1,0:T(8,128)(2,1)S(1)} %copy-done, ...), custom_call_target="tpu_custom_call" | custom-call | tf_op jit(solution)/shard_map/query_gradients/pallas_call | solution.py:162
  42.0 3.0 %all-to-all-start.1 = ((bf16[32,8,640]{2,1,0:T(8,128)(2,1)}), bf16[32,8,640]{2,1,0:T(8,128)(2,1)S(1)}, u32[]{:S(2)}, u32[]{:S(2)}) async-start(bf16[32,8,640]{2,1,0:T(8,128)(2,1)} %bitcast.97), calls=%async_computation.1 | async-start | bytes 655360 | tf_op jit(solution)/shard_map/all_to_all | solution.py:242
  45.0 1.0 %cache_gradients.1 = (bf16[128,640]{1,0:T(8,128)(2,1)}, bf16[128,640]{1,0:T(8,128)(2,1)}) custom-call(bf16[256,640]{1,0:T(8,128)(2,1)S(1)} %bitcast.92, bf16[256,768]{1,0:T(8,128)(2,1)S(1)} %bitcast.94, bf16[5,128,256]{2,1,0:T(8,128)(2,1)S(1)} %get-tuple-element.13.p_ref, bf16[5,128,256]{2,1,0:T(8,128)(2,1)S(1)} %get-tuple-element.14.ds_ref), custom_call_target="tpu_custom_call" | custom-call | tf_op jit(solution)/shard_map/cache_gradients/pallas_call | solution.py:185
  46.1 11.0 %all-to-all-done.1 = bf16[32,8,640]{2,1,0:T(8,128)(2,1)S(1)} async-done(((bf16[32,8,640]{2,1,0:T(8,128)(2,1)}), bf16[32,8,640]{2,1,0:T(8,128)(2,1)S(1)}, u32[]{:S(2)}, u32[]{:S(2)}) %all-to-all-start.1) | async-done | bytes 327712 | tf_op jit(solution)/shard_map/all_to_all | solution.py:242
  57.1 0.7 %bitcast_reduce_fusion = bf16[4,8,640]{2,1,0:T(8,128)(2,1)} fusion(bf16[32,8,640]{2,1,0:T(8,128)(2,1)S(1)} %all-to-all-done.1), kind=kLoop, calls=%fused_computation.1 | loop fusion | flops 143360 | bytes 368640 | tf_op jit(solution)/shard_map/reduce_sum | solution.py:270
  (25 shorter events, 1.1 us)
Async XLA Ops:
  2.2 1.3 %collective-permute-start = (bf16[2,8,768]{2,1,0:T(8,128)(2,1)S(1)}, bf16[2,8,768]{2,1,0:T(8,128)(2,1)S(1)}, u32[]{:S(2)}, u32[]{:S(2)}) collective-permute-start(bf16[2,8,768]{2,1,0:T(8,128)(2,1)S(1)} %fusion.4), channel_id=1, source_target_pairs={{0,8},{8,0},{16,24},{24,16},{1,9},{9,1},{17,25},{25,17},{2,10},{10... | collective-permute-start | bytes 73736 | tf_op jit(solution)/shard_map/ppermute | solution.py:205
  3.6 4.7 %collective-permute-start.1 = (bf16[2,8,768]{2,1,0:T(8,128)(2,1)S(1)}, bf16[2,8,768]{2,1,0:T(8,128)(2,1)S(1)}, u32[]{:S(2)}, u32[]{:S(2)}) collective-permute-start(bf16[2,8,768]{2,1,0:T(8,128)(2,1)S(1)} %fusion.3), channel_id=1, source_target_pairs={{0,16},{8,24},{16,0},{24,8},{1,17},{9,25},{17,1},{25,9},{2,18},{10... | collective-permute-start | bytes 73736 | tf_op jit(solution)/shard_map/ppermute | solution.py:205
  8.3 7.0 %collective-permute-start.2 = (bf16[4,8,768]{2,1,0:T(8,128)(2,1)S(1)}, bf16[4,8,768]{2,1,0:T(8,128)(2,1)S(1)}, u32[]{:S(2)}, u32[]{:S(2)}) collective-permute-start(bf16[4,8,768]{2,1,0:T(8,128)(2,1)S(1)} %bitcast.98), channel_id=1, source_target_pairs={{0,4},{1,5},{2,6},{3,7},{4,0},{5,1},{6,2},{7,3},{8,12},{9,13},{10,... | collective-permute-start | bytes 147464 | tf_op jit(solution)/shard_map/ppermute | solution.py:205
  11.5 15.7 %all-to-all-start = ((bf16[32,8,640]{2,1,0:T(8,128)(2,1)}), bf16[32,8,640]{2,1,0:T(8,128)(2,1)S(1)}, u32[]{:S(2)}, u32[]{:S(2)}) async-start(bf16[32,8,640]{2,1,0:T(8,128)(2,1)} %bitcast.3), calls=%async_computation | async-start | bytes 655360 | tf_op jit(solution)/shard_map/all_to_all | solution.py:242
  15.4 9.1 %collective-permute-start.3 = (bf16[4,2,8,768]{3,2,1,0:T(8,128)(2,1)S(1)}, bf16[4,2,8,768]{3,2,1,0:T(8,128)(2,1)S(1)}, u32[]{:S(2)}, u32[]{:S(2)}) collective-permute-start(bf16[4,2,8,768]{3,2,1,0:T(8,128)(2,1)S(1)} %pad_maximum_fusion.2), channel_id=1, source_target_pairs={{0,2},{1,3},{2,0},{3,1},{4,6},{5,7},{6,4},{7,5},{8,10},{9,11},{10,... | collective-permute-start | bytes 294920 | tf_op jit(solution)/shard_map/ppermute | solution.py:205
  17.2 0.7 %copy-start.2 = (s32[8]{0:T(128)S(1)}, s32[8]{0:T(128)}, u32[]{:S(2)}) copy-start(s32[8]{0:T(128)} %param.6) | copy-start | bytes 100
  19.1 8.1 %copy-start = (bf16[128,640]{1,0:T(8,128)(2,1)S(1)}, bf16[128,640]{1,0:T(8,128)(2,1)}, u32[]{:S(2)}) copy-start(bf16[128,640]{1,0:T(8,128)(2,1)} %k_ref.3) | copy-start | bytes 491524
  27.6 4.7 %collective-permute-start.5 = (f32[2,8,256]{2,1,0:T(8,128)S(1)}, f32[2,8,256]{2,1,0:T(8,128)S(1)}, u32[]{:S(2)}, u32[]{:S(2)}) collective-permute-start(f32[2,8,256]{2,1,0:T(8,128)S(1)} %stats.1), channel_id=1, source_target_pairs={{0,4},{1,5},{2,6},{3,7},{4,0},{5,1},{6,2},{7,3},{8,12},{9,13},{10,... | collective-permute-start | bytes 49160 | tf_op jit(solution)/shard_map/ppermute | solution.py:205
  28.5 6.5 %collective-permute-start.4 = (bf16[4,2,2,8,768]{4,3,2,1,0:T(8,128)(2,1)S(1)}, bf16[4,2,2,8,768]{4,3,2,1,0:T(8,128)(2,1)S(1)}, u32[]{:S(2)}, u32[]{:S(2)}) collective-permute-start(bf16[4,2,2,8,768]{4,3,2,1,0:T(8,128)(2,1)S(1)} %pad_maximum_fusion.1), channel_id=1, source_target_pairs={{0,1},{1,0},{2,3},{3,2},{4,5},{5,4},{6,7},{7,6},{8,9},{9,8},{10,11... | collective-permute-start | bytes 589832 | tf_op jit(solution)/shard_map/ppermute | solution.py:205
  32.3 3.8 %collective-permute-start.6 = (f32[2,8,256]{2,1,0:T(8,128)S(1)}, f32[2,8,256]{2,1,0:T(8,128)S(1)}, u32[]{:S(2)}, u32[]{:S(2)}) collective-permute-start(f32[2,8,256]{2,1,0:T(8,128)S(1)} %pad_maximum_fusion.5), channel_id=1, source_target_pairs={{0,2},{1,3},{2,0},{3,1},{4,6},{5,7},{6,4},{7,5},{8,10},{9,11},{10,... | collective-permute-start | bytes 49160 | tf_op jit(solution)/shard_map/ppermute | solution.py:205
  36.2 3.8 %collective-permute-start.7 = (f32[2,8,256]{2,1,0:T(8,128)S(1)}, f32[2,8,256]{2,1,0:T(8,128)S(1)}, u32[]{:S(2)}, u32[]{:S(2)}) collective-permute-start(f32[2,8,256]{2,1,0:T(8,128)S(1)} %pad_maximum_fusion.6), channel_id=1, source_target_pairs={{0,1},{1,0},{2,3},{3,2},{4,5},{5,4},{6,7},{7,6},{8,9},{9,8},{10,11... | collective-permute-start | bytes 49160 | tf_op jit(solution)/shard_map/ppermute | solution.py:205
  37.4 2.6 %copy-start.1 = (bf16[128,640]{1,0:T(8,128)(2,1)S(1)}, bf16[128,640]{1,0:T(8,128)(2,1)}, u32[]{:S(2)}) copy-start(bf16[128,640]{1,0:T(8,128)(2,1)} %v_ref.1) | copy-start | bytes 491524
  42.0 15.0 %all-to-all-start.1 = ((bf16[32,8,640]{2,1,0:T(8,128)(2,1)}), bf16[32,8,640]{2,1,0:T(8,128)(2,1)S(1)}, u32[]{:S(2)}, u32[]{:S(2)}) async-start(bf16[32,8,640]{2,1,0:T(8,128)(2,1)} %bitcast.97), calls=%async_computation.1 | async-start | bytes 655360 | tf_op jit(solution)/shard_map/all_to_all | solution.py:242

commit v4 on v3

--- a/solution.py
+++ b/solution.py
@@ -64,19 +64,12 @@
     return pl.ds(h * HEAD_DIM, HEAD_DIM)
 
 
-def pack(queries, grads, outs, sections, copies):
-    rows, features = queries.shape
+def pack(grads, outs, sections):
+    rows, features = grads.shape
     here = features // sections
     heads = here // HEAD_DIM
 
-    def body(q_ref, g_ref, o_ref, sent_ref, out_ref):
-        for s in range(sections):
-            q = q_ref[:, pl.ds(s * here, here)]
-
-            @pl.loop(0, copies, unroll=copies <= 8)
-            def _(c):
-                sent_ref[s, c] = q
-
+    def body(g_ref, o_ref, out_ref):
         lane = lax.broadcasted_iota(jnp.int32, (rows, LANES), 1)
         for s in range(sections):
             extra = jnp.zeros((rows, LANES), F32)
@@ -91,14 +84,11 @@
 
     return pl.pallas_call(
         body,
-        in_specs=in_vmem(3),
-        out_specs=in_vmem(2),
-        out_shape=[
-            jax.ShapeDtypeStruct((sections, copies, rows, here), BF),
-            held((sections, rows, here + LANES), BF),
-        ],
+        in_specs=in_vmem(2),
+        out_specs=in_vmem(1)[0],
+        out_shape=held((sections, rows, here + LANES), BF),
         name="pack",
-    )(queries, grads, outs)
+    )(grads, outs)
 
 
 def visible_of(start_ref, shape, row_count, key_total):
@@ -107,14 +97,14 @@
     return key_pos <= key_total - row_count + row
 
 
-def stats_kernel(start, queries, keys, row_count, key_total):
+def stats_kernel(start, queries, keys, values, row_count, key_total):
     m, here = queries.shape
     key_count = keys.shape[0]
     heads = here // HEAD_DIM
     slots = -(-heads // 8) * 8
     scaling = HEAD_DIM ** (-0.5)
 
-    def body(start_ref, q_ref, k_ref, out_ref):
+    def body(start_ref, q_ref, k_ref, _, out_ref):
         visible = visible_of(start_ref, (key_count, m), row_count, key_total)
         out_ref[...] = jnp.ones_like(out_ref)
         for h in range(heads):
@@ -127,44 +117,52 @@
 
     return pl.pallas_call(
         body,
-        in_specs=[in_smem(), *in_vmem(2)],
+        in_specs=[in_smem(), *in_vmem(3)],
         out_specs=in_vmem(1)[0],
         out_shape=held((2, slots, m), F32),
         name="stats",
-    )(start, vmem(queries), vmem(keys))
+    )(start, vmem(queries), vmem(keys), vmem(values))
 
 
 def query_kernel(start, queries, grads, keys, values, stats, row_count, key_total):
     m = queries.shape[0]
     key_count, here = keys.shape
     heads = here // HEAD_DIM
+    slots = stats.shape[1]
     scaling = HEAD_DIM ** (-0.5)
 
     def body(start_ref, q_ref, g_ref, k_ref, v_ref, l_ref, u_ref, p_ref, ds_ref):
         visible = visible_of(start_ref, (key_count, m), row_count, key_total)
         extra = g_ref[:, pl.ds(here, LANES)]
-        slot = lax.broadcasted_iota(jnp.int32, (l_ref.shape[1], LANES), 0)
-        lane = lax.broadcasted_iota(jnp.int32, (l_ref.shape[1], LANES), 1)
+        slot = lax.broadcasted_iota(jnp.int32, (slots, LANES), 0)
+        lane = lax.broadcasted_iota(jnp.int32, (slots, LANES), 1)
         pick = (lane % heads == slot) & (lane < 3 * heads)
         delta = nt(jnp.where(pick, 1.0, 0.0).astype(BF), extra)
-        log_total = l_ref[0] + jnp.log(l_ref[1])
+        tops = l_ref[0]
         for h in range(heads):
             at = head_of(h)
             k = k_ref[:, at]
             s = nt(k, q_ref[:, at]) * scaling
-            prob = jnp.where(visible, jnp.exp(s - log_total[h : h + 1, :]), 0.0)
+            prob = jnp.where(visible, jnp.exp(s - tops[h : h + 1, :]), 0.0)
             ds = prob * (nt(v_ref[:, at], g_ref[:, at]) - delta[h : h + 1, :]) * scaling
             ds = ds.astype(BF)
             u_ref[:, at] = tn(ds, k).astype(BF)
             p_ref[h] = prob.astype(BF)
             ds_ref[h] = ds
+        sent = jnp.zeros((m, LANES), F32)
+        for i in range(2):
+            for part, value in enumerate(split3(l_ref[i])):
+                at = (3 * i + part) * heads
+                place = (lane == at + slot) & (slot < heads)
+                sent += tn(value, jnp.where(place, 1.0, 0.0).astype(BF))
+        u_ref[:, pl.ds(here, LANES)] = sent.astype(BF)
 
     return pl.pallas_call(
         body,
         in_specs=[in_smem(), *in_vmem(5)],
         out_specs=in_vmem(3),
         out_shape=[
-            jax.ShapeDtypeStruct((m, here), BF),
+            jax.ShapeDtypeStruct((m, here + LANES), BF),
             held((heads, key_count, m), BF),
             held((heads, key_count, m), BF),
         ],
@@ -172,23 +170,64 @@
     )(start, vmem(queries), vmem(grads), vmem(keys), vmem(values), vmem(stats))
 
 
-def cache_kernel(queries, grads, probs, score_grads):
+def cache_kernel(queries, grads, probs, score_grads, own, merged):
     here = queries.shape[1]
     heads, key_count, _ = probs.shape
 
-    def body(q_ref, g_ref, p_ref, ds_ref, dk_ref, dv_ref):
+    def body(q_ref, g_ref, p_ref, ds_ref, own_ref, all_ref, dk_ref, dv_ref):
+        share = jnp.exp(own_ref[0] - all_ref[0]) / all_ref[1]
         for h in range(heads):
             at = head_of(h)
-            dk_ref[:, at] = nn(ds_ref[h], q_ref[:, at]).astype(BF)
-            dv_ref[:, at] = nn(p_ref[h], g_ref[:, at]).astype(BF)
-
-    return pl.pallas_call(
-        body,
-        in_specs=in_vmem(4),
+            row = share[h : h + 1, :]
+            ds = (ds_ref[h].astype(F32) * row).astype(BF)
+            prob = (p_ref[h].astype(F32) * row).astype(BF)
+            dk_ref[:, at] = nn(ds, q_ref[:, at]).astype(BF)
+            dv_ref[:, at] = nn(prob, g_ref[:, at]).astype(BF)
+
+    return pl.pallas_call(
+        body,
+        in_specs=in_vmem(6),
         out_specs=in_vmem(2),
         out_shape=[jax.ShapeDtypeStruct((key_count, here), BF)] * 2,
         name="cache_gradients",
-    )(vmem(queries), vmem(grads), vmem(probs), vmem(score_grads))
+    )(vmem(queries), vmem(grads), vmem(probs), vmem(score_grads), vmem(own), vmem(merged))
+
+
+def combine_kernel(parts):
+    sections, holders, rows, width = parts.shape
+    here = width - LANES
+    heads = here // HEAD_DIM
+
+    def body(p_ref, out_ref):
+        def stats_of(s, c):
+            e = p_ref[s, c, :, pl.ds(here, LANES)].astype(F32)
+            e += pltpu.roll(e, LANES - heads, 1) + pltpu.roll(e, LANES - 2 * heads, 1)
+            return e, pltpu.roll(e, LANES - 3 * heads, 1)
+
+        for s in range(sections):
+            top = jnp.full((rows, LANES), -jnp.inf, F32)
+            for c in range(holders):
+                top = jnp.maximum(top, stats_of(s, c)[0])
+            total = jnp.zeros((rows, LANES), F32)
+            for c in range(holders):
+                own, count = stats_of(s, c)
+                total += jnp.exp(own - top) * count
+            sums = [jnp.zeros((rows, HEAD_DIM), F32) for _ in range(heads)]
+            for c in range(holders):
+                share = jnp.exp(stats_of(s, c)[0] - top) / total
+                for h in range(heads):
+                    value = p_ref[s, c, :, head_of(h)].astype(F32)
+                    sums[h] += share[:, h : h + 1] * value
+            for h in range(heads):
+                out_ref[:, head_of(s * heads + h)] = sums[h].astype(BF)
+
+    return pl.pallas_call(
+        body,
+        in_specs=in_vmem(1),
+        out_specs=in_vmem(1)[0],
+        out_shape=jax.ShapeDtypeStruct((rows, sections * here), BF),
+        name="combine",
+    )(vmem(parts))
 
 
 def merge_stats(stats, axis, count):
@@ -221,20 +260,21 @@
         first = lax.index_in_dim(blocks, 0, bits - 1, keepdims=False)
         second = lax.index_in_dim(blocks, 1, bits - 1, keepdims=False)
         mine = jnp.where(upper, second, first)
-        other = flip(jnp.where(upper, first, second), axis, 1 << i)
+        other = jnp.where(upper, first, second)
+        other = flip(other, axis, 1 << i)
         blocks = ordered(mine, other, upper, 0)
     return blocks.reshape((count,) + rest)
 
 
-def spread_blocks(blocks, axis):
+def spread_blocks(blocks, axis, order):
     count = lax.axis_size(axis)
-    bits = count.bit_length() - 1
     lead, rest = blocks.shape[0], blocks.shape[1:]
-    for i in range(bits):
-        bit = count >> (i + 1)
-        upper = lax.axis_index(axis) & bit != 0
-        other = flip(blocks, axis, bit)
-        blocks = ordered(blocks, other, upper, i + 1)
+    done = []
+    for bit in order:
+        upper = lax.axis_index(axis) & (1 << bit) != 0
+        other = flip(blocks, axis, 1 << bit)
+        blocks = ordered(blocks, other, upper, 1 + sum(b > bit for b in done))
+        done.append(bit)
     return blocks.reshape((lead, count) + rest)
 
 
@@ -247,7 +287,7 @@
     ctx_count = lax.axis_size("ctx")
     assert ctx_count & (ctx_count - 1) == 0
     assert sections & (sections - 1) == 0
-    layers, rows, features = queries.shape
+    layers, rows, _ = queries.shape
     assert layers == 1
     key_count, here = cache_keys.shape
     row_count = rows * ctx_count
@@ -255,21 +295,27 @@
     peers = sections * ctx_count
     start = (block_order[lax.axis_index("ctx")] * key_count).reshape(1)
 
-    sent, own = pack(queries[0], output_grad[0], attention_out[0], sections, ctx_count)
-    query_all = exchange(sent.reshape(peers, rows, here)).reshape(-1, here)
-    own = spread_blocks(swap_blocks(own, "section"), "ctx")
-    grad_all = own.reshape(peers * rows, -1)
-
-    stats = stats_kernel(start, query_all, cache_keys, row_count, key_total)
-    stats = merge_stats(stats, "ctx", ctx_count)
+    ctx_bits = ctx_count.bit_length() - 1
+    down = list(range(ctx_bits))[::-1]
+
+    sent = queries.reshape(rows, sections, here).transpose(1, 0, 2)
+    sent = swap_blocks(sent, "section")
+    query_all = spread_blocks(sent, "ctx", down)
+    query_all = query_all.reshape(peers * rows, here)
+    sent = pack(output_grad[0], attention_out[0], sections)
+    sent = swap_blocks(sent, "section")
+    grad_all = spread_blocks(sent, "ctx", down[:1] + down[1:][::-1])
+    grad_all = grad_all.reshape(peers * rows, here + LANES)
+
+    own = stats_kernel(start, query_all, cache_keys, cache_values, row_count, key_total)
+    merged = merge_stats(own, "ctx", ctx_count)
     part, probs, score_grads = query_kernel(
-        start, query_all, grad_all, cache_keys, cache_values, stats, row_count, key_total
+        start, query_all, grad_all, cache_keys, cache_values, own, row_count, key_total
     )
-    part = exchange(part.reshape(peers, rows, here))
-    grad_keys, grad_values = cache_kernel(query_all, grad_all, probs, score_grads)
-    part = part.reshape(sections, ctx_count, rows, here).astype(F32).sum(axis=1)
-    grad_queries = part.transpose(1, 0, 2).reshape(1, rows, features).astype(BF)
-    return (grad_queries, grad_keys, grad_values)
+    part = exchange(part.reshape(peers, rows, here + LANES))
+    grad_keys, grad_values = cache_kernel(query_all, grad_all, probs, score_grads, own, merged)
+    grad_queries = combine_kernel(part.reshape(sections, ctx_count, rows, here + LANES))
+    return (grad_queries[None], grad_keys, grad_values)
 
 
 def solution(mesh):

time: 58.1 us -> 57.3 us (0.986)
  waiting for transfers between devices: 29.2 us -> 18.9 us
  starting transfers between devices: 19.9 us -> 27.1 us
  Pallas kernels: 5.04 us -> 6.03 us
  local copies, waits for them, and re-layouts: 1.25 us -> 2.17 us
    all_to_all x2 -> x1, waiting for transfers between devices: 13.7 us -> 1.11 us  [exchange(): return lax.all_to_all(blocks, ('section', 'ctx'), 0, 0, tiled=True)]
    ppermute x8 -> x13, starting transfers between devices: 13.1 us -> 22.6 us  [flip(): return lax.ppermute(value, axis, [(i, i ^ bit) for i in range(count)])]
    all_to_all x2 -> x1, starting transfers between devices: 6.82 us -> 4.48 us  [exchange(): return lax.all_to_all(blocks, ('section', 'ctx'), 0, 0, tiled=True)]
    ppermute x8 -> x13, waiting for transfers between devices: 15.5 us -> 17.8 us  [flip(): return lax.ppermute(value, axis, [(i, i ^ bit) for i in range(count)])]
    unnamed x6 -> x8, local copies, waits for them, and re-layouts: 0.66 us -> 1.59 us
    select_n x2 -> x4, other arithmetic: 0.02 us -> 0.78 us  [swap_blocks(): other = jnp.where(upper, first, second)]
    pallas_call x3 -> x4, Pallas kernels: 3.01 us -> 3.72 us  [the longest x1 1.36 us: combine_kernel(): pl.pallas_call(body, in_specs=in_vmem(1), out_specs=in_vmem(1)[0], out_sh...]
    reduce_sum x1 -> x0, other arithmetic: 0.66 us -> none  [compute(): part = part.reshape(sections, ctx_count, rows, here).astype(F32).sum(axis=1)]
  transfers between devices with their start and end apart: 10 -> 14, of which waited for: 9 -> 9; matrix products, arithmetic and copies ran while one was open for 1% -> 2% of each run, Pallas kernels for 2% -> 3%
where the time goes in v4:
time: 57.3 us; the launch traced here: 56.9 us
  starting transfers between devices  27.1 us (47%)
  waiting for transfers between devices  18.9 us (33%)
  Pallas kernels  6.03 us (11%)
  local copies, waits for them, and re-layouts  2.17 us (4%)
  between operations  1.54 us (3%)
  other arithmetic  1.19 us (2%)
    ppermute x13, starting transfers between devices, flip(): return lax.ppermute(value, axis, [(i, i ^ bit) for i in range(count)])  22.6 us
    ppermute x13, waiting for transfers between devices, flip(): return lax.ppermute(value, axis, [(i, i ^ bit) for i in range(count)])  17.8 us
    all_to_all x1, starting transfers between devices, exchange(): return lax.all_to_all(blocks, ('section', 'ctx'), 0, 0, tiled=True)  4.48 us
    pallas_call x1, Pallas kernels, query_kernel(): pl.pallas_call(body, in_specs=[in_smem(), *in_vmem(5)], out_specs=in_vmem...  2.31 us
    unnamed x8, local copies, waits for them, and re-layouts  1.59 us
    pallas_call x1, Pallas kernels, combine_kernel(): pl.pallas_call(body, in_specs=in_vmem(1), out_specs=in_vmem(1)[0], out_sh...  1.36 us
  transfers between devices with their start and end apart: 14, of which 9 were waited for; matrix products, arithmetic and copies ran while one was open for 2% of the time, Pallas kernels for 3%

profile of v4, /device:TPU:0, one launch (start us, length us, event | category | flops | bytes accessed | tf_op | source)
XLA Modules:
  0.0 56.9 jit_solution(3433999891603962682)
XLA Ops:
  1.9 0.9 %pack.1 = bf16[4,8,768]{2,1,0:T(8,128)(2,1)S(1)} custom-call(bf16[8,2560]{1,0:T(8,128)(2,1)} %bitcast.172, bf16[8,2560]{1,0:T(8,128)(2,1)} %bitcast.173), custom_call_target="tpu_custom_call" | custom-call | tf_op jit(solution)/shard_map/pack/pallas_call | solution.py:85
  4.9 3.0 %collective-permute-start.1 = (bf16[2,8,640]{2,1,0:T(8,128)(2,1)S(1)}, bf16[2,8,640]{2,1,0:T(8,128)(2,1)S(1)}, u32[]{:S(2)}, u32[]{:S(2)}) collective-permute-start(bf16[2,8,640]{2,1,0:T(8,128)(2,1)S(1)} %select_bitcast_fusion.16), channel_id=1, source_target_pairs={{0,16},{8,24},{16,0},{24,8},{1,17},{9,25},{17,1},{25,9},{2,18},{10... | collective-permute-start | bytes 61448 | tf_op jit(solution)/shard_map/ppermute | solution.py:244
  8.0 1.6 %collective-permute-done.1 = bf16[2,8,640]{2,1,0:T(8,128)(2,1)S(1)} collective-permute-done((bf16[2,8,640]{2,1,0:T(8,128)(2,1)S(1)}, bf16[2,8,640]{2,1,0:T(8,128)(2,1)S(1)}, u32[]{:S(2)}, u32[]{:S(2)}) %collective-permute-start.1) | collective-permute-done | bytes 20512 | tf_op jit(solution)/shard_map/ppermute | solution.py:244
  9.7 3.2 %collective-permute-start.2 = (bf16[4,8,640]{2,1,0:T(8,128)(2,1)S(1)}, bf16[4,8,640]{2,1,0:T(8,128)(2,1)S(1)}, u32[]{:S(2)}, u32[]{:S(2)}) collective-permute-start(bf16[4,8,640]{2,1,0:T(8,128)(2,1)S(1)} %bitcast.169), channel_id=1, source_target_pairs={{0,4},{1,5},{2,6},{3,7},{4,0},{5,1},{6,2},{7,3},{8,12},{9,13},{10,... | collective-permute-start | bytes 122888 | tf_op jit(solution)/shard_map/ppermute | solution.py:244
  12.9 1.6 %collective-permute-start.7 = (bf16[4,8,768]{2,1,0:T(8,128)(2,1)S(1)}, bf16[4,8,768]{2,1,0:T(8,128)(2,1)S(1)}, u32[]{:S(2)}, u32[]{:S(2)}) collective-permute-start(bf16[4,8,768]{2,1,0:T(8,128)(2,1)S(1)} %bitcast.168), channel_id=1, source_target_pairs={{0,4},{1,5},{2,6},{3,7},{4,0},{5,1},{6,2},{7,3},{8,12},{9,13},{10,... | collective-permute-start | bytes 147464 | tf_op jit(solution)/shard_map/ppermute | solution.py:244
  14.9 2.1 %collective-permute-start.3 = (bf16[4,2,8,640]{3,2,1,0:T(8,128)(2,1)S(1)}, bf16[4,2,8,640]{3,2,1,0:T(8,128)(2,1)S(1)}, u32[]{:S(2)}, u32[]{:S(2)}) collective-permute-start(bf16[4,2,8,640]{3,2,1,0:T(8,128)(2,1)S(1)} %pad_maximum_fusion.5), channel_id=1, source_target_pairs={{0,2},{1,3},{2,0},{3,1},{4,6},{5,7},{6,4},{7,5},{8,10},{9,11},{10,... | collective-permute-start | bytes 245768 | tf_op jit(solution)/shard_map/ppermute | solution.py:244
  17.0 1.0 %collective-permute-done.7 = bf16[4,8,768]{2,1,0:T(8,128)(2,1)S(1)} collective-permute-done((bf16[4,8,768]{2,1,0:T(8,128)(2,1)S(1)}, bf16[4,8,768]{2,1,0:T(8,128)(2,1)S(1)}, u32[]{:S(2)}, u32[]{:S(2)}) %collective-permute-start.7) | collective-permute-done | bytes 49184 | tf_op jit(solution)/shard_map/ppermute | solution.py:244
  18.0 1.6 %collective-permute-start.8 = (bf16[4,2,8,768]{3,2,1,0:T(8,128)(2,1)S(1)}, bf16[4,2,8,768]{3,2,1,0:T(8,128)(2,1)S(1)}, u32[]{:S(2)}, u32[]{:S(2)}) collective-permute-start(bf16[4,2,8,768]{3,2,1,0:T(8,128)(2,1)S(1)} %pad_maximum_fusion.4), channel_id=1, source_target_pairs={{0,1},{1,0},{2,3},{3,2},{4,5},{5,4},{6,7},{7,6},{8,9},{9,8},{10,11... | collective-permute-start | bytes 294920 | tf_op jit(solution)/shard_map/ppermute | solution.py:244
  19.7 1.8 %collective-permute-start.4 = (bf16[4,2,2,8,640]{4,3,2,1,0:T(8,128)(2,1)S(1)}, bf16[4,2,2,8,640]{4,3,2,1,0:T(8,128)(2,1)S(1)}, u32[]{:S(2)}, u32[]{:S(2)}) collective-permute-start(bf16[4,2,2,8,640]{4,3,2,1,0:T(8,128)(2,1)S(1)} %pad_maximum_fusion.3), channel_id=1, source_target_pairs={{0,1},{1,0},{2,3},{3,2},{4,5},{5,4},{6,7},{7,6},{8,9},{9,8},{10,11... | collective-permute-start | bytes 491528 | tf_op jit(solution)/shard_map/ppermute | solution.py:244
  21.5 1.2 %collective-permute-done.8 = bf16[4,2,8,768]{3,2,1,0:T(8,128)(2,1)S(1)} collective-permute-done((bf16[4,2,8,768]{3,2,1,0:T(8,128)(2,1)S(1)}, bf16[4,2,8,768]{3,2,1,0:T(8,128)(2,1)S(1)}, u32[]{:S(2)}, u32[]{:S(2)}) %collective-permute-start.8) | collective-permute-done | bytes 98336 | tf_op jit(solution)/shard_map/ppermute | solution.py:244
  22.7 2.3 %collective-permute-done.4 = bf16[4,2,2,8,640]{4,3,2,1,0:T(8,128)(2,1)S(1)} collective-permute-done((bf16[4,2,2,8,640]{4,3,2,1,0:T(8,128)(2,1)S(1)}, bf16[4,2,2,8,640]{4,3,2,1,0:T(8,128)(2,1)S(1)}, u32[]{:S(2)}, u32[]{:S(2)}) %collective-permute-start.4) | collective-permute-done | bytes 163872 | tf_op jit(solution)/shard_map/ppermute | solution.py:244
  25.2 0.8 %copy-done = bf16[128,640]{1,0:T(8,128)(2,1)S(1)} copy-done((bf16[128,640]{1,0:T(8,128)(2,1)S(1)}, bf16[128,640]{1,0:T(8,128)(2,1)}, u32[]{:S(2)}) %copy-start) | copy-done | bytes 163864
  26.5 3.0 %collective-permute-start.10 = (f32[2,8,256]{2,1,0:T(8,128)S(1)}, f32[2,8,256]{2,1,0:T(8,128)S(1)}, u32[]{:S(2)}, u32[]{:S(2)}) collective-permute-start(f32[2,8,256]{2,1,0:T(8,128)S(1)} %stats.1.l_ref.own_ref), channel_id=1, source_target_pairs={{0,4},{1,5},{2,6},{3,7},{4,0},{5,1},{6,2},{7,3},{8,12},{9,13},{10,... | collective-permute-start | bytes 49160 | tf_op jit(solution)/shard_map/ppermute | solution.py:244
  29.5 2.1 %collective-permute-start.9 = (bf16[4,2,2,8,768]{4,3,2,1,0:T(8,128)(2,1)S(1)}, bf16[4,2,2,8,768]{4,3,2,1,0:T(8,128)(2,1)S(1)}, u32[]{:S(2)}, u32[]{:S(2)}) collective-permute-start(bf16[4,2,2,8,768]{4,3,2,1,0:T(8,128)(2,1)S(1)} %pad_maximum_fusion.2), channel_id=1, source_target_pairs={{0,2},{1,3},{2,0},{3,1},{4,6},{5,7},{6,4},{7,5},{8,10},{9,11},{10,... | collective-permute-start | bytes 589832 | tf_op jit(solution)/shard_map/ppermute | solution.py:244
  31.6 3.6 %collective-permute-done.9 = bf16[4,2,2,8,768]{4,3,2,1,0:T(8,128)(2,1)S(1)} collective-permute-done((bf16[4,2,2,8,768]{4,3,2,1,0:T(8,128)(2,1)S(1)}, bf16[4,2,2,8,768]{4,3,2,1,0:T(8,128)(2,1)S(1)}, u32[]{:S(2)}, u32[]{:S(2)}) %collective-permute-start.9) | collective-permute-done | bytes 196640 | tf_op jit(solution)/shard_map/ppermute | solution.py:244
  35.3 2.3 %query_gradients.1 = (bf16[256,768]{1,0:T(8,128)(2,1)}, bf16[5,128,256]{2,1,0:T(8,128)(2,1)S(1)}, bf16[5,128,256]{2,1,0:T(8,128)(2,1)S(1)}) custom-call(s32[1]{0:T(128)S(6)} %mul.34.start_ref, bf16[256,640]{1,0:T(8,128)(2,1)S(1)} %bitcast.160, bf16[256,768]{1,0:T(8,128)(2,1)S(1)} %bitcast.162, bf16[128,640]{1,0:T(8,128)(2,1)S(1)} %copy-done, ...), custom_call_target="tpu_custom_call" | custom-call | tf_op jit(solution)/shard_map/query_gradients/pallas_call | solution.py:160
  37.6 4.5 %all-to-all-start = ((bf16[32,8,768]{2,1,0:T(8,128)(2,1)}), bf16[32,8,768]{2,1,0:T(8,128)(2,1)S(1)}, u32[]{:S(2)}, u32[]{:S(2)}) async-start(bf16[32,8,768]{2,1,0:T(8,128)(2,1)} %bitcast.167), calls=%async_computation | async-start | bytes 786432 | tf_op jit(solution)/shard_map/all_to_all | solution.py:282
  42.1 1.8 %collective-permute-start.11 = (f32[2,8,256]{2,1,0:T(8,128)S(1)}, f32[2,8,256]{2,1,0:T(8,128)S(1)}, u32[]{:S(2)}, u32[]{:S(2)}) collective-permute-start(f32[2,8,256]{2,1,0:T(8,128)S(1)} %pad_maximum_fusion.10), channel_id=1, source_target_pairs={{0,2},{1,3},{2,0},{3,1},{4,6},{5,7},{6,4},{7,5},{8,10},{9,11},{10,... | collective-permute-start | bytes 49160 | tf_op jit(solution)/shard_map/ppermute | solution.py:244
  44.0 5.6 %collective-permute-done.11 = f32[2,8,256]{2,1,0:T(8,128)S(1)} collective-permute-done((f32[2,8,256]{2,1,0:T(8,128)S(1)}, f32[2,8,256]{2,1,0:T(8,128)S(1)}, u32[]{:S(2)}, u32[]{:S(2)}) %collective-permute-start.11) | collective-permute-done | bytes 16416 | tf_op jit(solution)/shard_map/ppermute | solution.py:244
  49.6 1.7 %collective-permute-start.12 = (f32[2,8,256]{2,1,0:T(8,128)S(1)}, f32[2,8,256]{2,1,0:T(8,128)S(1)}, u32[]{:S(2)}, u32[]{:S(2)}) collective-permute-start(f32[2,8,256]{2,1,0:T(8,128)S(1)} %pad_maximum_fusion.11), channel_id=1, source_target_pairs={{0,1},{1,0},{2,3},{3,2},{4,5},{5,4},{6,7},{7,6},{8,9},{9,8},{10,11... | collective-permute-start | bytes 49160 | tf_op jit(solution)/shard_map/ppermute | solution.py:244
  51.3 2.1 %collective-permute-done.12 = f32[2,8,256]{2,1,0:T(8,128)S(1)} collective-permute-done((f32[2,8,256]{2,1,0:T(8,128)S(1)}, f32[2,8,256]{2,1,0:T(8,128)S(1)}, u32[]{:S(2)}, u32[]{:S(2)}) %collective-permute-start.12) | collective-permute-done | bytes 16416 | tf_op jit(solution)/shard_map/ppermute | solution.py:244
  53.4 1.0 %cache_gradients.1 = (bf16[128,640]{1,0:T(8,128)(2,1)}, bf16[128,640]{1,0:T(8,128)(2,1)}) custom-call(bf16[256,640]{1,0:T(8,128)(2,1)S(1)} %bitcast.161, bf16[256,768]{1,0:T(8,128)(2,1)S(1)} %bitcast.163, bf16[5,128,256]{2,1,0:T(8,128)(2,1)S(1)} %get-tuple-element.9.p_ref, bf16[5,128,256]{2,1,0:T(8,128)(2,1)S(1)} %get-tuple-element.10.ds_ref, ...), custom_call_target="tpu_custom_call" | custom-call | tf_op jit(solution)/shard_map/cache_gradients/pallas_call | solution.py:187
  54.4 1.1 %all-to-all-done = bf16[32,8,768]{2,1,0:T(8,128)(2,1)S(1)} async-done(((bf16[32,8,768]{2,1,0:T(8,128)(2,1)}), bf16[32,8,768]{2,1,0:T(8,128)(2,1)S(1)}, u32[]{:S(2)}, u32[]{:S(2)}) %all-to-all-start) | async-done | bytes 393248 | tf_op jit(solution)/shard_map/all_to_all | solution.py:282
  55.5 1.4 %combine.1 = bf16[8,2560]{1,0:T(8,128)(2,1)} custom-call(bf16[4,8,8,768]{3,2,1,0:T(8,128)(2,1)S(1)} %bitcast.164), custom_call_target="tpu_custom_call" | custom-call | tf_op jit(solution)/shard_map/combine/pallas_call | solution.py:224
  (46 shorter events, 4.0 us)
Async XLA Ops:
  1.4 3.4 %collective-permute-start = (bf16[2,8,640]{2,1,0:T(8,128)(2,1)S(1)}, bf16[2,8,640]{2,1,0:T(8,128)(2,1)S(1)}, u32[]{:S(2)}, u32[]{:S(2)}) collective-permute-start(bf16[2,8,640]{2,1,0:T(8,128)(2,1)S(1)} %select_bitcast_fusion.17), channel_id=1, source_target_pairs={{0,8},{8,0},{16,24},{24,16},{1,9},{9,1},{17,25},{25,17},{2,10},{10... | collective-permute-start | bytes 61448 | tf_op jit(solution)/shard_map/ppermute | solution.py:244
  2.8 2.0 %copy-start.2 = (bf16[1,8,2560]{2,1,0:T(8,128)(2,1)S(1)}, bf16[1,8,2560]{2,1,0:T(8,128)(2,1)}, u32[]{:S(2)}) copy-start(bf16[1,8,2560]{2,1,0:T(8,128)(2,1)} %param.7) | copy-start | bytes 122884
  2.8 5.1 %collective-permute-start.5 = (bf16[2,8,768]{2,1,0:T(8,128)(2,1)S(1)}, bf16[2,8,768]{2,1,0:T(8,128)(2,1)S(1)}, u32[]{:S(2)}, u32[]{:S(2)}) collective-permute-start(bf16[2,8,768]{2,1,0:T(8,128)(2,1)S(1)} %fusion.4), channel_id=1, source_target_pairs={{0,8},{8,0},{16,24},{24,16},{1,9},{9,1},{17,25},{25,17},{2,10},{10... | collective-permute-start | bytes 73736 | tf_op jit(solution)/shard_map/ppermute | solution.py:244
  2.9 0.7 %copy-start.3 = (s32[8]{0:T(128)S(1)}, s32[8]{0:T(128)}, u32[]{:S(2)}) copy-start(s32[8]{0:T(128)} %param.6) | copy-start | bytes 100
  4.9 4.8 %collective-permute-start.1 = (bf16[2,8,640]{2,1,0:T(8,128)(2,1)S(1)}, bf16[2,8,640]{2,1,0:T(8,128)(2,1)S(1)}, u32[]{:S(2)}, u32[]{:S(2)}) collective-permute-start(bf16[2,8,640]{2,1,0:T(8,128)(2,1)S(1)} %select_bitcast_fusion.16), channel_id=1, source_target_pairs={{0,16},{8,24},{16,0},{24,8},{1,17},{9,25},{17,1},{25,9},{2,18},{10... | collective-permute-start | bytes 61448 | tf_op jit(solution)/shard_map/ppermute | solution.py:244
  7.9 5.0 %collective-permute-start.6 = (bf16[2,8,768]{2,1,0:T(8,128)(2,1)S(1)}, bf16[2,8,768]{2,1,0:T(8,128)(2,1)S(1)}, u32[]{:S(2)}, u32[]{:S(2)}) collective-permute-start(bf16[2,8,768]{2,1,0:T(8,128)(2,1)S(1)} %fusion.3), channel_id=1, source_target_pairs={{0,16},{8,24},{16,0},{24,8},{1,17},{9,25},{17,1},{25,9},{2,18},{10... | collective-permute-start | bytes 73736 | tf_op jit(solution)/shard_map/ppermute | solution.py:244
  9.7 5.2 %collective-permute-start.2 = (bf16[4,8,640]{2,1,0:T(8,128)(2,1)S(1)}, bf16[4,8,640]{2,1,0:T(8,128)(2,1)S(1)}, u32[]{:S(2)}, u32[]{:S(2)}) collective-permute-start(bf16[4,8,640]{2,1,0:T(8,128)(2,1)S(1)} %bitcast.169), channel_id=1, source_target_pairs={{0,4},{1,5},{2,6},{3,7},{4,0},{5,1},{6,2},{7,3},{8,12},{9,13},{10,... | collective-permute-start | bytes 122888 | tf_op jit(solution)/shard_map/ppermute | solution.py:244
  12.9 5.1 %collective-permute-start.7 = (bf16[4,8,768]{2,1,0:T(8,128)(2,1)S(1)}, bf16[4,8,768]{2,1,0:T(8,128)(2,1)S(1)}, u32[]{:S(2)}, u32[]{:S(2)}) collective-permute-start(bf16[4,8,768]{2,1,0:T(8,128)(2,1)S(1)} %bitcast.168), channel_id=1, source_target_pairs={{0,4},{1,5},{2,6},{3,7},{4,0},{5,1},{6,2},{7,3},{8,12},{9,13},{10,... | collective-permute-start | bytes 147464 | tf_op jit(solution)/shard_map/ppermute | solution.py:244
  14.9 4.7 %collective-permute-start.3 = (bf16[4,2,8,640]{3,2,1,0:T(8,128)(2,1)S(1)}, bf16[4,2,8,640]{3,2,1,0:T(8,128)(2,1)S(1)}, u32[]{:S(2)}, u32[]{:S(2)}) collective-permute-start(bf16[4,2,8,640]{3,2,1,0:T(8,128)(2,1)S(1)} %pad_maximum_fusion.5), channel_id=1, source_target_pairs={{0,2},{1,3},{2,0},{3,1},{4,6},{5,7},{6,4},{7,5},{8,10},{9,11},{10,... | collective-permute-start | bytes 245768 | tf_op jit(solution)/shard_map/ppermute | solution.py:244
  18.0 4.7 %collective-permute-start.8 = (bf16[4,2,8,768]{3,2,1,0:T(8,128)(2,1)S(1)}, bf16[4,2,8,768]{3,2,1,0:T(8,128)(2,1)S(1)}, u32[]{:S(2)}, u32[]{:S(2)}) collective-permute-start(bf16[4,2,8,768]{3,2,1,0:T(8,128)(2,1)S(1)} %pad_maximum_fusion.4), channel_id=1, source_target_pairs={{0,1},{1,0},{2,3},{3,2},{4,5},{5,4},{6,7},{7,6},{8,9},{9,8},{10,11... | collective-permute-start | bytes 294920 | tf_op jit(solution)/shard_map/ppermute | solution.py:244
  19.7 5.4 %collective-permute-start.4 = (bf16[4,2,2,8,640]{4,3,2,1,0:T(8,128)(2,1)S(1)}, bf16[4,2,2,8,640]{4,3,2,1,0:T(8,128)(2,1)S(1)}, u32[]{:S(2)}, u32[]{:S(2)}) collective-permute-start(bf16[4,2,2,8,640]{4,3,2,1,0:T(8,128)(2,1)S(1)} %pad_maximum_fusion.3), channel_id=1, source_target_pairs={{0,1},{1,0},{2,3},{3,2},{4,5},{5,4},{6,7},{7,6},{8,9},{9,8},{10,11... | collective-permute-start | bytes 491528 | tf_op jit(solution)/shard_map/ppermute | solution.py:244
  25.1 0.9 %copy-start = (bf16[128,640]{1,0:T(8,128)(2,1)S(1)}, bf16[128,640]{1,0:T(8,128)(2,1)}, u32[]{:S(2)}) copy-start(bf16[128,640]{1,0:T(8,128)(2,1)} %k_ref.3) | copy-start | bytes 491524
  25.1 1.0 %copy-start.1 = (bf16[128,640]{1,0:T(8,128)(2,1)S(1)}, bf16[128,640]{1,0:T(8,128)(2,1)}, u32[]{:S(2)}) copy-start(bf16[128,640]{1,0:T(8,128)(2,1)} %v_ref.1) | copy-start | bytes 491524
  26.5 5.1 %collective-permute-start.10 = (f32[2,8,256]{2,1,0:T(8,128)S(1)}, f32[2,8,256]{2,1,0:T(8,128)S(1)}, u32[]{:S(2)}, u32[]{:S(2)}) collective-permute-start(f32[2,8,256]{2,1,0:T(8,128)S(1)} %stats.1.l_ref.own_ref), channel_id=1, source_target_pairs={{0,4},{1,5},{2,6},{3,7},{4,0},{5,1},{6,2},{7,3},{8,12},{9,13},{10,... | collective-permute-start | bytes 49160 | tf_op jit(solution)/shard_map/ppermute | solution.py:244
  29.5 5.7 %collective-permute-start.9 = (bf16[4,2,2,8,768]{4,3,2,1,0:T(8,128)(2,1)S(1)}, bf16[4,2,2,8,768]{4,3,2,1,0:T(8,128)(2,1)S(1)}, u32[]{:S(2)}, u32[]{:S(2)}) collective-permute-start(bf16[4,2,2,8,768]{4,3,2,1,0:T(8,128)(2,1)S(1)} %pad_maximum_fusion.2), channel_id=1, source_target_pairs={{0,2},{1,3},{2,0},{3,1},{4,6},{5,7},{6,4},{7,5},{8,10},{9,11},{10,... | collective-permute-start | bytes 589832 | tf_op jit(solution)/shard_map/ppermute | solution.py:244
  37.6 17.9 %all-to-all-start = ((bf16[32,8,768]{2,1,0:T(8,128)(2,1)}), bf16[32,8,768]{2,1,0:T(8,128)(2,1)S(1)}, u32[]{:S(2)}, u32[]{:S(2)}) async-start(bf16[32,8,768]{2,1,0:T(8,128)(2,1)} %bitcast.167), calls=%async_computation | async-start | bytes 786432 | tf_op jit(solution)/shard_map/all_to_all | solution.py:282
  42.1 7.4 %collective-permute-start.11 = (f32[2,8,256]{2,1,0:T(8,128)S(1)}, f32[2,8,256]{2,1,0:T(8,128)S(1)}, u32[]{:S(2)}, u32[]{:S(2)}) collective-permute-start(f32[2,8,256]{2,1,0:T(8,128)S(1)} %pad_maximum_fusion.10), channel_id=1, source_target_pairs={{0,2},{1,3},{2,0},{3,1},{4,6},{5,7},{6,4},{7,5},{8,10},{9,11},{10,... | collective-permute-start | bytes 49160 | tf_op jit(solution)/shard_map/ppermute | solution.py:244
  49.6 3.8 %collective-permute-start.12 = (f32[2,8,256]{2,1,0:T(8,128)S(1)}, f32[2,8,256]{2,1,0:T(8,128)S(1)}, u32[]{:S(2)}, u32[]{:S(2)}) collective-permute-start(f32[2,8,256]{2,1,0:T(8,128)S(1)} %pad_maximum_fusion.11), channel_id=1, source_target_pairs={{0,1},{1,0},{2,3},{3,2},{4,5},{5,4},{6,7},{7,6},{8,9},{9,8},{10,11... | collective-permute-start | bytes 49160 | tf_op jit(solution)/shard_map/ppermute | solution.py:244

commit v5 on v4

--- a/solution.py
+++ b/solution.py
@@ -64,12 +64,21 @@
     return pl.ds(h * HEAD_DIM, HEAD_DIM)
 
 
-def pack(grads, outs, sections):
+def pack(block_order, keys, values, grads, outs, sections):
     rows, features = grads.shape
     here = features // sections
     heads = here // HEAD_DIM
-
-    def body(g_ref, o_ref, out_ref):
+    key_count = keys.shape[0]
+
+    def body(order_ref, k_hbm, v_hbm, g_ref, o_ref, out_ref, start_ref, k_ref, v_ref, sems):
+        copies = [
+            pltpu.make_async_copy(k_hbm, k_ref, sems.at[0]),
+            pltpu.make_async_copy(v_hbm, v_ref, sems.at[1]),
+        ]
+        for copy in copies:
+            copy.start()
+        block = order_ref[lax.axis_index("ctx")]
+        start_ref[...] = jnp.full(start_ref.shape, block * key_count, jnp.int32)
         lane = lax.broadcasted_iota(jnp.int32, (rows, LANES), 1)
         for s in range(sections):
             extra = jnp.zeros((rows, LANES), F32)
@@ -81,30 +90,38 @@
                     extra = jnp.where(lane == part * heads + h, value.astype(F32), extra)
             out_ref[s, :, pl.ds(0, here)] = g_ref[:, pl.ds(s * here, here)]
             out_ref[s, :, pl.ds(here, LANES)] = extra.astype(BF)
-
-    return pl.pallas_call(
-        body,
-        in_specs=in_vmem(2),
-        out_specs=in_vmem(1)[0],
-        out_shape=held((sections, rows, here + LANES), BF),
+        for copy in copies:
+            copy.wait()
+
+    return pl.pallas_call(
+        body,
+        in_specs=[in_smem(), *[pl.BlockSpec(memory_space=pl.ANY)] * 2, *in_vmem(2)],
+        out_specs=in_vmem(4),
+        out_shape=[
+            held((sections, rows, here + LANES), BF),
+            held((8, LANES), jnp.int32),
+            held(keys.shape, BF),
+            held(values.shape, BF),
+        ],
+        scratch_shapes=[pltpu.SemaphoreType.DMA((2,))],
         name="pack",
-    )(grads, outs)
+    )(block_order, keys, values, grads, outs)
 
 
 def visible_of(start_ref, shape, row_count, key_total):
-    key_pos = start_ref[0] + lax.broadcasted_iota(jnp.int32, shape, 0)
+    key_pos = start_ref[0:1, 0:1] + lax.broadcasted_iota(jnp.int32, shape, 0)
     row = lax.broadcasted_iota(jnp.int32, shape, 1) % row_count
     return key_pos <= key_total - row_count + row
 
 
-def stats_kernel(start, queries, keys, values, row_count, key_total):
+def stats_kernel(start, queries, keys, row_count, key_total):
     m, here = queries.shape
     key_count = keys.shape[0]
     heads = here // HEAD_DIM
     slots = -(-heads // 8) * 8
     scaling = HEAD_DIM ** (-0.5)
 
-    def body(start_ref, q_ref, k_ref, _, out_ref):
+    def body(start_ref, q_ref, k_ref, out_ref):
         visible = visible_of(start_ref, (key_count, m), row_count, key_total)
         out_ref[...] = jnp.ones_like(out_ref)
         for h in range(heads):
@@ -117,11 +134,11 @@
 
     return pl.pallas_call(
         body,
-        in_specs=[in_smem(), *in_vmem(3)],
+        in_specs=in_vmem(3),
         out_specs=in_vmem(1)[0],
         out_shape=held((2, slots, m), F32),
         name="stats",
-    )(start, vmem(queries), vmem(keys), vmem(values))
+    )(vmem(start), vmem(queries), vmem(keys))
 
 
 def query_kernel(start, queries, grads, keys, values, stats, row_count, key_total):
@@ -159,7 +176,7 @@
 
     return pl.pallas_call(
         body,
-        in_specs=[in_smem(), *in_vmem(5)],
+        in_specs=in_vmem(6),
         out_specs=in_vmem(3),
         out_shape=[
             jax.ShapeDtypeStruct((m, here + LANES), BF),
@@ -167,7 +184,7 @@
             held((heads, key_count, m), BF),
         ],
         name="query_gradients",
-    )(start, vmem(queries), vmem(grads), vmem(keys), vmem(values), vmem(stats))
+    )(vmem(start), vmem(queries), vmem(grads), vmem(keys), vmem(values), vmem(stats))
 
 
 def cache_kernel(queries, grads, probs, score_grads, own, merged):
@@ -293,7 +310,6 @@
     row_count = rows * ctx_count
     key_total = key_count * ctx_count
     peers = sections * ctx_count
-    start = (block_order[lax.axis_index("ctx")] * key_count).reshape(1)
 
     ctx_bits = ctx_count.bit_length() - 1
     down = list(range(ctx_bits))[::-1]
@@ -302,15 +318,17 @@
     sent = swap_blocks(sent, "section")
     query_all = spread_blocks(sent, "ctx", down)
     query_all = query_all.reshape(peers * rows, here)
-    sent = pack(output_grad[0], attention_out[0], sections)
+    sent, start, keys, values = pack(
+        block_order, cache_keys, cache_values, output_grad[0], attention_out[0], sections
+    )
     sent = swap_blocks(sent, "section")
     grad_all = spread_blocks(sent, "ctx", down[:1] + down[1:][::-1])
     grad_all = grad_all.reshape(peers * rows, here + LANES)
 
-    own = stats_kernel(start, query_all, cache_keys, cache_values, row_count, key_total)
+    own = stats_kernel(start, query_all, keys, row_count, key_total)
     merged = merge_stats(own, "ctx", ctx_count)
     part, probs, score_grads = query_kernel(
-        start, query_all, grad_all, cache_keys, cache_values, own, row_count, key_total
+        start, query_all, grad_all, keys, values, own, row_count, key_total
     )
     part = exchange(part.reshape(peers, rows, here + LANES))
     grad_keys, grad_values = cache_kernel(query_all, grad_all, probs, score_grads, own, merged)

time: 57.3 us -> 56 us (0.977)
  local copies, waits for them, and re-layouts: 2.17 us -> 0.65 us
  Pallas kernels: 6.03 us -> 6.99 us
  between operations: 1.54 us -> 0.85 us
    unnamed x8 -> x2, local copies, waits for them, and re-layouts: 1.59 us -> 0.65 us
    pallas_call x3, Pallas kernels: 3.62 us -> 4.56 us  [the longest x1 2.33 us: query_kernel(): pl.pallas_call(body, in_specs=in_vmem(6), out_specs=in_vmem(3), out_shape...]
    dynamic_slice x1 -> x0, local copies, waits for them, and re-layouts: 0.58 us -> none  [compute(): start = (block_order[lax.axis_index('ctx')] * key_count).reshape(1)]
  transfers between devices with their start and end apart: 14 -> 14, of which waited for: 9 -> 9; matrix products, arithmetic and copies ran while one was open for 2% -> 1% of each run, Pallas kernels for 3% -> 5%
where the time goes in v5:
time: 56 us; the launch traced here: 55.6 us
  starting transfers between devices  27.3 us (49%)
  waiting for transfers between devices  18.5 us (33%)
  Pallas kernels  6.99 us (12%)
  other arithmetic  1.2 us (2%)
  between operations  0.85 us (2%)
  local copies, waits for them, and re-layouts  0.65 us (1%)
    ppermute x13, starting transfers between devices, flip(): return lax.ppermute(value, axis, [(i, i ^ bit) for i in range(count)])  22.9 us
    ppermute x13, waiting for transfers between devices, flip(): return lax.ppermute(value, axis, [(i, i ^ bit) for i in range(count)])  17.4 us
    all_to_all x1, starting transfers between devices, exchange(): return lax.all_to_all(blocks, ('section', 'ctx'), 0, 0, tiled=True)  4.46 us
    pallas_call x1, Pallas kernels, query_kernel(): pl.pallas_call(body, in_specs=in_vmem(6), out_specs=in_vmem(3), out_shape...  2.33 us
    pallas_call x1, Pallas kernels, pack(): pl.pallas_call(body, in_specs=[in_smem(), *[pl.BlockSpec(memory_space=pl....  1.82 us
    pallas_call x1, Pallas kernels, combine_kernel(): pl.pallas_call(body, in_specs=in_vmem(1), out_specs=in_vmem(1)[0], out_sh...  1.37 us
  transfers between devices with their start and end apart: 14, of which 9 were waited for; matrix products, arithmetic and copies ran while one was open for 1% of the time, Pallas kernels for 5%

profile of v5, /device:TPU:0, one launch (start us, length us, event | category | flops | bytes accessed | tf_op | source)
XLA Modules:
  0.0 55.6 jit_solution(2216065769678245392)
XLA Ops:
  0.6 0.8 %select_bitcast_fusion.17 = bf16[2,8,640]{2,1,0:T(8,128)(2,1)S(1)} fusion(pred[]{:T(512)S(6)} %eq.14, bf16[2,2,8,640]{3,2,1,0:T(8,128)(2,1)} %bitcast.170), kind=kLoop, calls=%fused_computation.51 | loop fusion | flops 10240 | bytes 61441 | tf_op jit(solution)/shard_map/jit(_where)/select_n | solution.py:280
  1.9 1.8 %pack.1 = (bf16[4,8,768]{2,1,0:T(8,128)(2,1)S(1)}, s32[8,128]{1,0:T(8,128)S(1)}, bf16[128,640]{1,0:T(8,128)(2,1)S(1)}, bf16[128,640]{1,0:T(8,128)(2,1)S(1)}) custom-call(s32[8]{0:T(128)} %order_ref.1, bf16[128,640]{1,0:T(8,128)(2,1)} %k_hbm.1, bf16[128,640]{1,0:T(8,128)(2,1)} %v_hbm.1, bf16[8,2560]{1,0:T(8,128)(2,1)} %bitcast.172, bf16[8,2560]{1,0:T(8,128)(2,1)} %bitcast.173), custom_call_target="tpu_custom_call" | custom-call | tf_op jit(solution)/shard_map/pack/pallas_call | solution.py:96
  4.5 2.6 %collective-permute-start.1 = (bf16[2,8,640]{2,1,0:T(8,128)(2,1)S(1)}, bf16[2,8,640]{2,1,0:T(8,128)(2,1)S(1)}, u32[]{:S(2)}, u32[]{:S(2)}) collective-permute-start(bf16[2,8,640]{2,1,0:T(8,128)(2,1)S(1)} %select_bitcast_fusion.16), channel_id=1, source_target_pairs={{0,16},{8,24},{16,0},{24,8},{1,17},{9,25},{17,1},{25,9},{2,18},{10... | collective-permute-start | bytes 61448 | tf_op jit(solution)/shard_map/ppermute | solution.py:261
  7.7 1.1 %collective-permute-done.1 = bf16[2,8,640]{2,1,0:T(8,128)(2,1)S(1)} collective-permute-done((bf16[2,8,640]{2,1,0:T(8,128)(2,1)S(1)}, bf16[2,8,640]{2,1,0:T(8,128)(2,1)S(1)}, u32[]{:S(2)}, u32[]{:S(2)}) %collective-permute-start.1) | collective-permute-done | bytes 20512 | tf_op jit(solution)/shard_map/ppermute | solution.py:261
  8.9 3.2 %collective-permute-start.2 = (bf16[4,8,640]{2,1,0:T(8,128)(2,1)S(1)}, bf16[4,8,640]{2,1,0:T(8,128)(2,1)S(1)}, u32[]{:S(2)}, u32[]{:S(2)}) collective-permute-start(bf16[4,8,640]{2,1,0:T(8,128)(2,1)S(1)} %bitcast.169), channel_id=1, source_target_pairs={{0,4},{1,5},{2,6},{3,7},{4,0},{5,1},{6,2},{7,3},{8,12},{9,13},{10,... | collective-permute-start | bytes 122888 | tf_op jit(solution)/shard_map/ppermute | solution.py:261
  12.1 1.6 %collective-permute-start.7 = (bf16[4,8,768]{2,1,0:T(8,128)(2,1)S(1)}, bf16[4,8,768]{2,1,0:T(8,128)(2,1)S(1)}, u32[]{:S(2)}, u32[]{:S(2)}) collective-permute-start(bf16[4,8,768]{2,1,0:T(8,128)(2,1)S(1)} %bitcast.168), channel_id=1, source_target_pairs={{0,4},{1,5},{2,6},{3,7},{4,0},{5,1},{6,2},{7,3},{8,12},{9,13},{10,... | collective-permute-start | bytes 147464 | tf_op jit(solution)/shard_map/ppermute | solution.py:261
  14.2 2.1 %collective-permute-start.3 = (bf16[4,2,8,640]{3,2,1,0:T(8,128)(2,1)S(1)}, bf16[4,2,8,640]{3,2,1,0:T(8,128)(2,1)S(1)}, u32[]{:S(2)}, u32[]{:S(2)}) collective-permute-start(bf16[4,2,8,640]{3,2,1,0:T(8,128)(2,1)S(1)} %pad_maximum_fusion.5), channel_id=1, source_target_pairs={{0,2},{1,3},{2,0},{3,1},{4,6},{5,7},{6,4},{7,5},{8,10},{9,11},{10,... | collective-permute-start | bytes 245768 | tf_op jit(solution)/shard_map/ppermute | solution.py:261
  16.3 0.8 %collective-permute-done.7 = bf16[4,8,768]{2,1,0:T(8,128)(2,1)S(1)} collective-permute-done((bf16[4,8,768]{2,1,0:T(8,128)(2,1)S(1)}, bf16[4,8,768]{2,1,0:T(8,128)(2,1)S(1)}, u32[]{:S(2)}, u32[]{:S(2)}) %collective-permute-start.7) | collective-permute-done | bytes 49184 | tf_op jit(solution)/shard_map/ppermute | solution.py:261
  17.2 1.6 %collective-permute-start.8 = (bf16[4,2,8,768]{3,2,1,0:T(8,128)(2,1)S(1)}, bf16[4,2,8,768]{3,2,1,0:T(8,128)(2,1)S(1)}, u32[]{:S(2)}, u32[]{:S(2)}) collective-permute-start(bf16[4,2,8,768]{3,2,1,0:T(8,128)(2,1)S(1)} %pad_maximum_fusion.4), channel_id=1, source_target_pairs={{0,1},{1,0},{2,3},{3,2},{4,5},{5,4},{6,7},{7,6},{8,9},{9,8},{10,11... | collective-permute-start | bytes 294920 | tf_op jit(solution)/shard_map/ppermute | solution.py:261
  18.8 1.7 %collective-permute-start.4 = (bf16[4,2,2,8,640]{4,3,2,1,0:T(8,128)(2,1)S(1)}, bf16[4,2,2,8,640]{4,3,2,1,0:T(8,128)(2,1)S(1)}, u32[]{:S(2)}, u32[]{:S(2)}) collective-permute-start(bf16[4,2,2,8,640]{4,3,2,1,0:T(8,128)(2,1)S(1)} %pad_maximum_fusion.3), channel_id=1, source_target_pairs={{0,1},{1,0},{2,3},{3,2},{4,5},{5,4},{6,7},{7,6},{8,9},{9,8},{10,11... | collective-permute-start | bytes 491528 | tf_op jit(solution)/shard_map/ppermute | solution.py:261
  20.6 1.9 %collective-permute-done.8 = bf16[4,2,8,768]{3,2,1,0:T(8,128)(2,1)S(1)} collective-permute-done((bf16[4,2,8,768]{3,2,1,0:T(8,128)(2,1)S(1)}, bf16[4,2,8,768]{3,2,1,0:T(8,128)(2,1)S(1)}, u32[]{:S(2)}, u32[]{:S(2)}) %collective-permute-start.8) | collective-permute-done | bytes 98336 | tf_op jit(solution)/shard_map/ppermute | solution.py:261
  22.5 1.7 %collective-permute-done.4 = bf16[4,2,2,8,640]{4,3,2,1,0:T(8,128)(2,1)S(1)} collective-permute-done((bf16[4,2,2,8,640]{4,3,2,1,0:T(8,128)(2,1)S(1)}, bf16[4,2,2,8,640]{4,3,2,1,0:T(8,128)(2,1)S(1)}, u32[]{:S(2)}, u32[]{:S(2)}) %collective-permute-start.4) | collective-permute-done | bytes 163872 | tf_op jit(solution)/shard_map/ppermute | solution.py:261
  24.7 3.4 %collective-permute-start.10 = (f32[2,8,256]{2,1,0:T(8,128)S(1)}, f32[2,8,256]{2,1,0:T(8,128)S(1)}, u32[]{:S(2)}, u32[]{:S(2)}) collective-permute-start(f32[2,8,256]{2,1,0:T(8,128)S(1)} %stats.1.l_ref.own_ref), channel_id=1, source_target_pairs={{0,4},{1,5},{2,6},{3,7},{4,0},{5,1},{6,2},{7,3},{8,12},{9,13},{10,... | collective-permute-start | bytes 49160 | tf_op jit(solution)/shard_map/ppermute | solution.py:261
  28.2 2.1 %collective-permute-start.9 = (bf16[4,2,2,8,768]{4,3,2,1,0:T(8,128)(2,1)S(1)}, bf16[4,2,2,8,768]{4,3,2,1,0:T(8,128)(2,1)S(1)}, u32[]{:S(2)}, u32[]{:S(2)}) collective-permute-start(bf16[4,2,2,8,768]{4,3,2,1,0:T(8,128)(2,1)S(1)} %pad_maximum_fusion.2), channel_id=1, source_target_pairs={{0,2},{1,3},{2,0},{3,1},{4,6},{5,7},{6,4},{7,5},{8,10},{9,11},{10,... | collective-permute-start | bytes 589832 | tf_op jit(solution)/shard_map/ppermute | solution.py:261
  30.3 3.6 %collective-permute-done.9 = bf16[4,2,2,8,768]{4,3,2,1,0:T(8,128)(2,1)S(1)} collective-permute-done((bf16[4,2,2,8,768]{4,3,2,1,0:T(8,128)(2,1)S(1)}, bf16[4,2,2,8,768]{4,3,2,1,0:T(8,128)(2,1)S(1)}, u32[]{:S(2)}, u32[]{:S(2)}) %collective-permute-start.9) | collective-permute-done | bytes 196640 | tf_op jit(solution)/shard_map/ppermute | solution.py:261
  34.0 2.3 %query_gradients.1 = (bf16[256,768]{1,0:T(8,128)(2,1)}, bf16[5,128,256]{2,1,0:T(8,128)(2,1)S(1)}, bf16[5,128,256]{2,1,0:T(8,128)(2,1)S(1)}) custom-call(s32[8,128]{1,0:T(8,128)S(1)} %get-tuple-element.12.start_ref, bf16[256,640]{1,0:T(8,128)(2,1)S(1)} %bitcast.160, bf16[256,768]{1,0:T(8,128)(2,1)S(1)} %bitcast.162, ...), custom_call_target="tpu_custom_call" | custom-call | tf_op jit(solution)/shard_map/query_gradients/pallas_call | solution.py:177
  36.3 4.5 %all-to-all-start = ((bf16[32,8,768]{2,1,0:T(8,128)(2,1)}), bf16[32,8,768]{2,1,0:T(8,128)(2,1)S(1)}, u32[]{:S(2)}, u32[]{:S(2)}) async-start(bf16[32,8,768]{2,1,0:T(8,128)(2,1)} %bitcast.167), calls=%async_computation | async-start | bytes 786432 | tf_op jit(solution)/shard_map/all_to_all | solution.py:299
  40.8 1.8 %collective-permute-start.11 = (f32[2,8,256]{2,1,0:T(8,128)S(1)}, f32[2,8,256]{2,1,0:T(8,128)S(1)}, u32[]{:S(2)}, u32[]{:S(2)}) collective-permute-start(f32[2,8,256]{2,1,0:T(8,128)S(1)} %pad_maximum_fusion.10), channel_id=1, source_target_pairs={{0,2},{1,3},{2,0},{3,1},{4,6},{5,7},{6,4},{7,5},{8,10},{9,11},{10,... | collective-permute-start | bytes 49160 | tf_op jit(solution)/shard_map/ppermute | solution.py:261
  42.6 5.6 %collective-permute-done.11 = f32[2,8,256]{2,1,0:T(8,128)S(1)} collective-permute-done((f32[2,8,256]{2,1,0:T(8,128)S(1)}, f32[2,8,256]{2,1,0:T(8,128)S(1)}, u32[]{:S(2)}, u32[]{:S(2)}) %collective-permute-start.11) | collective-permute-done | bytes 16416 | tf_op jit(solution)/shard_map/ppermute | solution.py:261
  48.2 1.7 %collective-permute-start.12 = (f32[2,8,256]{2,1,0:T(8,128)S(1)}, f32[2,8,256]{2,1,0:T(8,128)S(1)}, u32[]{:S(2)}, u32[]{:S(2)}) collective-permute-start(f32[2,8,256]{2,1,0:T(8,128)S(1)} %pad_maximum_fusion.11), channel_id=1, source_target_pairs={{0,1},{1,0},{2,3},{3,2},{4,5},{5,4},{6,7},{7,6},{8,9},{9,8},{10,11... | collective-permute-start | bytes 49160 | tf_op jit(solution)/shard_map/ppermute | solution.py:261
  49.9 2.1 %collective-permute-done.12 = f32[2,8,256]{2,1,0:T(8,128)S(1)} collective-permute-done((f32[2,8,256]{2,1,0:T(8,128)S(1)}, f32[2,8,256]{2,1,0:T(8,128)S(1)}, u32[]{:S(2)}, u32[]{:S(2)}) %collective-permute-start.12) | collective-permute-done | bytes 16416 | tf_op jit(solution)/shard_map/ppermute | solution.py:261
  52.0 1.1 %cache_gradients.1 = (bf16[128,640]{1,0:T(8,128)(2,1)}, bf16[128,640]{1,0:T(8,128)(2,1)}) custom-call(bf16[256,640]{1,0:T(8,128)(2,1)S(1)} %bitcast.161, bf16[256,768]{1,0:T(8,128)(2,1)S(1)} %bitcast.163, bf16[5,128,256]{2,1,0:T(8,128)(2,1)S(1)} %get-tuple-element.17.p_ref, bf16[5,128,256]{2,1,0:T(8,128)(2,1)S(1)} %get-tuple-element.18.ds_ref, ...), custom_call_target="tpu_custom_call" | custom-call | tf_op jit(solution)/shard_map/cache_gradients/pallas_call | solution.py:204
  53.1 1.1 %all-to-all-done = bf16[32,8,768]{2,1,0:T(8,128)(2,1)S(1)} async-done(((bf16[32,8,768]{2,1,0:T(8,128)(2,1)}), bf16[32,8,768]{2,1,0:T(8,128)(2,1)S(1)}, u32[]{:S(2)}, u32[]{:S(2)}) %all-to-all-start) | async-done | bytes 393248 | tf_op jit(solution)/shard_map/all_to_all | solution.py:299
  54.2 1.4 %combine.1 = bf16[8,2560]{1,0:T(8,128)(2,1)} custom-call(bf16[4,8,8,768]{3,2,1,0:T(8,128)(2,1)S(1)} %bitcast.164), custom_call_target="tpu_custom_call" | custom-call | tf_op jit(solution)/shard_map/combine/pallas_call | solution.py:241
  (39 shorter events, 3.2 us)
Async XLA Ops:
  1.4 2.5 %collective-permute-start = (bf16[2,8,640]{2,1,0:T(8,128)(2,1)S(1)}, bf16[2,8,640]{2,1,0:T(8,128)(2,1)S(1)}, u32[]{:S(2)}, u32[]{:S(2)}) collective-permute-start(bf16[2,8,640]{2,1,0:T(8,128)(2,1)S(1)} %select_bitcast_fusion.17), channel_id=1, source_target_pairs={{0,8},{8,0},{16,24},{24,16},{1,9},{9,1},{17,25},{25,17},{2,10},{10... | collective-permute-start | bytes 61448 | tf_op jit(solution)/shard_map/ppermute | solution.py:261
  3.7 0.8 %copy-start = (bf16[1,8,2560]{2,1,0:T(8,128)(2,1)S(1)}, bf16[1,8,2560]{2,1,0:T(8,128)(2,1)}, u32[]{:S(2)}) copy-start(bf16[1,8,2560]{2,1,0:T(8,128)(2,1)} %param.7) | copy-start | bytes 122884
  3.7 3.3 %collective-permute-start.5 = (bf16[2,8,768]{2,1,0:T(8,128)(2,1)S(1)}, bf16[2,8,768]{2,1,0:T(8,128)(2,1)S(1)}, u32[]{:S(2)}, u32[]{:S(2)}) collective-permute-start(bf16[2,8,768]{2,1,0:T(8,128)(2,1)S(1)} %fusion.4), channel_id=1, source_target_pairs={{0,8},{8,0},{16,24},{24,16},{1,9},{9,1},{17,25},{25,17},{2,10},{10... | collective-permute-start | bytes 73736 | tf_op jit(solution)/shard_map/ppermute | solution.py:261
  4.5 4.3 %collective-permute-start.1 = (bf16[2,8,640]{2,1,0:T(8,128)(2,1)S(1)}, bf16[2,8,640]{2,1,0:T(8,128)(2,1)S(1)}, u32[]{:S(2)}, u32[]{:S(2)}) collective-permute-start(bf16[2,8,640]{2,1,0:T(8,128)(2,1)S(1)} %select_bitcast_fusion.16), channel_id=1, source_target_pairs={{0,16},{8,24},{16,0},{24,8},{1,17},{9,25},{17,1},{25,9},{2,18},{10... | collective-permute-start | bytes 61448 | tf_op jit(solution)/shard_map/ppermute | solution.py:261
  7.1 5.0 %collective-permute-start.6 = (bf16[2,8,768]{2,1,0:T(8,128)(2,1)S(1)}, bf16[2,8,768]{2,1,0:T(8,128)(2,1)S(1)}, u32[]{:S(2)}, u32[]{:S(2)}) collective-permute-start(bf16[2,8,768]{2,1,0:T(8,128)(2,1)S(1)} %fusion.3), channel_id=1, source_target_pairs={{0,16},{8,24},{16,0},{24,8},{1,17},{9,25},{17,1},{25,9},{2,18},{10... | collective-permute-start | bytes 73736 | tf_op jit(solution)/shard_map/ppermute | solution.py:261
  8.9 5.3 %collective-permute-start.2 = (bf16[4,8,640]{2,1,0:T(8,128)(2,1)S(1)}, bf16[4,8,640]{2,1,0:T(8,128)(2,1)S(1)}, u32[]{:S(2)}, u32[]{:S(2)}) collective-permute-start(bf16[4,8,640]{2,1,0:T(8,128)(2,1)S(1)} %bitcast.169), channel_id=1, source_target_pairs={{0,4},{1,5},{2,6},{3,7},{4,0},{5,1},{6,2},{7,3},{8,12},{9,13},{10,... | collective-permute-start | bytes 122888 | tf_op jit(solution)/shard_map/ppermute | solution.py:261
  12.1 5.1 %collective-permute-start.7 = (bf16[4,8,768]{2,1,0:T(8,128)(2,1)S(1)}, bf16[4,8,768]{2,1,0:T(8,128)(2,1)S(1)}, u32[]{:S(2)}, u32[]{:S(2)}) collective-permute-start(bf16[4,8,768]{2,1,0:T(8,128)(2,1)S(1)} %bitcast.168), channel_id=1, source_target_pairs={{0,4},{1,5},{2,6},{3,7},{4,0},{5,1},{6,2},{7,3},{8,12},{9,13},{10,... | collective-permute-start | bytes 147464 | tf_op jit(solution)/shard_map/ppermute | solution.py:261
  14.2 4.5 %collective-permute-start.3 = (bf16[4,2,8,640]{3,2,1,0:T(8,128)(2,1)S(1)}, bf16[4,2,8,640]{3,2,1,0:T(8,128)(2,1)S(1)}, u32[]{:S(2)}, u32[]{:S(2)}) collective-permute-start(bf16[4,2,8,640]{3,2,1,0:T(8,128)(2,1)S(1)} %pad_maximum_fusion.5), channel_id=1, source_target_pairs={{0,2},{1,3},{2,0},{3,1},{4,6},{5,7},{6,4},{7,5},{8,10},{9,11},{10,... | collective-permute-start | bytes 245768 | tf_op jit(solution)/shard_map/ppermute | solution.py:261
  17.2 5.3 %collective-permute-start.8 = (bf16[4,2,8,768]{3,2,1,0:T(8,128)(2,1)S(1)}, bf16[4,2,8,768]{3,2,1,0:T(8,128)(2,1)S(1)}, u32[]{:S(2)}, u32[]{:S(2)}) collective-permute-start(bf16[4,2,8,768]{3,2,1,0:T(8,128)(2,1)S(1)} %pad_maximum_fusion.4), channel_id=1, source_target_pairs={{0,1},{1,0},{2,3},{3,2},{4,5},{5,4},{6,7},{7,6},{8,9},{9,8},{10,11... | collective-permute-start | bytes 294920 | tf_op jit(solution)/shard_map/ppermute | solution.py:261
  18.8 5.4 %collective-permute-start.4 = (bf16[4,2,2,8,640]{4,3,2,1,0:T(8,128)(2,1)S(1)}, bf16[4,2,2,8,640]{4,3,2,1,0:T(8,128)(2,1)S(1)}, u32[]{:S(2)}, u32[]{:S(2)}) collective-permute-start(bf16[4,2,2,8,640]{4,3,2,1,0:T(8,128)(2,1)S(1)} %pad_maximum_fusion.3), channel_id=1, source_target_pairs={{0,1},{1,0},{2,3},{3,2},{4,5},{5,4},{6,7},{7,6},{8,9},{9,8},{10,11... | collective-permute-start | bytes 491528 | tf_op jit(solution)/shard_map/ppermute | solution.py:261
  24.7 5.5 %collective-permute-start.10 = (f32[2,8,256]{2,1,0:T(8,128)S(1)}, f32[2,8,256]{2,1,0:T(8,128)S(1)}, u32[]{:S(2)}, u32[]{:S(2)}) collective-permute-start(f32[2,8,256]{2,1,0:T(8,128)S(1)} %stats.1.l_ref.own_ref), channel_id=1, source_target_pairs={{0,4},{1,5},{2,6},{3,7},{4,0},{5,1},{6,2},{7,3},{8,12},{9,13},{10,... | collective-permute-start | bytes 49160 | tf_op jit(solution)/shard_map/ppermute | solution.py:261
  28.2 5.7 %collective-permute-start.9 = (bf16[4,2,2,8,768]{4,3,2,1,0:T(8,128)(2,1)S(1)}, bf16[4,2,2,8,768]{4,3,2,1,0:T(8,128)(2,1)S(1)}, u32[]{:S(2)}, u32[]{:S(2)}) collective-permute-start(bf16[4,2,2,8,768]{4,3,2,1,0:T(8,128)(2,1)S(1)} %pad_maximum_fusion.2), channel_id=1, source_target_pairs={{0,2},{1,3},{2,0},{3,1},{4,6},{5,7},{6,4},{7,5},{8,10},{9,11},{10,... | collective-permute-start | bytes 589832 | tf_op jit(solution)/shard_map/ppermute | solution.py:261
  36.3 17.9 %all-to-all-start = ((bf16[32,8,768]{2,1,0:T(8,128)(2,1)}), bf16[32,8,768]{2,1,0:T(8,128)(2,1)S(1)}, u32[]{:S(2)}, u32[]{:S(2)}) async-start(bf16[32,8,768]{2,1,0:T(8,128)(2,1)} %bitcast.167), calls=%async_computation | async-start | bytes 786432 | tf_op jit(solution)/shard_map/all_to_all | solution.py:299
  40.8 7.4 %collective-permute-start.11 = (f32[2,8,256]{2,1,0:T(8,128)S(1)}, f32[2,8,256]{2,1,0:T(8,128)S(1)}, u32[]{:S(2)}, u32[]{:S(2)}) collective-permute-start(f32[2,8,256]{2,1,0:T(8,128)S(1)} %pad_maximum_fusion.10), channel_id=1, source_target_pairs={{0,2},{1,3},{2,0},{3,1},{4,6},{5,7},{6,4},{7,5},{8,10},{9,11},{10,... | collective-permute-start | bytes 49160 | tf_op jit(solution)/shard_map/ppermute | solution.py:261
  48.2 3.8 %collective-permute-start.12 = (f32[2,8,256]{2,1,0:T(8,128)S(1)}, f32[2,8,256]{2,1,0:T(8,128)S(1)}, u32[]{:S(2)}, u32[]{:S(2)}) collective-permute-start(f32[2,8,256]{2,1,0:T(8,128)S(1)} %pad_maximum_fusion.11), channel_id=1, source_target_pairs={{0,1},{1,0},{2,3},{3,2},{4,5},{5,4},{6,7},{7,6},{8,9},{9,8},{10,11... | collective-permute-start | bytes 49160 | tf_op jit(solution)/shard_map/ppermute | solution.py:261

commit v6 on v5

--- a/solution.py
+++ b/solution.py
@@ -56,56 +56,84 @@
     return jax.ShapeDtypeStruct(shape, dtype)
 
 
-def in_smem():
-    return pl.BlockSpec(memory_space=pltpu.SMEM)
-
-
 def head_of(h):
     return pl.ds(h * HEAD_DIM, HEAD_DIM)
 
 
-def pack(block_order, keys, values, grads, outs, sections):
+def pack(block_order, keys, values, queries, grads, outs, sections):
     rows, features = grads.shape
     here = features // sections
     heads = here // HEAD_DIM
     key_count = keys.shape[0]
-
-    def body(order_ref, k_hbm, v_hbm, g_ref, o_ref, out_ref, start_ref, k_ref, v_ref, sems):
-        copies = [
-            pltpu.make_async_copy(k_hbm, k_ref, sems.at[0]),
-            pltpu.make_async_copy(v_hbm, v_ref, sems.at[1]),
+    half = sections // 2
+
+    def body(order_hbm, k_hbm, v_hbm, q_hbm, g_hbm, o_hbm, *refs):
+        q_mine, q_other, g_mine, g_other, start_ref, k_ref, v_ref = refs[:7]
+        q_ref, g_ref, o_ref, order_ref, sems = refs[7:]
+        pairs = [
+            (q_hbm, q_ref),
+            (g_hbm, g_ref),
+            (o_hbm, o_ref),
+            (order_hbm, order_ref),
+            (k_hbm, k_ref),
+            (v_hbm, v_ref),
         ]
+        copies = [pltpu.make_async_copy(*pair, sems.at[i]) for i, pair in enumerate(pairs)]
         for copy in copies:
             copy.start()
+        odd = lax.axis_index("section") % 2
+        lane = lax.broadcasted_iota(jnp.int32, (rows, LANES), 1)
+
+        def at(s, h, count=1):
+            return pl.ds(pl.multiple_of(s * here + h * HEAD_DIM, HEAD_DIM), count * HEAD_DIM)
+
+        copies[0].wait()
+        for q_out, bit in ((q_mine, odd), (q_other, 1 - odd)):
+            for j in range(half):
+                q_out[j] = q_ref[:, at(2 * j + bit, 0, heads)]
+        copies[1].wait()
+        copies[2].wait()
+        for g_out, bit in ((g_mine, odd), (g_other, 1 - odd)):
+            for j in range(half):
+                extra = jnp.zeros((rows, LANES), F32)
+                for h in range(heads):
+                    g = g_ref[:, at(2 * j + bit, h)]
+                    terms = g.astype(F32) * o_ref[:, at(2 * j + bit, h)].astype(F32)
+                    delta = jnp.sum(terms, axis=1, keepdims=True)
+                    for part, value in enumerate(split3(delta)):
+                        extra = jnp.where(lane == part * heads + h, value.astype(F32), extra)
+                    g_out[j, :, head_of(h)] = g
+                g_out[j, :, pl.ds(here, LANES)] = extra.astype(BF)
+        copies[3].wait()
         block = order_ref[lax.axis_index("ctx")]
         start_ref[...] = jnp.full(start_ref.shape, block * key_count, jnp.int32)
-        lane = lax.broadcasted_iota(jnp.int32, (rows, LANES), 1)
-        for s in range(sections):
-            extra = jnp.zeros((rows, LANES), F32)
-            for h in range(heads):
-                at = head_of(s * heads + h)
-                terms = g_ref[:, at].astype(F32) * o_ref[:, at].astype(F32)
-                delta = jnp.sum(terms, axis=1, keepdims=True)
-                for part, value in enumerate(split3(delta)):
-                    extra = jnp.where(lane == part * heads + h, value.astype(F32), extra)
-            out_ref[s, :, pl.ds(0, here)] = g_ref[:, pl.ds(s * here, here)]
-            out_ref[s, :, pl.ds(here, LANES)] = extra.astype(BF)
-        for copy in copies:
-            copy.wait()
-
-    return pl.pallas_call(
-        body,
-        in_specs=[in_smem(), *[pl.BlockSpec(memory_space=pl.ANY)] * 2, *in_vmem(2)],
-        out_specs=in_vmem(4),
+        copies[4].wait()
+        copies[5].wait()
+
+    query_half = held((half, rows, here), BF)
+    grad_half = held((half, rows, here + LANES), BF)
+    return pl.pallas_call(
+        body,
+        in_specs=[pl.BlockSpec(memory_space=pl.ANY)] * 6,
+        out_specs=in_vmem(7),
         out_shape=[
-            held((sections, rows, here + LANES), BF),
+            query_half,
+            query_half,
+            grad_half,
+            grad_half,
             held((8, LANES), jnp.int32),
             held(keys.shape, BF),
             held(values.shape, BF),
         ],
-        scratch_shapes=[pltpu.SemaphoreType.DMA((2,))],
+        scratch_shapes=[
+            pltpu.VMEM((rows, features), BF),
+            pltpu.VMEM((rows, features), BF),
+            pltpu.VMEM((rows, features), BF),
+            pltpu.SMEM(block_order.shape, jnp.int32),
+            pltpu.SemaphoreType.DMA((6,)),
+        ],
         name="pack",
-    )(block_order, keys, values, grads, outs)
+    )(block_order, keys, values, queries, grads, outs)
 
 
 def visible_of(start_ref, shape, row_count, key_total):
@@ -247,9 +275,9 @@
     )(vmem(parts))
 
 
-def merge_stats(stats, axis, count):
-    for i in range(count.bit_length() - 1):
-        other = flip(stats, axis, count >> (i + 1))
+def merge_stats(stats, axis, order):
+    for bit in order:
+        other = flip(stats, axis, 1 << bit)
         top = jnp.maximum(stats[0], other[0])
         total = stats[1] * jnp.exp(stats[0] - top) + other[1] * jnp.exp(other[0] - top)
         stats = jnp.stack([top, total])
@@ -267,17 +295,19 @@
     return jnp.stack([first, second], axis)
 
 
-def swap_blocks(blocks, axis):
+def swap_blocks(mine, other, axis):
     count = lax.axis_size(axis)
     bits = count.bit_length() - 1
-    rest = blocks.shape[1:]
-    blocks = blocks.reshape((2,) * bits + rest)
+    rest = mine.shape[1:]
+    mine = mine.reshape((2,) * (bits - 1) + rest)
+    other = other.reshape(mine.shape)
     for i in range(bits):
         upper = (lax.axis_index(axis) >> i) % 2 == 1
-        first = lax.index_in_dim(blocks, 0, bits - 1, keepdims=False)
-        second = lax.index_in_dim(blocks, 1, bits - 1, keepdims=False)
-        mine = jnp.where(upper, second, first)
-        other = jnp.where(upper, first, second)
+        if i:
+            first = lax.index_in_dim(blocks, 0, bits - 1, keepdims=False)
+            second = lax.index_in_dim(blocks, 1, bits - 1, keepdims=False)
+            mine = jnp.where(upper, second, first)
+            other = jnp.where(upper, first, second)
         other = flip(other, axis, 1 << i)
         blocks = ordered(mine, other, upper, 0)
     return blocks.reshape((count,) + rest)
@@ -303,7 +333,7 @@
     sections = lax.axis_size("section")
     ctx_count = lax.axis_size("ctx")
     assert ctx_count & (ctx_count - 1) == 0
-    assert sections & (sections - 1) == 0
+    assert sections & (sections - 1) == 0 and sections > 1
     layers, rows, _ = queries.shape
     assert layers == 1
     key_count, here = cache_keys.shape
@@ -314,19 +344,25 @@
     ctx_bits = ctx_count.bit_length() - 1
     down = list(range(ctx_bits))[::-1]
 
-    sent = queries.reshape(rows, sections, here).transpose(1, 0, 2)
-    sent = swap_blocks(sent, "section")
-    query_all = spread_blocks(sent, "ctx", down)
+    packed = pack(
+        block_order,
+        cache_keys,
+        cache_values,
+        queries[0],
+        output_grad[0],
+        attention_out[0],
+        sections,
+    )
+    start, keys, values = packed[4:]
+    query_all = swap_blocks(packed[0], packed[1], "section")
+    query_all = spread_blocks(query_all, "ctx", down)
     query_all = query_all.reshape(peers * rows, here)
-    sent, start, keys, values = pack(
-        block_order, cache_keys, cache_values, output_grad[0], attention_out[0], sections
-    )
-    sent = swap_blocks(sent, "section")
-    grad_all = spread_blocks(sent, "ctx", down[:1] + down[1:][::-1])
+    grad_all = swap_blocks(packed[2], packed[3], "section")
+    grad_all = spread_blocks(grad_all, "ctx", down[:1] + down[1:][::-1])
     grad_all = grad_all.reshape(peers * rows, here + LANES)
 
     own = stats_kernel(start, query_all, keys, row_count, key_total)
-    merged = merge_stats(own, "ctx", ctx_count)
+    merged = merge_stats(own, "ctx", down[-1:] + down[:-1])
     part, probs, score_grads = query_kernel(
         start, query_all, grad_all, keys, values, own, row_count, key_total
     )

time: 56 us -> 59 us (1.054)
  waiting for transfers between devices: 18.5 us -> 25.5 us
  starting transfers between devices: 27.3 us -> 25.6 us
  other arithmetic: 1.2 us -> 0.43 us
  Pallas kernels: 6.99 us -> 6.3 us
  local copies, waits for them, and re-layouts: 0.65 us -> 0 us
    ppermute x13, waiting for transfers between devices: 17.4 us -> 25.5 us  [flip(): return lax.ppermute(value, axis, [(i, i ^ bit) for i in range(count)])]
    ppermute x13, starting transfers between devices: 22.9 us -> 19.9 us  [flip(): return lax.ppermute(value, axis, [(i, i ^ bit) for i in range(count)])]
    all_to_all x1, starting transfers between devices: 4.46 us -> 5.74 us  [exchange(): return lax.all_to_all(blocks, ('section', 'ctx'), 0, 0, tiled=True)]
    all_to_all x1, waiting for transfers between devices: 1.09 us -> 0.01 us  [exchange(): return lax.all_to_all(blocks, ('section', 'ctx'), 0, 0, tiled=True)]
    select_n x4 -> x2, other arithmetic: 0.78 us -> 0.02 us  [swap_blocks(): other = jnp.where(upper, first, second)]
    pallas_call x1, Pallas kernels: 1.82 us -> 1.12 us  [pack(): pl.pallas_call(body, in_specs=[pl.BlockSpec(memory_space=pl.ANY)] * 6, ou...]
    unnamed x2 -> x0, local copies, waits for them, and re-layouts: 0.65 us -> none
  transfers between devices with their start and end apart: 14 -> 14, of which waited for: 9 -> 10; matrix products, arithmetic and copies ran while one was open for 1% -> 0% of each run, Pallas kernels for 5% -> 2%
where the time goes in v6:
time: 59 us; the launch traced here: 58.7 us
  starting transfers between devices  25.6 us (43%)
  waiting for transfers between devices  25.5 us (43%)
  Pallas kernels  6.3 us (11%)
  between operations  0.8 us (1%)
    ppermute x13, waiting for transfers between devices, flip(): return lax.ppermute(value, axis, [(i, i ^ bit) for i in range(count)])  25.5 us
    ppermute x13, starting transfers between devices, flip(): return lax.ppermute(value, axis, [(i, i ^ bit) for i in range(count)])  19.9 us
    all_to_all x1, starting transfers between devices, exchange(): return lax.all_to_all(blocks, ('section', 'ctx'), 0, 0, tiled=True)  5.74 us
    pallas_call x1, Pallas kernels, query_kernel(): pl.pallas_call(body, in_specs=in_vmem(6), out_specs=in_vmem(3), out_shape...  2.33 us
    pallas_call x1, Pallas kernels, combine_kernel(): pl.pallas_call(body, in_specs=in_vmem(1), out_specs=in_vmem(1)[0], out_sh...  1.37 us
  transfers between devices with their start and end apart: 14, of which 10 were waited for; matrix products, arithmetic and copies ran while one was open for 0% of the time, Pallas kernels for 2%

profile of v6, /device:TPU:0, one launch (start us, length us, event | category | flops | bytes accessed | tf_op | source)
XLA Modules:
  0.0 58.7 jit_solution(4972225930505838209)
XLA Ops:
  0.6 1.1 %pack.1 = (bf16[2,8,640]{2,1,0:T(8,128)(2,1)S(1)}, bf16[2,8,640]{2,1,0:T(8,128)(2,1)S(1)}, bf16[2,8,768]{2,1,0:T(8,128)(2,1)S(1)}, bf16[2,8,768]{2,1,0:T(8,128)(...) custom-call(s32[8]{0:T(128)} %order_hbm.1, bf16[128,640]{1,0:T(8,128)(2,1)} %k_hbm.1, ...), custom_call_target="tpu_custom_call" | custom-call | tf_op jit(solution)/shard_map/pack/pallas_call | solution.py:115
  1.8 0.6 collective-permute-start
  2.4 0.8 %collective-permute-done = bf16[2,8,640]{2,1,0:T(8,128)(2,1)S(1)} collective-permute-done((bf16[2,8,640]{2,1,0:T(8,128)(2,1)S(1)}, bf16[2,8,640]{2,1,0:T(8,128)(2,1)S(1)}, u32[]{:S(2)}, u32[]{:S(2)}) %collective-permute-start) | collective-permute-done | bytes 20512 | tf_op jit(solution)/shard_map/ppermute | solution.py:289
  3.2 2.9 %collective-permute-start.1 = (bf16[2,8,640]{2,1,0:T(8,128)(2,1)S(1)}, bf16[2,8,640]{2,1,0:T(8,128)(2,1)S(1)}, u32[]{:S(2)}, u32[]{:S(2)}) collective-permute-start(bf16[2,8,640]{2,1,0:T(8,128)(2,1)S(1)} %fusion.5), channel_id=1, source_target_pairs={{0,16},{8,24},{16,0},{24,8},{1,17},{9,25},{17,1},{25,9},{2,18},{10... | collective-permute-start | bytes 61448 | tf_op jit(solution)/shard_map/ppermute | solution.py:289
  6.2 1.6 %collective-permute-done.1 = bf16[2,8,640]{2,1,0:T(8,128)(2,1)S(1)} collective-permute-done((bf16[2,8,640]{2,1,0:T(8,128)(2,1)S(1)}, bf16[2,8,640]{2,1,0:T(8,128)(2,1)S(1)}, u32[]{:S(2)}, u32[]{:S(2)}) %collective-permute-start.1) | collective-permute-done | bytes 20512 | tf_op jit(solution)/shard_map/ppermute | solution.py:289
  7.9 3.2 %collective-permute-start.2 = (bf16[4,8,640]{2,1,0:T(8,128)(2,1)S(1)}, bf16[4,8,640]{2,1,0:T(8,128)(2,1)S(1)}, u32[]{:S(2)}, u32[]{:S(2)}) collective-permute-start(bf16[4,8,640]{2,1,0:T(8,128)(2,1)S(1)} %bitcast.122), channel_id=1, source_target_pairs={{0,4},{1,5},{2,6},{3,7},{4,0},{5,1},{6,2},{7,3},{8,12},{9,13},{10,... | collective-permute-start | bytes 122888 | tf_op jit(solution)/shard_map/ppermute | solution.py:289
  11.1 1.6 %collective-permute-start.7 = (bf16[4,8,768]{2,1,0:T(8,128)(2,1)S(1)}, bf16[4,8,768]{2,1,0:T(8,128)(2,1)S(1)}, u32[]{:S(2)}, u32[]{:S(2)}) collective-permute-start(bf16[4,8,768]{2,1,0:T(8,128)(2,1)S(1)} %bitcast.121), channel_id=1, source_target_pairs={{0,4},{1,5},{2,6},{3,7},{4,0},{5,1},{6,2},{7,3},{8,12},{9,13},{10,... | collective-permute-start | bytes 147464 | tf_op jit(solution)/shard_map/ppermute | solution.py:289
  13.1 2.0 %collective-permute-start.3 = (bf16[4,2,8,640]{3,2,1,0:T(8,128)(2,1)S(1)}, bf16[4,2,8,640]{3,2,1,0:T(8,128)(2,1)S(1)}, u32[]{:S(2)}, u32[]{:S(2)}) collective-permute-start(bf16[4,2,8,640]{3,2,1,0:T(8,128)(2,1)S(1)} %pad_maximum_fusion.5), channel_id=1, source_target_pairs={{0,2},{1,3},{2,0},{3,1},{4,6},{5,7},{6,4},{7,5},{8,10},{9,11},{10,... | collective-permute-start | bytes 245768 | tf_op jit(solution)/shard_map/ppermute | solution.py:289
  15.1 1.1 %collective-permute-done.7 = bf16[4,8,768]{2,1,0:T(8,128)(2,1)S(1)} collective-permute-done((bf16[4,8,768]{2,1,0:T(8,128)(2,1)S(1)}, bf16[4,8,768]{2,1,0:T(8,128)(2,1)S(1)}, u32[]{:S(2)}, u32[]{:S(2)}) %collective-permute-start.7) | collective-permute-done | bytes 49184 | tf_op jit(solution)/shard_map/ppermute | solution.py:289
  16.2 1.6 %collective-permute-start.8 = (bf16[4,2,8,768]{3,2,1,0:T(8,128)(2,1)S(1)}, bf16[4,2,8,768]{3,2,1,0:T(8,128)(2,1)S(1)}, u32[]{:S(2)}, u32[]{:S(2)}) collective-permute-start(bf16[4,2,8,768]{3,2,1,0:T(8,128)(2,1)S(1)} %pad_maximum_fusion.4), channel_id=1, source_target_pairs={{0,1},{1,0},{2,3},{3,2},{4,5},{5,4},{6,7},{7,6},{8,9},{9,8},{10,11... | collective-permute-start | bytes 294920 | tf_op jit(solution)/shard_map/ppermute | solution.py:289
  17.8 1.7 %collective-permute-start.4 = (bf16[4,2,2,8,640]{4,3,2,1,0:T(8,128)(2,1)S(1)}, bf16[4,2,2,8,640]{4,3,2,1,0:T(8,128)(2,1)S(1)}, u32[]{:S(2)}, u32[]{:S(2)}) collective-permute-start(bf16[4,2,2,8,640]{4,3,2,1,0:T(8,128)(2,1)S(1)} %pad_maximum_fusion.3), channel_id=1, source_target_pairs={{0,1},{1,0},{2,3},{3,2},{4,5},{5,4},{6,7},{7,6},{8,9},{9,8},{10,11... | collective-permute-start | bytes 491528 | tf_op jit(solution)/shard_map/ppermute | solution.py:289
  19.6 1.3 %collective-permute-done.8 = bf16[4,2,8,768]{3,2,1,0:T(8,128)(2,1)S(1)} collective-permute-done((bf16[4,2,8,768]{3,2,1,0:T(8,128)(2,1)S(1)}, bf16[4,2,8,768]{3,2,1,0:T(8,128)(2,1)S(1)}, u32[]{:S(2)}, u32[]{:S(2)}) %collective-permute-start.8) | collective-permute-done | bytes 98336 | tf_op jit(solution)/shard_map/ppermute | solution.py:289
  20.9 2.5 %collective-permute-done.4 = bf16[4,2,2,8,640]{4,3,2,1,0:T(8,128)(2,1)S(1)} collective-permute-done((bf16[4,2,2,8,640]{4,3,2,1,0:T(8,128)(2,1)S(1)}, bf16[4,2,2,8,640]{4,3,2,1,0:T(8,128)(2,1)S(1)}, u32[]{:S(2)}, u32[]{:S(2)}) %collective-permute-start.4) | collective-permute-done | bytes 163872 | tf_op jit(solution)/shard_map/ppermute | solution.py:289
  23.5 0.4 stats.1.l_ref.own_ref
  23.9 1.7 %collective-permute-start.10 = (f32[2,8,256]{2,1,0:T(8,128)S(1)}, f32[2,8,256]{2,1,0:T(8,128)S(1)}, u32[]{:S(2)}, u32[]{:S(2)}) collective-permute-start(f32[2,8,256]{2,1,0:T(8,128)S(1)} %stats.1.l_ref.own_ref), channel_id=1, source_target_pairs={{0,1},{1,0},{2,3},{3,2},{4,5},{5,4},{6,7},{7,6},{8,9},{9,8},{10,11... | collective-permute-start | bytes 49160 | tf_op jit(solution)/shard_map/ppermute | solution.py:289
  25.7 1.6 %collective-permute-start.9 = (bf16[4,2,2,8,768]{4,3,2,1,0:T(8,128)(2,1)S(1)}, bf16[4,2,2,8,768]{4,3,2,1,0:T(8,128)(2,1)S(1)}, u32[]{:S(2)}, u32[]{:S(2)}) collective-permute-start(bf16[4,2,2,8,768]{4,3,2,1,0:T(8,128)(2,1)S(1)} %pad_maximum_fusion.2), channel_id=1, source_target_pairs={{0,2},{1,3},{2,0},{3,1},{4,6},{5,7},{6,4},{7,5},{8,10},{9,11},{10,... | collective-permute-start | bytes 589832 | tf_op jit(solution)/shard_map/ppermute | solution.py:289
  27.7 3.7 %collective-permute-done.9 = bf16[4,2,2,8,768]{4,3,2,1,0:T(8,128)(2,1)S(1)} collective-permute-done((bf16[4,2,2,8,768]{4,3,2,1,0:T(8,128)(2,1)S(1)}, bf16[4,2,2,8,768]{4,3,2,1,0:T(8,128)(2,1)S(1)}, u32[]{:S(2)}, u32[]{:S(2)}) %collective-permute-start.9) | collective-permute-done | bytes 196640 | tf_op jit(solution)/shard_map/ppermute | solution.py:289
  31.5 2.3 %query_gradients.1 = (bf16[256,768]{1,0:T(8,128)(2,1)}, bf16[5,128,256]{2,1,0:T(8,128)(2,1)S(1)}, bf16[5,128,256]{2,1,0:T(8,128)(2,1)S(1)}) custom-call(s32[8,128]{1,0:T(8,128)S(1)} %get-tuple-element.15.start_ref, bf16[256,640]{1,0:T(8,128)(2,1)S(1)} %bitcast.115, bf16[256,768]{1,0:T(8,128)(2,1)S(1)} %bitcast.117, ...), custom_call_target="tpu_custom_call" | custom-call | tf_op jit(solution)/shard_map/query_gradients/pallas_call | solution.py:205
  33.8 5.7 %all-to-all-start = ((bf16[32,8,768]{2,1,0:T(8,128)(2,1)}), bf16[32,8,768]{2,1,0:T(8,128)(2,1)S(1)}, u32[]{:S(2)}, u32[]{:S(2)}) async-start(bf16[32,8,768]{2,1,0:T(8,128)(2,1)} %bitcast.120), calls=%async_computation | async-start | bytes 786432 | tf_op jit(solution)/shard_map/all_to_all | solution.py:329
  39.6 2.7 %collective-permute-start.11 = (f32[2,8,256]{2,1,0:T(8,128)S(1)}, f32[2,8,256]{2,1,0:T(8,128)S(1)}, u32[]{:S(2)}, u32[]{:S(2)}) collective-permute-start(f32[2,8,256]{2,1,0:T(8,128)S(1)} %pad_maximum_fusion.10), channel_id=1, source_target_pairs={{0,4},{1,5},{2,6},{3,7},{4,0},{5,1},{6,2},{7,3},{8,12},{9,13},{10,... | collective-permute-start | bytes 49160 | tf_op jit(solution)/shard_map/ppermute | solution.py:289
  42.3 10.1 %collective-permute-done.11 = f32[2,8,256]{2,1,0:T(8,128)S(1)} collective-permute-done((f32[2,8,256]{2,1,0:T(8,128)S(1)}, f32[2,8,256]{2,1,0:T(8,128)S(1)}, u32[]{:S(2)}, u32[]{:S(2)}) %collective-permute-start.11) | collective-permute-done | bytes 16416 | tf_op jit(solution)/shard_map/ppermute | solution.py:289
  52.5 3.7 %collective-permute-done.12 = f32[2,8,256]{2,1,0:T(8,128)S(1)} collective-permute-done((f32[2,8,256]{2,1,0:T(8,128)S(1)}, f32[2,8,256]{2,1,0:T(8,128)S(1)}, u32[]{:S(2)}, u32[]{:S(2)}) %collective-permute-start.12) | collective-permute-done | bytes 16416 | tf_op jit(solution)/shard_map/ppermute | solution.py:289
  56.3 1.1 %cache_gradients.1 = (bf16[128,640]{1,0:T(8,128)(2,1)}, bf16[128,640]{1,0:T(8,128)(2,1)}) custom-call(bf16[256,640]{1,0:T(8,128)(2,1)S(1)} %bitcast.116, bf16[256,768]{1,0:T(8,128)(2,1)S(1)} %bitcast.118, bf16[5,128,256]{2,1,0:T(8,128)(2,1)S(1)} %get-tuple-element.23.p_ref, bf16[5,128,256]{2,1,0:T(8,128)(2,1)S(1)} %get-tuple-element.24.ds_ref, ...), custom_call_target="tpu_custom_call" | custom-call | tf_op jit(solution)/shard_map/cache_gradients/pallas_call | solution.py:232
  57.3 1.4 %combine.1 = bf16[8,2560]{1,0:T(8,128)(2,1)} custom-call(bf16[4,8,8,768]{3,2,1,0:T(8,128)(2,1)S(1)} %bitcast.119), custom_call_target="tpu_custom_call" | custom-call | tf_op jit(solution)/shard_map/combine/pallas_call | solution.py:269
  (35 shorter events, 1.5 us)
Async XLA Ops:
  1.8 1.4 %collective-permute-start = (bf16[2,8,640]{2,1,0:T(8,128)(2,1)S(1)}, bf16[2,8,640]{2,1,0:T(8,128)(2,1)S(1)}, u32[]{:S(2)}, u32[]{:S(2)}) collective-permute-start(bf16[2,8,640]{2,1,0:T(8,128)(2,1)S(1)} %get-tuple-element.16), channel_id=1, source_target_pairs={{0,8},{8,0},{16,24},{24,16},{1,9},{9,1},{17,25},{25,17},{2,10},{10... | collective-permute-start | bytes 61448 | tf_op jit(solution)/shard_map/ppermute | solution.py:289
  2.3 3.8 %collective-permute-start.5 = (bf16[2,8,768]{2,1,0:T(8,128)(2,1)S(1)}, bf16[2,8,768]{2,1,0:T(8,128)(2,1)S(1)}, u32[]{:S(2)}, u32[]{:S(2)}) collective-permute-start(bf16[2,8,768]{2,1,0:T(8,128)(2,1)S(1)} %get-tuple-element.18), channel_id=1, source_target_pairs={{0,8},{8,0},{16,24},{24,16},{1,9},{9,1},{17,25},{25,17},{2,10},{10... | collective-permute-start | bytes 73736 | tf_op jit(solution)/shard_map/ppermute | solution.py:289
  3.2 4.6 %collective-permute-start.1 = (bf16[2,8,640]{2,1,0:T(8,128)(2,1)S(1)}, bf16[2,8,640]{2,1,0:T(8,128)(2,1)S(1)}, u32[]{:S(2)}, u32[]{:S(2)}) collective-permute-start(bf16[2,8,640]{2,1,0:T(8,128)(2,1)S(1)} %fusion.5), channel_id=1, source_target_pairs={{0,16},{8,24},{16,0},{24,8},{1,17},{9,25},{17,1},{25,9},{2,18},{10... | collective-permute-start | bytes 61448 | tf_op jit(solution)/shard_map/ppermute | solution.py:289
  6.1 5.0 %collective-permute-start.6 = (bf16[2,8,768]{2,1,0:T(8,128)(2,1)S(1)}, bf16[2,8,768]{2,1,0:T(8,128)(2,1)S(1)}, u32[]{:S(2)}, u32[]{:S(2)}) collective-permute-start(bf16[2,8,768]{2,1,0:T(8,128)(2,1)S(1)} %fusion.2), channel_id=1, source_target_pairs={{0,16},{8,24},{16,0},{24,8},{1,17},{9,25},{17,1},{25,9},{2,18},{10... | collective-permute-start | bytes 73736 | tf_op jit(solution)/shard_map/ppermute | solution.py:289
  7.9 5.2 %collective-permute-start.2 = (bf16[4,8,640]{2,1,0:T(8,128)(2,1)S(1)}, bf16[4,8,640]{2,1,0:T(8,128)(2,1)S(1)}, u32[]{:S(2)}, u32[]{:S(2)}) collective-permute-start(bf16[4,8,640]{2,1,0:T(8,128)(2,1)S(1)} %bitcast.122), channel_id=1, source_target_pairs={{0,4},{1,5},{2,6},{3,7},{4,0},{5,1},{6,2},{7,3},{8,12},{9,13},{10,... | collective-permute-start | bytes 122888 | tf_op jit(solution)/shard_map/ppermute | solution.py:289
  11.1 5.1 %collective-permute-start.7 = (bf16[4,8,768]{2,1,0:T(8,128)(2,1)S(1)}, bf16[4,8,768]{2,1,0:T(8,128)(2,1)S(1)}, u32[]{:S(2)}, u32[]{:S(2)}) collective-permute-start(bf16[4,8,768]{2,1,0:T(8,128)(2,1)S(1)} %bitcast.121), channel_id=1, source_target_pairs={{0,4},{1,5},{2,6},{3,7},{4,0},{5,1},{6,2},{7,3},{8,12},{9,13},{10,... | collective-permute-start | bytes 147464 | tf_op jit(solution)/shard_map/ppermute | solution.py:289
  13.1 4.7 %collective-permute-start.3 = (bf16[4,2,8,640]{3,2,1,0:T(8,128)(2,1)S(1)}, bf16[4,2,8,640]{3,2,1,0:T(8,128)(2,1)S(1)}, u32[]{:S(2)}, u32[]{:S(2)}) collective-permute-start(bf16[4,2,8,640]{3,2,1,0:T(8,128)(2,1)S(1)} %pad_maximum_fusion.5), channel_id=1, source_target_pairs={{0,2},{1,3},{2,0},{3,1},{4,6},{5,7},{6,4},{7,5},{8,10},{9,11},{10,... | collective-permute-start | bytes 245768 | tf_op jit(solution)/shard_map/ppermute | solution.py:289
  16.2 4.7 %collective-permute-start.8 = (bf16[4,2,8,768]{3,2,1,0:T(8,128)(2,1)S(1)}, bf16[4,2,8,768]{3,2,1,0:T(8,128)(2,1)S(1)}, u32[]{:S(2)}, u32[]{:S(2)}) collective-permute-start(bf16[4,2,8,768]{3,2,1,0:T(8,128)(2,1)S(1)} %pad_maximum_fusion.4), channel_id=1, source_target_pairs={{0,1},{1,0},{2,3},{3,2},{4,5},{5,4},{6,7},{7,6},{8,9},{9,8},{10,11... | collective-permute-start | bytes 294920 | tf_op jit(solution)/shard_map/ppermute | solution.py:289
  17.8 5.6 %collective-permute-start.4 = (bf16[4,2,2,8,640]{4,3,2,1,0:T(8,128)(2,1)S(1)}, bf16[4,2,2,8,640]{4,3,2,1,0:T(8,128)(2,1)S(1)}, u32[]{:S(2)}, u32[]{:S(2)}) collective-permute-start(bf16[4,2,2,8,640]{4,3,2,1,0:T(8,128)(2,1)S(1)} %pad_maximum_fusion.3), channel_id=1, source_target_pairs={{0,1},{1,0},{2,3},{3,2},{4,5},{5,4},{6,7},{7,6},{8,9},{9,8},{10,11... | collective-permute-start | bytes 491528 | tf_op jit(solution)/shard_map/ppermute | solution.py:289
  23.9 3.8 %collective-permute-start.10 = (f32[2,8,256]{2,1,0:T(8,128)S(1)}, f32[2,8,256]{2,1,0:T(8,128)S(1)}, u32[]{:S(2)}, u32[]{:S(2)}) collective-permute-start(f32[2,8,256]{2,1,0:T(8,128)S(1)} %stats.1.l_ref.own_ref), channel_id=1, source_target_pairs={{0,1},{1,0},{2,3},{3,2},{4,5},{5,4},{6,7},{7,6},{8,9},{9,8},{10,11... | collective-permute-start | bytes 49160 | tf_op jit(solution)/shard_map/ppermute | solution.py:289
  25.7 5.7 %collective-permute-start.9 = (bf16[4,2,2,8,768]{4,3,2,1,0:T(8,128)(2,1)S(1)}, bf16[4,2,2,8,768]{4,3,2,1,0:T(8,128)(2,1)S(1)}, u32[]{:S(2)}, u32[]{:S(2)}) collective-permute-start(bf16[4,2,2,8,768]{4,3,2,1,0:T(8,128)(2,1)S(1)} %pad_maximum_fusion.2), channel_id=1, source_target_pairs={{0,2},{1,3},{2,0},{3,1},{4,6},{5,7},{6,4},{7,5},{8,10},{9,11},{10,... | collective-permute-start | bytes 589832 | tf_op jit(solution)/shard_map/ppermute | solution.py:289
  33.8 23.5 %all-to-all-start = ((bf16[32,8,768]{2,1,0:T(8,128)(2,1)}), bf16[32,8,768]{2,1,0:T(8,128)(2,1)S(1)}, u32[]{:S(2)}, u32[]{:S(2)}) async-start(bf16[32,8,768]{2,1,0:T(8,128)(2,1)} %bitcast.120), calls=%async_computation | async-start | bytes 786432 | tf_op jit(solution)/shard_map/all_to_all | solution.py:329
  39.6 12.8 %collective-permute-start.11 = (f32[2,8,256]{2,1,0:T(8,128)S(1)}, f32[2,8,256]{2,1,0:T(8,128)S(1)}, u32[]{:S(2)}, u32[]{:S(2)}) collective-permute-start(f32[2,8,256]{2,1,0:T(8,128)S(1)} %pad_maximum_fusion.10), channel_id=1, source_target_pairs={{0,4},{1,5},{2,6},{3,7},{4,0},{5,1},{6,2},{7,3},{8,12},{9,13},{10,... | collective-permute-start | bytes 49160 | tf_op jit(solution)/shard_map/ppermute | solution.py:289
  52.4 3.8 %collective-permute-start.12 = (f32[2,8,256]{2,1,0:T(8,128)S(1)}, f32[2,8,256]{2,1,0:T(8,128)S(1)}, u32[]{:S(2)}, u32[]{:S(2)}) collective-permute-start(f32[2,8,256]{2,1,0:T(8,128)S(1)} %pad_maximum_fusion.11), channel_id=1, source_target_pairs={{0,2},{1,3},{2,0},{3,1},{4,6},{5,7},{6,4},{7,5},{8,10},{9,11},{10,... | collective-permute-start | bytes 49160 | tf_op jit(solution)/shard_map/ppermute | solution.py:289

commit v7 on v6

--- a/solution.py
+++ b/solution.py
@@ -84,16 +84,12 @@
         odd = lax.axis_index("section") % 2
         lane = lax.broadcasted_iota(jnp.int32, (rows, LANES), 1)
 
-        def at(s, h, count=1):
-            return pl.ds(pl.multiple_of(s * here + h * HEAD_DIM, HEAD_DIM), count * HEAD_DIM)
-
-        copies[0].wait()
-        for q_out, bit in ((q_mine, odd), (q_other, 1 - odd)):
-            for j in range(half):
-                q_out[j] = q_ref[:, at(2 * j + bit, 0, heads)]
-        copies[1].wait()
-        copies[2].wait()
-        for g_out, bit in ((g_mine, odd), (g_other, 1 - odd)):
+        def at(s, h):
+            return pl.ds(pl.multiple_of(s * here + h * HEAD_DIM, HEAD_DIM), HEAD_DIM)
+
+        for i in range(3):
+            copies[i].wait()
+        for q_out, g_out, bit in ((q_mine, g_mine, odd), (q_other, g_other, 1 - odd)):
             for j in range(half):
                 extra = jnp.zeros((rows, LANES), F32)
                 for h in range(heads):
@@ -103,15 +99,16 @@
                     for part, value in enumerate(split3(delta)):
                         extra = jnp.where(lane == part * heads + h, value.astype(F32), extra)
                     g_out[j, :, head_of(h)] = g
-                g_out[j, :, pl.ds(here, LANES)] = extra.astype(BF)
+                    q_out[j, :, head_of(h)] = q_ref[:, at(2 * j + bit, h)]
+                q_out[j, :, pl.ds(here, LANES)] = extra.astype(BF)
         copies[3].wait()
         block = order_ref[lax.axis_index("ctx")]
         start_ref[...] = jnp.full(start_ref.shape, block * key_count, jnp.int32)
         copies[4].wait()
         copies[5].wait()
 
-    query_half = held((half, rows, here), BF)
-    grad_half = held((half, rows, here + LANES), BF)
+    query_half = held((half, rows, here + LANES), BF)
+    grad_half = held((half, rows, here), BF)
     return pl.pallas_call(
         body,
         in_specs=[pl.BlockSpec(memory_space=pl.ANY)] * 6,
@@ -143,8 +140,8 @@
 
 
 def stats_kernel(start, queries, keys, row_count, key_total):
-    m, here = queries.shape
-    key_count = keys.shape[0]
+    m = queries.shape[0]
+    key_count, here = keys.shape
     heads = here // HEAD_DIM
     slots = -(-heads // 8) * 8
     scaling = HEAD_DIM ** (-0.5)
@@ -178,7 +175,7 @@
 
     def body(start_ref, q_ref, g_ref, k_ref, v_ref, l_ref, u_ref, p_ref, ds_ref):
         visible = visible_of(start_ref, (key_count, m), row_count, key_total)
-        extra = g_ref[:, pl.ds(here, LANES)]
+        extra = q_ref[:, pl.ds(here, LANES)]
         slot = lax.broadcasted_iota(jnp.int32, (slots, LANES), 0)
         lane = lax.broadcasted_iota(jnp.int32, (slots, LANES), 1)
         pick = (lane % heads == slot) & (lane < 3 * heads)
@@ -216,7 +213,7 @@
 
 
 def cache_kernel(queries, grads, probs, score_grads, own, merged):
-    here = queries.shape[1]
+    here = grads.shape[1]
     heads, key_count, _ = probs.shape
 
     def body(q_ref, g_ref, p_ref, ds_ref, own_ref, all_ref, dk_ref, dv_ref):
@@ -356,13 +353,13 @@
     start, keys, values = packed[4:]
     query_all = swap_blocks(packed[0], packed[1], "section")
     query_all = spread_blocks(query_all, "ctx", down)
-    query_all = query_all.reshape(peers * rows, here)
+    query_all = query_all.reshape(peers * rows, here + LANES)
     grad_all = swap_blocks(packed[2], packed[3], "section")
     grad_all = spread_blocks(grad_all, "ctx", down[:1] + down[1:][::-1])
-    grad_all = grad_all.reshape(peers * rows, here + LANES)
+    grad_all = grad_all.reshape(peers * rows, here)
 
     own = stats_kernel(start, query_all, keys, row_count, key_total)
-    merged = merge_stats(own, "ctx", down[-1:] + down[:-1])
+    merged = merge_stats(own, "ctx", down[::-1])
     part, probs, score_grads = query_kernel(
         start, query_all, grad_all, keys, values, own, row_count, key_total
     )

time: 59 us -> 52.7 us (0.89)
  waiting for transfers between devices: 25.5 us -> 16.7 us
  starting transfers between devices: 25.6 us -> 28.3 us
    ppermute x13, waiting for transfers between devices: 25.5 us -> 16.7 us  [flip(): return lax.ppermute(value, axis, [(i, i ^ bit) for i in range(count)])]
    ppermute x13, starting transfers between devices: 19.9 us -> 23.3 us  [flip(): return lax.ppermute(value, axis, [(i, i ^ bit) for i in range(count)])]
    all_to_all x1, starting transfers between devices: 5.74 us -> 4.99 us  [exchange(): return lax.all_to_all(blocks, ('section', 'ctx'), 0, 0, tiled=True)]
  transfers between devices with their start and end apart: 14 -> 14, of which waited for: 10 -> 9; matrix products, arithmetic and copies ran while one was open for 0% -> 1% of each run, Pallas kernels for 2% -> 6%
where the time goes in v7:
time: 52.7 us; the launch traced here: 52.5 us
  starting transfers between devices  28.3 us (54%)
  waiting for transfers between devices  16.7 us (32%)
  Pallas kernels  6.28 us (12%)
  between operations  0.8 us (2%)
    ppermute x13, starting transfers between devices, flip(): return lax.ppermute(value, axis, [(i, i ^ bit) for i in range(count)])  23.3 us
    ppermute x13, waiting for transfers between devices, flip(): return lax.ppermute(value, axis, [(i, i ^ bit) for i in range(count)])  16.7 us
    all_to_all x1, starting transfers between devices, exchange(): return lax.all_to_all(blocks, ('section', 'ctx'), 0, 0, tiled=True)  4.99 us
    pallas_call x1, Pallas kernels, query_kernel(): pl.pallas_call(body, in_specs=in_vmem(6), out_specs=in_vmem(3), out_shape...  2.33 us
    pallas_call x1, Pallas kernels, combine_kernel(): pl.pallas_call(body, in_specs=in_vmem(1), out_specs=in_vmem(1)[0], out_sh...  1.37 us
    pallas_call x1, Pallas kernels, pack(): pl.pallas_call(body, in_specs=[pl.BlockSpec(memory_space=pl.ANY)] * 6, ou...  1.12 us
  transfers between devices with their start and end apart: 14, of which 9 were waited for; matrix products, arithmetic and copies ran while one was open for 1% of the time, Pallas kernels for 6%

profile of v7, /device:TPU:0, one launch (start us, length us, event | category | flops | bytes accessed | tf_op | source)
XLA Modules:
  0.0 52.5 jit_solution(7862632345944097763)
XLA Ops:
  0.6 1.1 %pack.1 = (bf16[2,8,768]{2,1,0:T(8,128)(2,1)S(1)}, bf16[2,8,768]{2,1,0:T(8,128)(2,1)S(1)}, bf16[2,8,640]{2,1,0:T(8,128)(2,1)S(1)}, bf16[2,8,640]{2,1,0:T(8,128)(...) custom-call(s32[8]{0:T(128)} %order_hbm.1, bf16[128,640]{1,0:T(8,128)(2,1)} %k_hbm.1, ...), custom_call_target="tpu_custom_call" | custom-call | tf_op jit(solution)/shard_map/pack/pallas_call | solution.py:112
  1.8 0.6 %collective-permute-start.5 = (bf16[2,8,640]{2,1,0:T(8,128)(2,1)S(1)}, bf16[2,8,640]{2,1,0:T(8,128)(2,1)S(1)}, u32[]{:S(2)}, u32[]{:S(2)}) collective-permute-start(bf16[2,8,640]{2,1,0:T(8,128)(2,1)S(1)} %get-tuple-element.18), channel_id=1, source_target_pairs={{0,8},{8,0},{16,24},{24,16},{1,9},{9,1},{17,25},{25,17},{2,10},{10... | collective-permute-start | bytes 61448 | tf_op jit(solution)/shard_map/ppermute | solution.py:286
  2.4 0.8 %collective-permute-done.5 = bf16[2,8,640]{2,1,0:T(8,128)(2,1)S(1)} collective-permute-done((bf16[2,8,640]{2,1,0:T(8,128)(2,1)S(1)}, bf16[2,8,640]{2,1,0:T(8,128)(2,1)S(1)}, u32[]{:S(2)}, u32[]{:S(2)}) %collective-permute-start.5) | collective-permute-done | bytes 20512 | tf_op jit(solution)/shard_map/ppermute | solution.py:286
  3.2 2.9 %collective-permute-start.6 = (bf16[2,8,640]{2,1,0:T(8,128)(2,1)S(1)}, bf16[2,8,640]{2,1,0:T(8,128)(2,1)S(1)}, u32[]{:S(2)}, u32[]{:S(2)}) collective-permute-start(bf16[2,8,640]{2,1,0:T(8,128)(2,1)S(1)} %fusion.5), channel_id=1, source_target_pairs={{0,16},{8,24},{16,0},{24,8},{1,17},{9,25},{17,1},{25,9},{2,18},{10... | collective-permute-start | bytes 61448 | tf_op jit(solution)/shard_map/ppermute | solution.py:286
  6.2 1.6 %collective-permute-done.6 = bf16[2,8,640]{2,1,0:T(8,128)(2,1)S(1)} collective-permute-done((bf16[2,8,640]{2,1,0:T(8,128)(2,1)S(1)}, bf16[2,8,640]{2,1,0:T(8,128)(2,1)S(1)}, u32[]{:S(2)}, u32[]{:S(2)}) %collective-permute-start.6) | collective-permute-done | bytes 20512 | tf_op jit(solution)/shard_map/ppermute | solution.py:286
  7.9 3.2 %collective-permute-start.7 = (bf16[4,8,640]{2,1,0:T(8,128)(2,1)S(1)}, bf16[4,8,640]{2,1,0:T(8,128)(2,1)S(1)}, u32[]{:S(2)}, u32[]{:S(2)}) collective-permute-start(bf16[4,8,640]{2,1,0:T(8,128)(2,1)S(1)} %bitcast.122), channel_id=1, source_target_pairs={{0,4},{1,5},{2,6},{3,7},{4,0},{5,1},{6,2},{7,3},{8,12},{9,13},{10,... | collective-permute-start | bytes 122888 | tf_op jit(solution)/shard_map/ppermute | solution.py:286
  11.1 1.6 %collective-permute-start.2 = (bf16[4,8,768]{2,1,0:T(8,128)(2,1)S(1)}, bf16[4,8,768]{2,1,0:T(8,128)(2,1)S(1)}, u32[]{:S(2)}, u32[]{:S(2)}) collective-permute-start(bf16[4,8,768]{2,1,0:T(8,128)(2,1)S(1)} %bitcast.121), channel_id=1, source_target_pairs={{0,4},{1,5},{2,6},{3,7},{4,0},{5,1},{6,2},{7,3},{8,12},{9,13},{10,... | collective-permute-start | bytes 147464 | tf_op jit(solution)/shard_map/ppermute | solution.py:286
  13.1 1.9 %collective-permute-start.8 = (bf16[4,2,8,640]{3,2,1,0:T(8,128)(2,1)S(1)}, bf16[4,2,8,640]{3,2,1,0:T(8,128)(2,1)S(1)}, u32[]{:S(2)}, u32[]{:S(2)}) collective-permute-start(bf16[4,2,8,640]{3,2,1,0:T(8,128)(2,1)S(1)} %pad_maximum_fusion.5), channel_id=1, source_target_pairs={{0,1},{1,0},{2,3},{3,2},{4,5},{5,4},{6,7},{7,6},{8,9},{9,8},{10,11... | collective-permute-start | bytes 245768 | tf_op jit(solution)/shard_map/ppermute | solution.py:286
  15.0 1.1 %collective-permute-done.2 = bf16[4,8,768]{2,1,0:T(8,128)(2,1)S(1)} collective-permute-done((bf16[4,8,768]{2,1,0:T(8,128)(2,1)S(1)}, bf16[4,8,768]{2,1,0:T(8,128)(2,1)S(1)}, u32[]{:S(2)}, u32[]{:S(2)}) %collective-permute-start.2) | collective-permute-done | bytes 49184 | tf_op jit(solution)/shard_map/ppermute | solution.py:286
  16.2 1.6 %collective-permute-start.3 = (bf16[4,2,8,768]{3,2,1,0:T(8,128)(2,1)S(1)}, bf16[4,2,8,768]{3,2,1,0:T(8,128)(2,1)S(1)}, u32[]{:S(2)}, u32[]{:S(2)}) collective-permute-start(bf16[4,2,8,768]{3,2,1,0:T(8,128)(2,1)S(1)} %pad_maximum_fusion.4), channel_id=1, source_target_pairs={{0,2},{1,3},{2,0},{3,1},{4,6},{5,7},{6,4},{7,5},{8,10},{9,11},{10,... | collective-permute-start | bytes 294920 | tf_op jit(solution)/shard_map/ppermute | solution.py:286
  17.9 1.7 %collective-permute-start.9 = (bf16[4,2,2,8,640]{4,3,2,1,0:T(8,128)(2,1)S(1)}, bf16[4,2,2,8,640]{4,3,2,1,0:T(8,128)(2,1)S(1)}, u32[]{:S(2)}, u32[]{:S(2)}) collective-permute-start(bf16[4,2,2,8,640]{4,3,2,1,0:T(8,128)(2,1)S(1)} %pad_maximum_fusion.3), channel_id=1, source_target_pairs={{0,2},{1,3},{2,0},{3,1},{4,6},{5,7},{6,4},{7,5},{8,10},{9,11},{10,... | collective-permute-start | bytes 491528 | tf_op jit(solution)/shard_map/ppermute | solution.py:286
  19.6 1.2 %collective-permute-done.3 = bf16[4,2,8,768]{3,2,1,0:T(8,128)(2,1)S(1)} collective-permute-done((bf16[4,2,8,768]{3,2,1,0:T(8,128)(2,1)S(1)}, bf16[4,2,8,768]{3,2,1,0:T(8,128)(2,1)S(1)}, u32[]{:S(2)}, u32[]{:S(2)}) %collective-permute-start.3) | collective-permute-done | bytes 98336 | tf_op jit(solution)/shard_map/ppermute | solution.py:286
  20.9 1.6 %collective-permute-start.4 = (bf16[4,2,2,8,768]{4,3,2,1,0:T(8,128)(2,1)S(1)}, bf16[4,2,2,8,768]{4,3,2,1,0:T(8,128)(2,1)S(1)}, u32[]{:S(2)}, u32[]{:S(2)}) collective-permute-start(bf16[4,2,2,8,768]{4,3,2,1,0:T(8,128)(2,1)S(1)} %pad_maximum_fusion.2), channel_id=1, source_target_pairs={{0,1},{1,0},{2,3},{3,2},{4,5},{5,4},{6,7},{7,6},{8,9},{9,8},{10,11... | collective-permute-start | bytes 589832 | tf_op jit(solution)/shard_map/ppermute | solution.py:286
  22.5 0.8 %collective-permute-done.9 = bf16[4,2,2,8,640]{4,3,2,1,0:T(8,128)(2,1)S(1)} collective-permute-done((bf16[4,2,2,8,640]{4,3,2,1,0:T(8,128)(2,1)S(1)}, bf16[4,2,2,8,640]{4,3,2,1,0:T(8,128)(2,1)S(1)}, u32[]{:S(2)}, u32[]{:S(2)}) %collective-permute-start.9) | collective-permute-done | bytes 163872 | tf_op jit(solution)/shard_map/ppermute | solution.py:286
  23.3 3.5 %collective-permute-done.4 = bf16[4,2,2,8,768]{4,3,2,1,0:T(8,128)(2,1)S(1)} collective-permute-done((bf16[4,2,2,8,768]{4,3,2,1,0:T(8,128)(2,1)S(1)}, bf16[4,2,2,8,768]{4,3,2,1,0:T(8,128)(2,1)S(1)}, u32[]{:S(2)}, u32[]{:S(2)}) %collective-permute-start.4) | collective-permute-done | bytes 196640 | tf_op jit(solution)/shard_map/ppermute | solution.py:286
  27.3 1.6 %collective-permute-start.10 = (f32[2,8,256]{2,1,0:T(8,128)S(1)}, f32[2,8,256]{2,1,0:T(8,128)S(1)}, u32[]{:S(2)}, u32[]{:S(2)}) collective-permute-start(f32[2,8,256]{2,1,0:T(8,128)S(1)} %stats.1.l_ref.own_ref), channel_id=1, source_target_pairs={{0,1},{1,0},{2,3},{3,2},{4,5},{5,4},{6,7},{7,6},{8,9},{9,8},{10,11... | collective-permute-start | bytes 49160 | tf_op jit(solution)/shard_map/ppermute | solution.py:286
  29.0 2.3 %query_gradients.1 = (bf16[256,768]{1,0:T(8,128)(2,1)}, bf16[5,128,256]{2,1,0:T(8,128)(2,1)S(1)}, bf16[5,128,256]{2,1,0:T(8,128)(2,1)S(1)}) custom-call(s32[8,128]{1,0:T(8,128)S(1)} %get-tuple-element.15.start_ref, bf16[256,768]{1,0:T(8,128)(2,1)S(1)} %bitcast.115, bf16[256,640]{1,0:T(8,128)(2,1)S(1)} %bitcast.117, ...), custom_call_target="tpu_custom_call" | custom-call | tf_op jit(solution)/shard_map/query_gradients/pallas_call | solution.py:202
  31.3 5.0 %all-to-all-start = ((bf16[32,8,768]{2,1,0:T(8,128)(2,1)}), bf16[32,8,768]{2,1,0:T(8,128)(2,1)S(1)}, u32[]{:S(2)}, u32[]{:S(2)}) async-start(bf16[32,8,768]{2,1,0:T(8,128)(2,1)} %bitcast.120), calls=%async_computation | async-start | bytes 786432 | tf_op jit(solution)/shard_map/all_to_all | solution.py:326
  36.3 1.8 %collective-permute-start.11 = (f32[2,8,256]{2,1,0:T(8,128)S(1)}, f32[2,8,256]{2,1,0:T(8,128)S(1)}, u32[]{:S(2)}, u32[]{:S(2)}) collective-permute-start(f32[2,8,256]{2,1,0:T(8,128)S(1)} %pad_maximum_fusion.10), channel_id=1, source_target_pairs={{0,2},{1,3},{2,0},{3,1},{4,6},{5,7},{6,4},{7,5},{8,10},{9,11},{10,... | collective-permute-start | bytes 49160 | tf_op jit(solution)/shard_map/ppermute | solution.py:286
  38.2 5.5 %collective-permute-done.11 = f32[2,8,256]{2,1,0:T(8,128)S(1)} collective-permute-done((f32[2,8,256]{2,1,0:T(8,128)S(1)}, f32[2,8,256]{2,1,0:T(8,128)S(1)}, u32[]{:S(2)}, u32[]{:S(2)}) %collective-permute-start.11) | collective-permute-done | bytes 16416 | tf_op jit(solution)/shard_map/ppermute | solution.py:286
  43.7 4.6 %collective-permute-start.12 = (f32[2,8,256]{2,1,0:T(8,128)S(1)}, f32[2,8,256]{2,1,0:T(8,128)S(1)}, u32[]{:S(2)}, u32[]{:S(2)}) collective-permute-start(f32[2,8,256]{2,1,0:T(8,128)S(1)} %pad_maximum_fusion.11), channel_id=1, source_target_pairs={{0,4},{1,5},{2,6},{3,7},{4,0},{5,1},{6,2},{7,3},{8,12},{9,13},{10,... | collective-permute-start | bytes 49160 | tf_op jit(solution)/shard_map/ppermute | solution.py:286
  48.3 1.7 %collective-permute-done.12 = f32[2,8,256]{2,1,0:T(8,128)S(1)} collective-permute-done((f32[2,8,256]{2,1,0:T(8,128)S(1)}, f32[2,8,256]{2,1,0:T(8,128)S(1)}, u32[]{:S(2)}, u32[]{:S(2)}) %collective-permute-start.12) | collective-permute-done | bytes 16416 | tf_op jit(solution)/shard_map/ppermute | solution.py:286
  50.0 1.0 %cache_gradients.1 = (bf16[128,640]{1,0:T(8,128)(2,1)}, bf16[128,640]{1,0:T(8,128)(2,1)}) custom-call(bf16[256,768]{1,0:T(8,128)(2,1)S(1)} %bitcast.116, bf16[256,640]{1,0:T(8,128)(2,1)S(1)} %bitcast.118, bf16[5,128,256]{2,1,0:T(8,128)(2,1)S(1)} %get-tuple-element.23.p_ref, bf16[5,128,256]{2,1,0:T(8,128)(2,1)S(1)} %get-tuple-element.24.ds_ref, ...), custom_call_target="tpu_custom_call" | custom-call | tf_op jit(solution)/shard_map/cache_gradients/pallas_call | solution.py:229
  51.1 1.4 %combine.1 = bf16[8,2560]{1,0:T(8,128)(2,1)} custom-call(bf16[4,8,8,768]{3,2,1,0:T(8,128)(2,1)S(1)} %bitcast.119), custom_call_target="tpu_custom_call" | custom-call | tf_op jit(solution)/shard_map/combine/pallas_call | solution.py:266
  (35 shorter events, 1.4 us)
Async XLA Ops:
  1.8 1.4 %collective-permute-start.5 = (bf16[2,8,640]{2,1,0:T(8,128)(2,1)S(1)}, bf16[2,8,640]{2,1,0:T(8,128)(2,1)S(1)}, u32[]{:S(2)}, u32[]{:S(2)}) collective-permute-start(bf16[2,8,640]{2,1,0:T(8,128)(2,1)S(1)} %get-tuple-element.18), channel_id=1, source_target_pairs={{0,8},{8,0},{16,24},{24,16},{1,9},{9,1},{17,25},{25,17},{2,10},{10... | collective-permute-start | bytes 61448 | tf_op jit(solution)/shard_map/ppermute | solution.py:286
  2.3 3.8 %collective-permute-start = (bf16[2,8,768]{2,1,0:T(8,128)(2,1)S(1)}, bf16[2,8,768]{2,1,0:T(8,128)(2,1)S(1)}, u32[]{:S(2)}, u32[]{:S(2)}) collective-permute-start(bf16[2,8,768]{2,1,0:T(8,128)(2,1)S(1)} %get-tuple-element.16), channel_id=1, source_target_pairs={{0,8},{8,0},{16,24},{24,16},{1,9},{9,1},{17,25},{25,17},{2,10},{10... | collective-permute-start | bytes 73736 | tf_op jit(solution)/shard_map/ppermute | solution.py:286
  3.2 4.6 %collective-permute-start.6 = (bf16[2,8,640]{2,1,0:T(8,128)(2,1)S(1)}, bf16[2,8,640]{2,1,0:T(8,128)(2,1)S(1)}, u32[]{:S(2)}, u32[]{:S(2)}) collective-permute-start(bf16[2,8,640]{2,1,0:T(8,128)(2,1)S(1)} %fusion.5), channel_id=1, source_target_pairs={{0,16},{8,24},{16,0},{24,8},{1,17},{9,25},{17,1},{25,9},{2,18},{10... | collective-permute-start | bytes 61448 | tf_op jit(solution)/shard_map/ppermute | solution.py:286
  6.1 5.0 %collective-permute-start.1 = (bf16[2,8,768]{2,1,0:T(8,128)(2,1)S(1)}, bf16[2,8,768]{2,1,0:T(8,128)(2,1)S(1)}, u32[]{:S(2)}, u32[]{:S(2)}) collective-permute-start(bf16[2,8,768]{2,1,0:T(8,128)(2,1)S(1)} %fusion.2), channel_id=1, source_target_pairs={{0,16},{8,24},{16,0},{24,8},{1,17},{9,25},{17,1},{25,9},{2,18},{10... | collective-permute-start | bytes 73736 | tf_op jit(solution)/shard_map/ppermute | solution.py:286
  7.9 5.2 %collective-permute-start.7 = (bf16[4,8,640]{2,1,0:T(8,128)(2,1)S(1)}, bf16[4,8,640]{2,1,0:T(8,128)(2,1)S(1)}, u32[]{:S(2)}, u32[]{:S(2)}) collective-permute-start(bf16[4,8,640]{2,1,0:T(8,128)(2,1)S(1)} %bitcast.122), channel_id=1, source_target_pairs={{0,4},{1,5},{2,6},{3,7},{4,0},{5,1},{6,2},{7,3},{8,12},{9,13},{10,... | collective-permute-start | bytes 122888 | tf_op jit(solution)/shard_map/ppermute | solution.py:286
  11.1 5.1 %collective-permute-start.2 = (bf16[4,8,768]{2,1,0:T(8,128)(2,1)S(1)}, bf16[4,8,768]{2,1,0:T(8,128)(2,1)S(1)}, u32[]{:S(2)}, u32[]{:S(2)}) collective-permute-start(bf16[4,8,768]{2,1,0:T(8,128)(2,1)S(1)} %bitcast.121), channel_id=1, source_target_pairs={{0,4},{1,5},{2,6},{3,7},{4,0},{5,1},{6,2},{7,3},{8,12},{9,13},{10,... | collective-permute-start | bytes 147464 | tf_op jit(solution)/shard_map/ppermute | solution.py:286
  13.1 4.7 %collective-permute-start.8 = (bf16[4,2,8,640]{3,2,1,0:T(8,128)(2,1)S(1)}, bf16[4,2,8,640]{3,2,1,0:T(8,128)(2,1)S(1)}, u32[]{:S(2)}, u32[]{:S(2)}) collective-permute-start(bf16[4,2,8,640]{3,2,1,0:T(8,128)(2,1)S(1)} %pad_maximum_fusion.5), channel_id=1, source_target_pairs={{0,1},{1,0},{2,3},{3,2},{4,5},{5,4},{6,7},{7,6},{8,9},{9,8},{10,11... | collective-permute-start | bytes 245768 | tf_op jit(solution)/shard_map/ppermute | solution.py:286
  16.2 4.7 %collective-permute-start.3 = (bf16[4,2,8,768]{3,2,1,0:T(8,128)(2,1)S(1)}, bf16[4,2,8,768]{3,2,1,0:T(8,128)(2,1)S(1)}, u32[]{:S(2)}, u32[]{:S(2)}) collective-permute-start(bf16[4,2,8,768]{3,2,1,0:T(8,128)(2,1)S(1)} %pad_maximum_fusion.4), channel_id=1, source_target_pairs={{0,2},{1,3},{2,0},{3,1},{4,6},{5,7},{6,4},{7,5},{8,10},{9,11},{10,... | collective-permute-start | bytes 294920 | tf_op jit(solution)/shard_map/ppermute | solution.py:286
  17.9 5.4 %collective-permute-start.9 = (bf16[4,2,2,8,640]{4,3,2,1,0:T(8,128)(2,1)S(1)}, bf16[4,2,2,8,640]{4,3,2,1,0:T(8,128)(2,1)S(1)}, u32[]{:S(2)}, u32[]{:S(2)}) collective-permute-start(bf16[4,2,2,8,640]{4,3,2,1,0:T(8,128)(2,1)S(1)} %pad_maximum_fusion.3), channel_id=1, source_target_pairs={{0,2},{1,3},{2,0},{3,1},{4,6},{5,7},{6,4},{7,5},{8,10},{9,11},{10,... | collective-permute-start | bytes 491528 | tf_op jit(solution)/shard_map/ppermute | solution.py:286
  20.9 5.9 %collective-permute-start.4 = (bf16[4,2,2,8,768]{4,3,2,1,0:T(8,128)(2,1)S(1)}, bf16[4,2,2,8,768]{4,3,2,1,0:T(8,128)(2,1)S(1)}, u32[]{:S(2)}, u32[]{:S(2)}) collective-permute-start(bf16[4,2,2,8,768]{4,3,2,1,0:T(8,128)(2,1)S(1)} %pad_maximum_fusion.2), channel_id=1, source_target_pairs={{0,1},{1,0},{2,3},{3,2},{4,5},{5,4},{6,7},{7,6},{8,9},{9,8},{10,11... | collective-permute-start | bytes 589832 | tf_op jit(solution)/shard_map/ppermute | solution.py:286
  27.3 9.0 %collective-permute-start.10 = (f32[2,8,256]{2,1,0:T(8,128)S(1)}, f32[2,8,256]{2,1,0:T(8,128)S(1)}, u32[]{:S(2)}, u32[]{:S(2)}) collective-permute-start(f32[2,8,256]{2,1,0:T(8,128)S(1)} %stats.1.l_ref.own_ref), channel_id=1, source_target_pairs={{0,1},{1,0},{2,3},{3,2},{4,5},{5,4},{6,7},{7,6},{8,9},{9,8},{10,11... | collective-permute-start | bytes 49160 | tf_op jit(solution)/shard_map/ppermute | solution.py:286
  31.3 19.8 %all-to-all-start = ((bf16[32,8,768]{2,1,0:T(8,128)(2,1)}), bf16[32,8,768]{2,1,0:T(8,128)(2,1)S(1)}, u32[]{:S(2)}, u32[]{:S(2)}) async-start(bf16[32,8,768]{2,1,0:T(8,128)(2,1)} %bitcast.120), calls=%async_computation | async-start | bytes 786432 | tf_op jit(solution)/shard_map/all_to_all | solution.py:326
  36.3 7.4 %collective-permute-start.11 = (f32[2,8,256]{2,1,0:T(8,128)S(1)}, f32[2,8,256]{2,1,0:T(8,128)S(1)}, u32[]{:S(2)}, u32[]{:S(2)}) collective-permute-start(f32[2,8,256]{2,1,0:T(8,128)S(1)} %pad_maximum_fusion.10), channel_id=1, source_target_pairs={{0,2},{1,3},{2,0},{3,1},{4,6},{5,7},{6,4},{7,5},{8,10},{9,11},{10,... | collective-permute-start | bytes 49160 | tf_op jit(solution)/shard_map/ppermute | solution.py:286
  43.7 6.3 %collective-permute-start.12 = (f32[2,8,256]{2,1,0:T(8,128)S(1)}, f32[2,8,256]{2,1,0:T(8,128)S(1)}, u32[]{:S(2)}, u32[]{:S(2)}) collective-permute-start(f32[2,8,256]{2,1,0:T(8,128)S(1)} %pad_maximum_fusion.11), channel_id=1, source_target_pairs={{0,4},{1,5},{2,6},{3,7},{4,0},{5,1},{6,2},{7,3},{8,12},{9,13},{10,... | collective-permute-start | bytes 49160 | tf_op jit(solution)/shard_map/ppermute | solution.py:286

commit v8 on v7

--- a/solution.py
+++ b/solution.py
@@ -173,7 +173,13 @@
     slots = stats.shape[1]
     scaling = HEAD_DIM ** (-0.5)
 
-    def body(start_ref, q_ref, g_ref, k_ref, v_ref, l_ref, u_ref, p_ref, ds_ref):
+    def body(start_ref, q_ref, g_ref, k_ref, v_ref, l_ref, *refs):
+        u_hbm, p_ref, ds_ref, u_ref, sems = refs
+
+        def copy_of(h, width):
+            at = pl.ds(h * HEAD_DIM, width)
+            return pltpu.make_async_copy(u_ref.at[:, at], u_hbm.at[:, at], sems.at[h])
+
         visible = visible_of(start_ref, (key_count, m), row_count, key_total)
         extra = q_ref[:, pl.ds(here, LANES)]
         slot = lax.broadcasted_iota(jnp.int32, (slots, LANES), 0)
@@ -181,6 +187,14 @@
         pick = (lane % heads == slot) & (lane < 3 * heads)
         delta = nt(jnp.where(pick, 1.0, 0.0).astype(BF), extra)
         tops = l_ref[0]
+        sent = jnp.zeros((m, LANES), F32)
+        for i in range(2):
+            for part, value in enumerate(split3(l_ref[i])):
+                at = (3 * i + part) * heads
+                place = (lane == at + slot) & (slot < heads)
+                sent += tn(value, jnp.where(place, 1.0, 0.0).astype(BF))
+        u_ref[:, pl.ds(here, LANES)] = sent.astype(BF)
+        copy_of(heads, LANES).start()
         for h in range(heads):
             at = head_of(h)
             k = k_ref[:, at]
@@ -189,24 +203,25 @@
             ds = prob * (nt(v_ref[:, at], g_ref[:, at]) - delta[h : h + 1, :]) * scaling
             ds = ds.astype(BF)
             u_ref[:, at] = tn(ds, k).astype(BF)
+            copy_of(h, HEAD_DIM).start()
             p_ref[h] = prob.astype(BF)
             ds_ref[h] = ds
-        sent = jnp.zeros((m, LANES), F32)
-        for i in range(2):
-            for part, value in enumerate(split3(l_ref[i])):
-                at = (3 * i + part) * heads
-                place = (lane == at + slot) & (slot < heads)
-                sent += tn(value, jnp.where(place, 1.0, 0.0).astype(BF))
-        u_ref[:, pl.ds(here, LANES)] = sent.astype(BF)
+        for h in range(heads):
+            copy_of(h, HEAD_DIM).wait()
+        copy_of(heads, LANES).wait()
 
     return pl.pallas_call(
         body,
         in_specs=in_vmem(6),
-        out_specs=in_vmem(3),
+        out_specs=[pl.BlockSpec(memory_space=pl.ANY), *in_vmem(2)],
         out_shape=[
             jax.ShapeDtypeStruct((m, here + LANES), BF),
             held((heads, key_count, m), BF),
             held((heads, key_count, m), BF),
+        ],
+        scratch_shapes=[
+            pltpu.VMEM((m, here + LANES), BF),
+            pltpu.SemaphoreType.DMA((heads + 1,)),
         ],
         name="query_gradients",
     )(vmem(start), vmem(queries), vmem(grads), vmem(keys), vmem(values), vmem(stats))

time: 52.7 us -> 52.6 us (level)
  no operation moved by 1% of the time
where the time goes in v8:
time: 52.6 us; the launch traced here: 52.4 us
  starting transfers between devices  28.3 us (54%)
  waiting for transfers between devices  16.7 us (32%)
  Pallas kernels  6.19 us (12%)
  between operations  0.81 us (2%)
    ppermute x13, starting transfers between devices, flip(): return lax.ppermute(value, axis, [(i, i ^ bit) for i in range(count)])  23.3 us
    ppermute x13, waiting for transfers between devices, flip(): return lax.ppermute(value, axis, [(i, i ^ bit) for i in range(count)])  16.7 us
    all_to_all x1, starting transfers between devices, exchange(): return lax.all_to_all(blocks, ('section', 'ctx'), 0, 0, tiled=True)  5 us
    pallas_call x1, Pallas kernels, query_kernel(): pl.pallas_call(body, in_specs=in_vmem(6), out_specs=[pl.BlockSpec(memory_...  2.24 us
    pallas_call x1, Pallas kernels, combine_kernel(): pl.pallas_call(body, in_specs=in_vmem(1), out_specs=in_vmem(1)[0], out_sh...  1.37 us
    pallas_call x1, Pallas kernels, pack(): pl.pallas_call(body, in_specs=[pl.BlockSpec(memory_space=pl.ANY)] * 6, ou...  1.12 us
  transfers between devices with their start and end apart: 14, of which 9 were waited for; matrix products, arithmetic and copies ran while one was open for 1% of the time, Pallas kernels for 6%

profile of v8, /device:TPU:0, one launch (start us, length us, event | category | flops | bytes accessed | tf_op | source)
XLA Modules:
  0.0 52.4 jit_solution(10547363654749460647)
XLA Ops:
  0.6 1.1 %pack.1 = (bf16[2,8,768]{2,1,0:T(8,128)(2,1)S(1)}, bf16[2,8,768]{2,1,0:T(8,128)(2,1)S(1)}, bf16[2,8,640]{2,1,0:T(8,128)(2,1)S(1)}, bf16[2,8,640]{2,1,0:T(8,128)(...) custom-call(s32[8]{0:T(128)} %order_hbm.1, bf16[128,640]{1,0:T(8,128)(2,1)} %k_hbm.1, ...), custom_call_target="tpu_custom_call" | custom-call | tf_op jit(solution)/shard_map/pack/pallas_call | solution.py:112
  1.8 0.6 %collective-permute-start.5 = (bf16[2,8,640]{2,1,0:T(8,128)(2,1)S(1)}, bf16[2,8,640]{2,1,0:T(8,128)(2,1)S(1)}, u32[]{:S(2)}, u32[]{:S(2)}) collective-permute-start(bf16[2,8,640]{2,1,0:T(8,128)(2,1)S(1)} %get-tuple-element.18), channel_id=1, source_target_pairs={{0,8},{8,0},{16,24},{24,16},{1,9},{9,1},{17,25},{25,17},{2,10},{10... | collective-permute-start | bytes 61448 | tf_op jit(solution)/shard_map/ppermute | solution.py:301
  2.4 0.8 %collective-permute-done.5 = bf16[2,8,640]{2,1,0:T(8,128)(2,1)S(1)} collective-permute-done((bf16[2,8,640]{2,1,0:T(8,128)(2,1)S(1)}, bf16[2,8,640]{2,1,0:T(8,128)(2,1)S(1)}, u32[]{:S(2)}, u32[]{:S(2)}) %collective-permute-start.5) | collective-permute-done | bytes 20512 | tf_op jit(solution)/shard_map/ppermute | solution.py:301
  3.2 2.9 %collective-permute-start.6 = (bf16[2,8,640]{2,1,0:T(8,128)(2,1)S(1)}, bf16[2,8,640]{2,1,0:T(8,128)(2,1)S(1)}, u32[]{:S(2)}, u32[]{:S(2)}) collective-permute-start(bf16[2,8,640]{2,1,0:T(8,128)(2,1)S(1)} %fusion.5), channel_id=1, source_target_pairs={{0,16},{8,24},{16,0},{24,8},{1,17},{9,25},{17,1},{25,9},{2,18},{10... | collective-permute-start | bytes 61448 | tf_op jit(solution)/shard_map/ppermute | solution.py:301
  6.2 1.6 %collective-permute-done.6 = bf16[2,8,640]{2,1,0:T(8,128)(2,1)S(1)} collective-permute-done((bf16[2,8,640]{2,1,0:T(8,128)(2,1)S(1)}, bf16[2,8,640]{2,1,0:T(8,128)(2,1)S(1)}, u32[]{:S(2)}, u32[]{:S(2)}) %collective-permute-start.6) | collective-permute-done | bytes 20512 | tf_op jit(solution)/shard_map/ppermute | solution.py:301
  7.9 3.2 %collective-permute-start.7 = (bf16[4,8,640]{2,1,0:T(8,128)(2,1)S(1)}, bf16[4,8,640]{2,1,0:T(8,128)(2,1)S(1)}, u32[]{:S(2)}, u32[]{:S(2)}) collective-permute-start(bf16[4,8,640]{2,1,0:T(8,128)(2,1)S(1)} %bitcast.122), channel_id=1, source_target_pairs={{0,4},{1,5},{2,6},{3,7},{4,0},{5,1},{6,2},{7,3},{8,12},{9,13},{10,... | collective-permute-start | bytes 122888 | tf_op jit(solution)/shard_map/ppermute | solution.py:301
  11.1 1.6 %collective-permute-start.2 = (bf16[4,8,768]{2,1,0:T(8,128)(2,1)S(1)}, bf16[4,8,768]{2,1,0:T(8,128)(2,1)S(1)}, u32[]{:S(2)}, u32[]{:S(2)}) collective-permute-start(bf16[4,8,768]{2,1,0:T(8,128)(2,1)S(1)} %bitcast.121), channel_id=1, source_target_pairs={{0,4},{1,5},{2,6},{3,7},{4,0},{5,1},{6,2},{7,3},{8,12},{9,13},{10,... | collective-permute-start | bytes 147464 | tf_op jit(solution)/shard_map/ppermute | solution.py:301
  13.1 1.9 %collective-permute-start.8 = (bf16[4,2,8,640]{3,2,1,0:T(8,128)(2,1)S(1)}, bf16[4,2,8,640]{3,2,1,0:T(8,128)(2,1)S(1)}, u32[]{:S(2)}, u32[]{:S(2)}) collective-permute-start(bf16[4,2,8,640]{3,2,1,0:T(8,128)(2,1)S(1)} %pad_maximum_fusion.5), channel_id=1, source_target_pairs={{0,1},{1,0},{2,3},{3,2},{4,5},{5,4},{6,7},{7,6},{8,9},{9,8},{10,11... | collective-permute-start | bytes 245768 | tf_op jit(solution)/shard_map/ppermute | solution.py:301
  15.0 1.1 %collective-permute-done.2 = bf16[4,8,768]{2,1,0:T(8,128)(2,1)S(1)} collective-permute-done((bf16[4,8,768]{2,1,0:T(8,128)(2,1)S(1)}, bf16[4,8,768]{2,1,0:T(8,128)(2,1)S(1)}, u32[]{:S(2)}, u32[]{:S(2)}) %collective-permute-start.2) | collective-permute-done | bytes 49184 | tf_op jit(solution)/shard_map/ppermute | solution.py:301
  16.2 1.6 %collective-permute-start.3 = (bf16[4,2,8,768]{3,2,1,0:T(8,128)(2,1)S(1)}, bf16[4,2,8,768]{3,2,1,0:T(8,128)(2,1)S(1)}, u32[]{:S(2)}, u32[]{:S(2)}) collective-permute-start(bf16[4,2,8,768]{3,2,1,0:T(8,128)(2,1)S(1)} %pad_maximum_fusion.4), channel_id=1, source_target_pairs={{0,2},{1,3},{2,0},{3,1},{4,6},{5,7},{6,4},{7,5},{8,10},{9,11},{10,... | collective-permute-start | bytes 294920 | tf_op jit(solution)/shard_map/ppermute | solution.py:301
  17.9 1.7 %collective-permute-start.9 = (bf16[4,2,2,8,640]{4,3,2,1,0:T(8,128)(2,1)S(1)}, bf16[4,2,2,8,640]{4,3,2,1,0:T(8,128)(2,1)S(1)}, u32[]{:S(2)}, u32[]{:S(2)}) collective-permute-start(bf16[4,2,2,8,640]{4,3,2,1,0:T(8,128)(2,1)S(1)} %pad_maximum_fusion.3), channel_id=1, source_target_pairs={{0,2},{1,3},{2,0},{3,1},{4,6},{5,7},{6,4},{7,5},{8,10},{9,11},{10,... | collective-permute-start | bytes 491528 | tf_op jit(solution)/shard_map/ppermute | solution.py:301
  19.6 1.2 %collective-permute-done.3 = bf16[4,2,8,768]{3,2,1,0:T(8,128)(2,1)S(1)} collective-permute-done((bf16[4,2,8,768]{3,2,1,0:T(8,128)(2,1)S(1)}, bf16[4,2,8,768]{3,2,1,0:T(8,128)(2,1)S(1)}, u32[]{:S(2)}, u32[]{:S(2)}) %collective-permute-start.3) | collective-permute-done | bytes 98336 | tf_op jit(solution)/shard_map/ppermute | solution.py:301
  20.9 1.6 %collective-permute-start.4 = (bf16[4,2,2,8,768]{4,3,2,1,0:T(8,128)(2,1)S(1)}, bf16[4,2,2,8,768]{4,3,2,1,0:T(8,128)(2,1)S(1)}, u32[]{:S(2)}, u32[]{:S(2)}) collective-permute-start(bf16[4,2,2,8,768]{4,3,2,1,0:T(8,128)(2,1)S(1)} %pad_maximum_fusion.2), channel_id=1, source_target_pairs={{0,1},{1,0},{2,3},{3,2},{4,5},{5,4},{6,7},{7,6},{8,9},{9,8},{10,11... | collective-permute-start | bytes 589832 | tf_op jit(solution)/shard_map/ppermute | solution.py:301
  22.5 0.8 %collective-permute-done.9 = bf16[4,2,2,8,640]{4,3,2,1,0:T(8,128)(2,1)S(1)} collective-permute-done((bf16[4,2,2,8,640]{4,3,2,1,0:T(8,128)(2,1)S(1)}, bf16[4,2,2,8,640]{4,3,2,1,0:T(8,128)(2,1)S(1)}, u32[]{:S(2)}, u32[]{:S(2)}) %collective-permute-start.9) | collective-permute-done | bytes 163872 | tf_op jit(solution)/shard_map/ppermute | solution.py:301
  23.3 3.5 %collective-permute-done.4 = bf16[4,2,2,8,768]{4,3,2,1,0:T(8,128)(2,1)S(1)} collective-permute-done((bf16[4,2,2,8,768]{4,3,2,1,0:T(8,128)(2,1)S(1)}, bf16[4,2,2,8,768]{4,3,2,1,0:T(8,128)(2,1)S(1)}, u32[]{:S(2)}, u32[]{:S(2)}) %collective-permute-start.4) | collective-permute-done | bytes 196640 | tf_op jit(solution)/shard_map/ppermute | solution.py:301
  27.3 1.6 %collective-permute-start.10 = (f32[2,8,256]{2,1,0:T(8,128)S(1)}, f32[2,8,256]{2,1,0:T(8,128)S(1)}, u32[]{:S(2)}, u32[]{:S(2)}) collective-permute-start(f32[2,8,256]{2,1,0:T(8,128)S(1)} %stats.1.l_ref.own_ref), channel_id=1, source_target_pairs={{0,1},{1,0},{2,3},{3,2},{4,5},{5,4},{6,7},{7,6},{8,9},{9,8},{10,11... | collective-permute-start | bytes 49160 | tf_op jit(solution)/shard_map/ppermute | solution.py:301
  29.0 2.2 %query_gradients.1 = (bf16[256,768]{1,0:T(8,128)(2,1)}, bf16[5,128,256]{2,1,0:T(8,128)(2,1)S(1)}, bf16[5,128,256]{2,1,0:T(8,128)(2,1)S(1)}) custom-call(s32[8,128]{1,0:T(8,128)S(1)} %get-tuple-element.15.start_ref, bf16[256,768]{1,0:T(8,128)(2,1)S(1)} %bitcast.115, bf16[256,640]{1,0:T(8,128)(2,1)S(1)} %bitcast.117, ...), custom_call_target="tpu_custom_call" | custom-call | tf_op jit(solution)/shard_map/query_gradients/pallas_call | solution.py:213
  31.2 5.0 %all-to-all-start = ((bf16[32,8,768]{2,1,0:T(8,128)(2,1)}), bf16[32,8,768]{2,1,0:T(8,128)(2,1)S(1)}, u32[]{:S(2)}, u32[]{:S(2)}) async-start(bf16[32,8,768]{2,1,0:T(8,128)(2,1)} %bitcast.120), calls=%async_computation | async-start | bytes 786432 | tf_op jit(solution)/shard_map/all_to_all | solution.py:341
  36.2 1.8 %collective-permute-start.11 = (f32[2,8,256]{2,1,0:T(8,128)S(1)}, f32[2,8,256]{2,1,0:T(8,128)S(1)}, u32[]{:S(2)}, u32[]{:S(2)}) collective-permute-start(f32[2,8,256]{2,1,0:T(8,128)S(1)} %pad_maximum_fusion.10), channel_id=1, source_target_pairs={{0,2},{1,3},{2,0},{3,1},{4,6},{5,7},{6,4},{7,5},{8,10},{9,11},{10,... | collective-permute-start | bytes 49160 | tf_op jit(solution)/shard_map/ppermute | solution.py:301
  38.1 5.5 %collective-permute-done.11 = f32[2,8,256]{2,1,0:T(8,128)S(1)} collective-permute-done((f32[2,8,256]{2,1,0:T(8,128)S(1)}, f32[2,8,256]{2,1,0:T(8,128)S(1)}, u32[]{:S(2)}, u32[]{:S(2)}) %collective-permute-start.11) | collective-permute-done | bytes 16416 | tf_op jit(solution)/shard_map/ppermute | solution.py:301
  43.6 4.6 %collective-permute-start.12 = (f32[2,8,256]{2,1,0:T(8,128)S(1)}, f32[2,8,256]{2,1,0:T(8,128)S(1)}, u32[]{:S(2)}, u32[]{:S(2)}) collective-permute-start(f32[2,8,256]{2,1,0:T(8,128)S(1)} %pad_maximum_fusion.11), channel_id=1, source_target_pairs={{0,4},{1,5},{2,6},{3,7},{4,0},{5,1},{6,2},{7,3},{8,12},{9,13},{10,... | collective-permute-start | bytes 49160 | tf_op jit(solution)/shard_map/ppermute | solution.py:301
  48.2 1.7 %collective-permute-done.12 = f32[2,8,256]{2,1,0:T(8,128)S(1)} collective-permute-done((f32[2,8,256]{2,1,0:T(8,128)S(1)}, f32[2,8,256]{2,1,0:T(8,128)S(1)}, u32[]{:S(2)}, u32[]{:S(2)}) %collective-permute-start.12) | collective-permute-done | bytes 16416 | tf_op jit(solution)/shard_map/ppermute | solution.py:301
  50.0 1.0 %cache_gradients.1 = (bf16[128,640]{1,0:T(8,128)(2,1)}, bf16[128,640]{1,0:T(8,128)(2,1)}) custom-call(bf16[256,768]{1,0:T(8,128)(2,1)S(1)} %bitcast.116, bf16[256,640]{1,0:T(8,128)(2,1)S(1)} %bitcast.118, bf16[5,128,256]{2,1,0:T(8,128)(2,1)S(1)} %get-tuple-element.23.p_ref, bf16[5,128,256]{2,1,0:T(8,128)(2,1)S(1)} %get-tuple-element.24.ds_ref, ...), custom_call_target="tpu_custom_call" | custom-call | tf_op jit(solution)/shard_map/cache_gradients/pallas_call | solution.py:244
  51.0 1.4 %combine.1 = bf16[8,2560]{1,0:T(8,128)(2,1)} custom-call(bf16[4,8,8,768]{3,2,1,0:T(8,128)(2,1)S(1)} %bitcast.119), custom_call_target="tpu_custom_call" | custom-call | tf_op jit(solution)/shard_map/combine/pallas_call | solution.py:281
  (35 shorter events, 1.4 us)
Async XLA Ops:
  1.8 1.4 %collective-permute-start.5 = (bf16[2,8,640]{2,1,0:T(8,128)(2,1)S(1)}, bf16[2,8,640]{2,1,0:T(8,128)(2,1)S(1)}, u32[]{:S(2)}, u32[]{:S(2)}) collective-permute-start(bf16[2,8,640]{2,1,0:T(8,128)(2,1)S(1)} %get-tuple-element.18), channel_id=1, source_target_pairs={{0,8},{8,0},{16,24},{24,16},{1,9},{9,1},{17,25},{25,17},{2,10},{10... | collective-permute-start | bytes 61448 | tf_op jit(solution)/shard_map/ppermute | solution.py:301
  2.3 3.8 %collective-permute-start = (bf16[2,8,768]{2,1,0:T(8,128)(2,1)S(1)}, bf16[2,8,768]{2,1,0:T(8,128)(2,1)S(1)}, u32[]{:S(2)}, u32[]{:S(2)}) collective-permute-start(bf16[2,8,768]{2,1,0:T(8,128)(2,1)S(1)} %get-tuple-element.16), channel_id=1, source_target_pairs={{0,8},{8,0},{16,24},{24,16},{1,9},{9,1},{17,25},{25,17},{2,10},{10... | collective-permute-start | bytes 73736 | tf_op jit(solution)/shard_map/ppermute | solution.py:301
  3.2 4.6 %collective-permute-start.6 = (bf16[2,8,640]{2,1,0:T(8,128)(2,1)S(1)}, bf16[2,8,640]{2,1,0:T(8,128)(2,1)S(1)}, u32[]{:S(2)}, u32[]{:S(2)}) collective-permute-start(bf16[2,8,640]{2,1,0:T(8,128)(2,1)S(1)} %fusion.5), channel_id=1, source_target_pairs={{0,16},{8,24},{16,0},{24,8},{1,17},{9,25},{17,1},{25,9},{2,18},{10... | collective-permute-start | bytes 61448 | tf_op jit(solution)/shard_map/ppermute | solution.py:301
  6.1 5.0 %collective-permute-start.1 = (bf16[2,8,768]{2,1,0:T(8,128)(2,1)S(1)}, bf16[2,8,768]{2,1,0:T(8,128)(2,1)S(1)}, u32[]{:S(2)}, u32[]{:S(2)}) collective-permute-start(bf16[2,8,768]{2,1,0:T(8,128)(2,1)S(1)} %fusion.2), channel_id=1, source_target_pairs={{0,16},{8,24},{16,0},{24,8},{1,17},{9,25},{17,1},{25,9},{2,18},{10... | collective-permute-start | bytes 73736 | tf_op jit(solution)/shard_map/ppermute | solution.py:301
  7.9 5.2 %collective-permute-start.7 = (bf16[4,8,640]{2,1,0:T(8,128)(2,1)S(1)}, bf16[4,8,640]{2,1,0:T(8,128)(2,1)S(1)}, u32[]{:S(2)}, u32[]{:S(2)}) collective-permute-start(bf16[4,8,640]{2,1,0:T(8,128)(2,1)S(1)} %bitcast.122), channel_id=1, source_target_pairs={{0,4},{1,5},{2,6},{3,7},{4,0},{5,1},{6,2},{7,3},{8,12},{9,13},{10,... | collective-permute-start | bytes 122888 | tf_op jit(solution)/shard_map/ppermute | solution.py:301
  11.1 5.1 %collective-permute-start.2 = (bf16[4,8,768]{2,1,0:T(8,128)(2,1)S(1)}, bf16[4,8,768]{2,1,0:T(8,128)(2,1)S(1)}, u32[]{:S(2)}, u32[]{:S(2)}) collective-permute-start(bf16[4,8,768]{2,1,0:T(8,128)(2,1)S(1)} %bitcast.121), channel_id=1, source_target_pairs={{0,4},{1,5},{2,6},{3,7},{4,0},{5,1},{6,2},{7,3},{8,12},{9,13},{10,... | collective-permute-start | bytes 147464 | tf_op jit(solution)/shard_map/ppermute | solution.py:301
  13.1 4.7 %collective-permute-start.8 = (bf16[4,2,8,640]{3,2,1,0:T(8,128)(2,1)S(1)}, bf16[4,2,8,640]{3,2,1,0:T(8,128)(2,1)S(1)}, u32[]{:S(2)}, u32[]{:S(2)}) collective-permute-start(bf16[4,2,8,640]{3,2,1,0:T(8,128)(2,1)S(1)} %pad_maximum_fusion.5), channel_id=1, source_target_pairs={{0,1},{1,0},{2,3},{3,2},{4,5},{5,4},{6,7},{7,6},{8,9},{9,8},{10,11... | collective-permute-start | bytes 245768 | tf_op jit(solution)/shard_map/ppermute | solution.py:301
  16.2 4.7 %collective-permute-start.3 = (bf16[4,2,8,768]{3,2,1,0:T(8,128)(2,1)S(1)}, bf16[4,2,8,768]{3,2,1,0:T(8,128)(2,1)S(1)}, u32[]{:S(2)}, u32[]{:S(2)}) collective-permute-start(bf16[4,2,8,768]{3,2,1,0:T(8,128)(2,1)S(1)} %pad_maximum_fusion.4), channel_id=1, source_target_pairs={{0,2},{1,3},{2,0},{3,1},{4,6},{5,7},{6,4},{7,5},{8,10},{9,11},{10,... | collective-permute-start | bytes 294920 | tf_op jit(solution)/shard_map/ppermute | solution.py:301
  17.9 5.4 %collective-permute-start.9 = (bf16[4,2,2,8,640]{4,3,2,1,0:T(8,128)(2,1)S(1)}, bf16[4,2,2,8,640]{4,3,2,1,0:T(8,128)(2,1)S(1)}, u32[]{:S(2)}, u32[]{:S(2)}) collective-permute-start(bf16[4,2,2,8,640]{4,3,2,1,0:T(8,128)(2,1)S(1)} %pad_maximum_fusion.3), channel_id=1, source_target_pairs={{0,2},{1,3},{2,0},{3,1},{4,6},{5,7},{6,4},{7,5},{8,10},{9,11},{10,... | collective-permute-start | bytes 491528 | tf_op jit(solution)/shard_map/ppermute | solution.py:301
  20.9 5.9 %collective-permute-start.4 = (bf16[4,2,2,8,768]{4,3,2,1,0:T(8,128)(2,1)S(1)}, bf16[4,2,2,8,768]{4,3,2,1,0:T(8,128)(2,1)S(1)}, u32[]{:S(2)}, u32[]{:S(2)}) collective-permute-start(bf16[4,2,2,8,768]{4,3,2,1,0:T(8,128)(2,1)S(1)} %pad_maximum_fusion.2), channel_id=1, source_target_pairs={{0,1},{1,0},{2,3},{3,2},{4,5},{5,4},{6,7},{7,6},{8,9},{9,8},{10,11... | collective-permute-start | bytes 589832 | tf_op jit(solution)/shard_map/ppermute | solution.py:301
  27.3 8.9 %collective-permute-start.10 = (f32[2,8,256]{2,1,0:T(8,128)S(1)}, f32[2,8,256]{2,1,0:T(8,128)S(1)}, u32[]{:S(2)}, u32[]{:S(2)}) collective-permute-start(f32[2,8,256]{2,1,0:T(8,128)S(1)} %stats.1.l_ref.own_ref), channel_id=1, source_target_pairs={{0,1},{1,0},{2,3},{3,2},{4,5},{5,4},{6,7},{7,6},{8,9},{9,8},{10,11... | collective-permute-start | bytes 49160 | tf_op jit(solution)/shard_map/ppermute | solution.py:301
  31.2 19.8 %all-to-all-start = ((bf16[32,8,768]{2,1,0:T(8,128)(2,1)}), bf16[32,8,768]{2,1,0:T(8,128)(2,1)S(1)}, u32[]{:S(2)}, u32[]{:S(2)}) async-start(bf16[32,8,768]{2,1,0:T(8,128)(2,1)} %bitcast.120), calls=%async_computation | async-start | bytes 786432 | tf_op jit(solution)/shard_map/all_to_all | solution.py:341
  36.2 7.4 %collective-permute-start.11 = (f32[2,8,256]{2,1,0:T(8,128)S(1)}, f32[2,8,256]{2,1,0:T(8,128)S(1)}, u32[]{:S(2)}, u32[]{:S(2)}) collective-permute-start(f32[2,8,256]{2,1,0:T(8,128)S(1)} %pad_maximum_fusion.10), channel_id=1, source_target_pairs={{0,2},{1,3},{2,0},{3,1},{4,6},{5,7},{6,4},{7,5},{8,10},{9,11},{10,... | collective-permute-start | bytes 49160 | tf_op jit(solution)/shard_map/ppermute | solution.py:301
  43.6 6.3 %collective-permute-start.12 = (f32[2,8,256]{2,1,0:T(8,128)S(1)}, f32[2,8,256]{2,1,0:T(8,128)S(1)}, u32[]{:S(2)}, u32[]{:S(2)}) collective-permute-start(f32[2,8,256]{2,1,0:T(8,128)S(1)} %pad_maximum_fusion.11), channel_id=1, source_target_pairs={{0,4},{1,5},{2,6},{3,7},{4,0},{5,1},{6,2},{7,3},{8,12},{9,13},{10,... | collective-permute-start | bytes 49160 | tf_op jit(solution)/shard_map/ppermute | solution.py:301

commit v9 on v8

--- a/solution.py
+++ b/solution.py
@@ -65,11 +65,10 @@
     here = features // sections
     heads = here // HEAD_DIM
     key_count = keys.shape[0]
-    half = sections // 2
 
     def body(order_hbm, k_hbm, v_hbm, q_hbm, g_hbm, o_hbm, *refs):
-        q_mine, q_other, g_mine, g_other, start_ref, k_ref, v_ref = refs[:7]
-        q_ref, g_ref, o_ref, order_ref, sems = refs[7:]
+        blocks = refs[:sections]
+        start_ref, k_ref, v_ref, q_ref, g_ref, o_ref, order_ref, sems = refs[sections:]
         pairs = [
             (q_hbm, q_ref),
             (g_hbm, g_ref),
@@ -81,7 +80,7 @@
         copies = [pltpu.make_async_copy(*pair, sems.at[i]) for i, pair in enumerate(pairs)]
         for copy in copies:
             copy.start()
-        odd = lax.axis_index("section") % 2
+        section = lax.axis_index("section")
         lane = lax.broadcasted_iota(jnp.int32, (rows, LANES), 1)
 
         def at(s, h):
@@ -89,35 +88,30 @@
 
         for i in range(3):
             copies[i].wait()
-        for q_out, g_out, bit in ((q_mine, g_mine, odd), (q_other, g_other, 1 - odd)):
-            for j in range(half):
-                extra = jnp.zeros((rows, LANES), F32)
-                for h in range(heads):
-                    g = g_ref[:, at(2 * j + bit, h)]
-                    terms = g.astype(F32) * o_ref[:, at(2 * j + bit, h)].astype(F32)
-                    delta = jnp.sum(terms, axis=1, keepdims=True)
-                    for part, value in enumerate(split3(delta)):
-                        extra = jnp.where(lane == part * heads + h, value.astype(F32), extra)
-                    g_out[j, :, head_of(h)] = g
-                    q_out[j, :, head_of(h)] = q_ref[:, at(2 * j + bit, h)]
-                q_out[j, :, pl.ds(here, LANES)] = extra.astype(BF)
+        for step, out_ref in enumerate(blocks):
+            to = section ^ step
+            extra = jnp.zeros((rows, LANES), F32)
+            for h in range(heads):
+                g = g_ref[:, at(to, h)]
+                terms = g.astype(F32) * o_ref[:, at(to, h)].astype(F32)
+                delta = jnp.sum(terms, axis=1, keepdims=True)
+                for part, value in enumerate(split3(delta)):
+                    extra = jnp.where(lane == part * heads + h, value.astype(F32), extra)
+                out_ref[:, head_of(h)] = q_ref[:, at(to, h)]
+                out_ref[:, head_of(heads + 1 + h)] = g
+            out_ref[:, head_of(heads)] = extra.astype(BF)
         copies[3].wait()
         block = order_ref[lax.axis_index("ctx")]
         start_ref[...] = jnp.full(start_ref.shape, block * key_count, jnp.int32)
         copies[4].wait()
         copies[5].wait()
 
-    query_half = held((half, rows, here + LANES), BF)
-    grad_half = held((half, rows, here), BF)
     return pl.pallas_call(
         body,
         in_specs=[pl.BlockSpec(memory_space=pl.ANY)] * 6,
-        out_specs=in_vmem(7),
+        out_specs=in_vmem(sections + 3),
         out_shape=[
-            query_half,
-            query_half,
-            grad_half,
-            grad_half,
+            *[held((rows, 2 * here + LANES), BF)] * sections,
             held((8, LANES), jnp.int32),
             held(keys.shape, BF),
             held(values.shape, BF),
@@ -307,22 +301,18 @@
     return jnp.stack([first, second], axis)
 
 
-def swap_blocks(mine, other, axis):
+def swap_blocks(blocks, axis):
     count = lax.axis_size(axis)
-    bits = count.bit_length() - 1
-    rest = mine.shape[1:]
-    mine = mine.reshape((2,) * (bits - 1) + rest)
-    other = other.reshape(mine.shape)
-    for i in range(bits):
-        upper = (lax.axis_index(axis) >> i) % 2 == 1
-        if i:
-            first = lax.index_in_dim(blocks, 0, bits - 1, keepdims=False)
-            second = lax.index_in_dim(blocks, 1, bits - 1, keepdims=False)
-            mine = jnp.where(upper, second, first)
-            other = jnp.where(upper, first, second)
-        other = flip(other, axis, 1 << i)
-        blocks = ordered(mine, other, upper, 0)
-    return blocks.reshape((count,) + rest)
+    here = lax.axis_index(axis)
+    got = [blocks[0]]
+    for step in range(1, count):
+        got.append(flip(blocks[step], axis, step))
+    bit = 1
+    while bit < count:
+        upper = here & bit != 0
+        got = [jnp.where(upper, got[i ^ bit], got[i]) for i in range(count)]
+        bit *= 2
+    return jnp.stack(got)
 
 
 def spread_blocks(blocks, axis, order):
@@ -365,16 +355,16 @@
         attention_out[0],
         sections,
     )
-    start, keys, values = packed[4:]
-    query_all = swap_blocks(packed[0], packed[1], "section")
+    start, keys, values = packed[sections:]
+    swapped = swap_blocks(packed[:sections], "section")
+    query_all, grad_all = swapped[..., : here + LANES], swapped[..., here + LANES :]
     query_all = spread_blocks(query_all, "ctx", down)
     query_all = query_all.reshape(peers * rows, here + LANES)
-    grad_all = swap_blocks(packed[2], packed[3], "section")
     grad_all = spread_blocks(grad_all, "ctx", down[:1] + down[1:][::-1])
     grad_all = grad_all.reshape(peers * rows, here)
 
     own = stats_kernel(start, query_all, keys, row_count, key_total)
-    merged = merge_stats(own, "ctx", down[::-1])
+    merged = merge_stats(own, "ctx", down[-1:] + down[:-1])
     part, probs, score_grads = query_kernel(
         start, query_all, grad_all, keys, values, own, row_count, key_total
     )

time: 52.6 us -> 54.9 us (1.044)
  waiting for transfers between devices: 16.7 us -> 25.5 us
  starting transfers between devices: 28.3 us -> 21.7 us
    ppermute x13 -> x12, waiting for transfers between devices: 16.7 us -> 25.5 us  [flip(): return lax.ppermute(value, axis, [(i, i ^ bit) for i in range(count)])]
    ppermute x13 -> x12, starting transfers between devices: 23.3 us -> 17.5 us  [flip(): return lax.ppermute(value, axis, [(i, i ^ bit) for i in range(count)])]
    all_to_all x1, starting transfers between devices: 5 us -> 4.2 us  [exchange(): return lax.all_to_all(blocks, ('section', 'ctx'), 0, 0, tiled=True)]
  transfers between devices with their start and end apart: 14 -> 13, of which waited for: 9 -> 10; matrix products, arithmetic and copies ran while one was open for 1% -> 1% of each run, Pallas kernels for 6% -> 6%
where the time goes in v9:
time: 54.9 us; the launch traced here: 54.7 us
  waiting for transfers between devices  25.5 us (46%)
  starting transfers between devices  21.7 us (40%)
  Pallas kernels  6.19 us (11%)
  between operations  0.82 us (1%)
    ppermute x12, waiting for transfers between devices, flip(): return lax.ppermute(value, axis, [(i, i ^ bit) for i in range(count)])  25.5 us
    ppermute x12, starting transfers between devices, flip(): return lax.ppermute(value, axis, [(i, i ^ bit) for i in range(count)])  17.5 us
    all_to_all x1, starting transfers between devices, exchange(): return lax.all_to_all(blocks, ('section', 'ctx'), 0, 0, tiled=True)  4.2 us
    pallas_call x1, Pallas kernels, query_kernel(): pl.pallas_call(body, in_specs=in_vmem(6), out_specs=[pl.BlockSpec(memory_...  2.23 us
    pallas_call x1, Pallas kernels, combine_kernel(): pl.pallas_call(body, in_specs=in_vmem(1), out_specs=in_vmem(1)[0], out_sh...  1.37 us
    pallas_call x1, Pallas kernels, pack(): pl.pallas_call(body, in_specs=[pl.BlockSpec(memory_space=pl.ANY)] * 6, ou...  1.12 us
  transfers between devices with their start and end apart: 13, of which 10 were waited for; matrix products, arithmetic and copies ran while one was open for 1% of the time, Pallas kernels for 6%

profile of v9, /device:TPU:0, one launch (start us, length us, event | category | flops | bytes accessed | tf_op | source)
XLA Modules:
  0.0 54.7 jit_solution(4773486636385030210)
XLA Ops:
  0.6 1.1 %pack.1 = (bf16[8,1408]{1,0:T(8,128)(2,1)S(1)}, bf16[8,1408]{1,0:T(8,128)(2,1)S(1)}, bf16[8,1408]{1,0:T(8,128)(2,1)S(1)}, bf16[8,1408]{1,0:T(8,128)(2,1)S(1)}, s...) custom-call(s32[8]{0:T(128)} %order_hbm.1, bf16[128,640]{1,0:T(8,128)(2,1)} %k_hbm.1, ...), custom_call_target="tpu_custom_call" | custom-call | tf_op jit(solution)/shard_map/pack/pallas_call | solution.py:109
  1.8 2.5 %collective-permute-start = (bf16[8,1408]{1,0:T(8,128)(2,1)S(1)}, bf16[8,1408]{1,0:T(8,128)(2,1)S(1)}, u32[]{:S(2)}, u32[]{:S(2)}) collective-permute-start(bf16[8,1408]{1,0:T(8,128)(2,1)S(1)} %get-tuple-element.16), channel_id=1, source_target_pairs={{0,24},{8,16},{16,8},{24,0},{1,25},{9,17},{17,9},{25,1},{2,26},{10... | collective-permute-start | bytes 67592 | tf_op jit(solution)/shard_map/ppermute | solution.py:295
  4.2 0.6 %collective-permute-start.1 = (bf16[8,1408]{1,0:T(8,128)(2,1)S(1)}, bf16[8,1408]{1,0:T(8,128)(2,1)S(1)}, u32[]{:S(2)}, u32[]{:S(2)}) collective-permute-start(bf16[8,1408]{1,0:T(8,128)(2,1)S(1)} %get-tuple-element.17), channel_id=1, source_target_pairs={{0,16},{8,24},{16,0},{24,8},{1,17},{9,25},{17,1},{25,9},{2,18},{10... | collective-permute-start | bytes 67592 | tf_op jit(solution)/shard_map/ppermute | solution.py:295
  4.9 0.9 %collective-permute-done = bf16[8,1408]{1,0:T(8,128)(2,1)S(1)} collective-permute-done((bf16[8,1408]{1,0:T(8,128)(2,1)S(1)}, bf16[8,1408]{1,0:T(8,128)(2,1)S(1)}, u32[]{:S(2)}, u32[]{:S(2)}) %collective-permute-start) | collective-permute-done | bytes 22560 | tf_op jit(solution)/shard_map/ppermute | solution.py:295
  5.8 2.2 %collective-permute-done.1 = bf16[8,1408]{1,0:T(8,128)(2,1)S(1)} collective-permute-done((bf16[8,1408]{1,0:T(8,128)(2,1)S(1)}, bf16[8,1408]{1,0:T(8,128)(2,1)S(1)}, u32[]{:S(2)}, u32[]{:S(2)}) %collective-permute-start.1) | collective-permute-done | bytes 22560 | tf_op jit(solution)/shard_map/ppermute | solution.py:295
  8.1 2.7 %collective-permute-start.6 = (bf16[4,8,640]{2,1,0:T(8,128)(2,1)S(1)}, bf16[4,8,640]{2,1,0:T(8,128)(2,1)S(1)}, u32[]{:S(2)}, u32[]{:S(2)}) collective-permute-start(bf16[4,8,640]{2,1,0:T(8,128)(2,1)S(1)} %pad_maximum_fusion.7), channel_id=1, source_target_pairs={{0,4},{1,5},{2,6},{3,7},{4,0},{5,1},{6,2},{7,3},{8,12},{9,13},{10,... | collective-permute-start | bytes 122888 | tf_op jit(solution)/shard_map/ppermute | solution.py:295
  11.2 1.9 %collective-permute-done.6 = bf16[4,8,640]{2,1,0:T(8,128)(2,1)S(1)} collective-permute-done((bf16[4,8,640]{2,1,0:T(8,128)(2,1)S(1)}, bf16[4,8,640]{2,1,0:T(8,128)(2,1)S(1)}, u32[]{:S(2)}, u32[]{:S(2)}) %collective-permute-start.6) | collective-permute-done | bytes 40992 | tf_op jit(solution)/shard_map/ppermute | solution.py:295
  13.1 1.6 %collective-permute-start.7 = (bf16[4,2,8,640]{3,2,0,1:T(8,128)(2,1)S(1)}, bf16[4,2,8,640]{3,2,0,1:T(8,128)(2,1)S(1)}, u32[]{:S(2)}, u32[]{:S(2)}) collective-permute-start(bf16[4,2,8,640]{3,2,0,1:T(8,128)(2,1)S(1)} %pad_maximum_fusion.6), channel_id=1, source_target_pairs={{0,1},{1,0},{2,3},{3,2},{4,5},{5,4},{6,7},{7,6},{8,9},{9,8},{10,11... | collective-permute-start | bytes 245768 | tf_op jit(solution)/shard_map/ppermute | solution.py:295
  14.7 1.1 %collective-permute-done.3 = bf16[4,8,768]{2,1,0:T(8,128)(2,1)S(1)} collective-permute-done((bf16[4,8,768]{2,1,0:T(8,128)(2,1)S(1)}, bf16[4,8,768]{2,1,0:T(8,128)(2,1)S(1)}, u32[]{:S(2)}, u32[]{:S(2)}) %collective-permute-start.3) | collective-permute-done | bytes 49184 | tf_op jit(solution)/shard_map/ppermute | solution.py:295
  15.9 1.6 %collective-permute-start.4 = (bf16[4,2,8,768]{3,2,0,1:T(8,128)(2,1)S(1)}, bf16[4,2,8,768]{3,2,0,1:T(8,128)(2,1)S(1)}, u32[]{:S(2)}, u32[]{:S(2)}) collective-permute-start(bf16[4,2,8,768]{3,2,0,1:T(8,128)(2,1)S(1)} %pad_maximum_fusion.4), channel_id=1, source_target_pairs={{0,2},{1,3},{2,0},{3,1},{4,6},{5,7},{6,4},{7,5},{8,10},{9,11},{10,... | collective-permute-start | bytes 294920 | tf_op jit(solution)/shard_map/ppermute | solution.py:295
  17.7 2.1 %collective-permute-start.8 = (bf16[4,2,2,8,640]{4,3,0,1,2:T(8,128)(2,1)S(1)}, bf16[4,2,2,8,640]{4,3,0,1,2:T(8,128)(2,1)S(1)}, u32[]{:S(2)}, u32[]{:S(2)}) collective-permute-start(bf16[4,2,2,8,640]{4,3,0,1,2:T(8,128)(2,1)S(1)} %pad_maximum_fusion.3), channel_id=1, source_target_pairs={{0,2},{1,3},{2,0},{3,1},{4,6},{5,7},{6,4},{7,5},{8,10},{9,11},{10,... | collective-permute-start | bytes 491528 | tf_op jit(solution)/shard_map/ppermute | solution.py:295
  19.8 1.1 %collective-permute-done.4 = bf16[4,2,8,768]{3,2,0,1:T(8,128)(2,1)S(1)} collective-permute-done((bf16[4,2,8,768]{3,2,0,1:T(8,128)(2,1)S(1)}, bf16[4,2,8,768]{3,2,0,1:T(8,128)(2,1)S(1)}, u32[]{:S(2)}, u32[]{:S(2)}) %collective-permute-start.4) | collective-permute-done | bytes 98336 | tf_op jit(solution)/shard_map/ppermute | solution.py:295
  21.0 1.6 %collective-permute-start.5 = (bf16[4,2,2,8,768]{4,3,0,1,2:T(8,128)(2,1)S(1)}, bf16[4,2,2,8,768]{4,3,0,1,2:T(8,128)(2,1)S(1)}, u32[]{:S(2)}, u32[]{:S(2)}) collective-permute-start(bf16[4,2,2,8,768]{4,3,0,1,2:T(8,128)(2,1)S(1)} %pad_maximum_fusion.2), channel_id=1, source_target_pairs={{0,1},{1,0},{2,3},{3,2},{4,5},{5,4},{6,7},{7,6},{8,9},{9,8},{10,11... | collective-permute-start | bytes 589832 | tf_op jit(solution)/shard_map/ppermute | solution.py:295
  22.6 0.5 collective-permute-done.8
  23.1 3.7 %collective-permute-done.5 = bf16[4,2,2,8,768]{4,3,0,1,2:T(8,128)(2,1)S(1)} collective-permute-done((bf16[4,2,2,8,768]{4,3,0,1,2:T(8,128)(2,1)S(1)}, bf16[4,2,2,8,768]{4,3,0,1,2:T(8,128)(2,1)S(1)}, u32[]{:S(2)}, u32[]{:S(2)}) %collective-permute-start.5) | collective-permute-done | bytes 196640 | tf_op jit(solution)/shard_map/ppermute | solution.py:295
  27.0 0.4 stats.1.l_ref.own_ref
  27.4 1.6 %collective-permute-start.9 = (f32[2,8,256]{2,1,0:T(8,128)S(1)}, f32[2,8,256]{2,1,0:T(8,128)S(1)}, u32[]{:S(2)}, u32[]{:S(2)}) collective-permute-start(f32[2,8,256]{2,1,0:T(8,128)S(1)} %stats.1.l_ref.own_ref), channel_id=1, source_target_pairs={{0,1},{1,0},{2,3},{3,2},{4,5},{5,4},{6,7},{7,6},{8,9},{9,8},{10,11... | collective-permute-start | bytes 49160 | tf_op jit(solution)/shard_map/ppermute | solution.py:295
  29.1 2.2 %query_gradients.1 = (bf16[256,768]{1,0:T(8,128)(2,1)}, bf16[5,128,256]{2,1,0:T(8,128)(2,1)S(1)}, bf16[5,128,256]{2,1,0:T(8,128)(2,1)S(1)}) custom-call(s32[8,128]{1,0:T(8,128)S(1)} %get-tuple-element.15.start_ref, bf16[256,768]{1,0:T(8,128)(2,1)S(1)} %bitcast.41, bf16[256,640]{1,0:T(8,128)(2,1)S(1)} %bitcast.43, ...), custom_call_target="tpu_custom_call" | custom-call | tf_op jit(solution)/shard_map/query_gradients/pallas_call | solution.py:207
  31.3 4.2 %all-to-all-start = ((bf16[32,8,768]{2,1,0:T(8,128)(2,1)}), bf16[32,8,768]{2,1,0:T(8,128)(2,1)S(1)}, u32[]{:S(2)}, u32[]{:S(2)}) async-start(bf16[32,8,768]{2,1,0:T(8,128)(2,1)} %bitcast.46), calls=%async_computation | async-start | bytes 786432 | tf_op jit(solution)/shard_map/all_to_all | solution.py:331
  35.6 2.7 %collective-permute-start.10 = (f32[2,8,256]{2,1,0:T(8,128)S(1)}, f32[2,8,256]{2,1,0:T(8,128)S(1)}, u32[]{:S(2)}, u32[]{:S(2)}) collective-permute-start(f32[2,8,256]{2,1,0:T(8,128)S(1)} %pad_maximum_fusion.8), channel_id=1, source_target_pairs={{0,4},{1,5},{2,6},{3,7},{4,0},{5,1},{6,2},{7,3},{8,12},{9,13},{10,... | collective-permute-start | bytes 49160 | tf_op jit(solution)/shard_map/ppermute | solution.py:295
  38.3 10.1 %collective-permute-done.10 = f32[2,8,256]{2,1,0:T(8,128)S(1)} collective-permute-done((f32[2,8,256]{2,1,0:T(8,128)S(1)}, f32[2,8,256]{2,1,0:T(8,128)S(1)}, u32[]{:S(2)}, u32[]{:S(2)}) %collective-permute-start.10) | collective-permute-done | bytes 16416 | tf_op jit(solution)/shard_map/ppermute | solution.py:295
  48.5 3.7 %collective-permute-done.11 = f32[2,8,256]{2,1,0:T(8,128)S(1)} collective-permute-done((f32[2,8,256]{2,1,0:T(8,128)S(1)}, f32[2,8,256]{2,1,0:T(8,128)S(1)}, u32[]{:S(2)}, u32[]{:S(2)}) %collective-permute-start.11) | collective-permute-done | bytes 16416 | tf_op jit(solution)/shard_map/ppermute | solution.py:295
  52.2 1.0 %cache_gradients.1 = (bf16[128,640]{1,0:T(8,128)(2,1)}, bf16[128,640]{1,0:T(8,128)(2,1)}) custom-call(bf16[256,768]{1,0:T(8,128)(2,1)S(1)} %bitcast.42, bf16[256,640]{1,0:T(8,128)(2,1)S(1)} %bitcast.44, bf16[5,128,256]{2,1,0:T(8,128)(2,1)S(1)} %get-tuple-element.23.p_ref, bf16[5,128,256]{2,1,0:T(8,128)(2,1)S(1)} %get-tuple-element.24.ds_ref, ...), custom_call_target="tpu_custom_call" | custom-call | tf_op jit(solution)/shard_map/cache_gradients/pallas_call | solution.py:238
  53.3 1.4 %combine.1 = bf16[8,2560]{1,0:T(8,128)(2,1)} custom-call(bf16[4,8,8,768]{3,2,1,0:T(8,128)(2,1)S(1)} %bitcast.45), custom_call_target="tpu_custom_call" | custom-call | tf_op jit(solution)/shard_map/combine/pallas_call | solution.py:275
  (31 shorter events, 1.1 us)
Async XLA Ops:
  1.8 4.0 %collective-permute-start = (bf16[8,1408]{1,0:T(8,128)(2,1)S(1)}, bf16[8,1408]{1,0:T(8,128)(2,1)S(1)}, u32[]{:S(2)}, u32[]{:S(2)}) collective-permute-start(bf16[8,1408]{1,0:T(8,128)(2,1)S(1)} %get-tuple-element.16), channel_id=1, source_target_pairs={{0,24},{8,16},{16,8},{24,0},{1,25},{9,17},{17,9},{25,1},{2,26},{10... | collective-permute-start | bytes 67592 | tf_op jit(solution)/shard_map/ppermute | solution.py:295
  4.2 3.8 %collective-permute-start.1 = (bf16[8,1408]{1,0:T(8,128)(2,1)S(1)}, bf16[8,1408]{1,0:T(8,128)(2,1)S(1)}, u32[]{:S(2)}, u32[]{:S(2)}) collective-permute-start(bf16[8,1408]{1,0:T(8,128)(2,1)S(1)} %get-tuple-element.17), channel_id=1, source_target_pairs={{0,16},{8,24},{16,0},{24,8},{1,17},{9,25},{17,1},{25,9},{2,18},{10... | collective-permute-start | bytes 67592 | tf_op jit(solution)/shard_map/ppermute | solution.py:295
  4.9 3.2 %collective-permute-start.2 = (bf16[8,1408]{1,0:T(8,128)(2,1)S(1)}, bf16[8,1408]{1,0:T(8,128)(2,1)S(1)}, u32[]{:S(2)}, u32[]{:S(2)}) collective-permute-start(bf16[8,1408]{1,0:T(8,128)(2,1)S(1)} %get-tuple-element.18), channel_id=1, source_target_pairs={{0,8},{8,0},{16,24},{24,16},{1,9},{9,1},{17,25},{25,17},{2,10},{10... | collective-permute-start | bytes 67592 | tf_op jit(solution)/shard_map/ppermute | solution.py:295
  8.1 5.0 %collective-permute-start.6 = (bf16[4,8,640]{2,1,0:T(8,128)(2,1)S(1)}, bf16[4,8,640]{2,1,0:T(8,128)(2,1)S(1)}, u32[]{:S(2)}, u32[]{:S(2)}) collective-permute-start(bf16[4,8,640]{2,1,0:T(8,128)(2,1)S(1)} %pad_maximum_fusion.7), channel_id=1, source_target_pairs={{0,4},{1,5},{2,6},{3,7},{4,0},{5,1},{6,2},{7,3},{8,12},{9,13},{10,... | collective-permute-start | bytes 122888 | tf_op jit(solution)/shard_map/ppermute | solution.py:295
  10.8 5.1 %collective-permute-start.3 = (bf16[4,8,768]{2,1,0:T(8,128)(2,1)S(1)}, bf16[4,8,768]{2,1,0:T(8,128)(2,1)S(1)}, u32[]{:S(2)}, u32[]{:S(2)}) collective-permute-start(bf16[4,8,768]{2,1,0:T(8,128)(2,1)S(1)} %slice.44), channel_id=1, source_target_pairs={{0,4},{1,5},{2,6},{3,7},{4,0},{5,1},{6,2},{7,3},{8,12},{9,13},{10,... | collective-permute-start | bytes 147464 | tf_op jit(solution)/shard_map/ppermute | solution.py:295
  13.1 4.5 %collective-permute-start.7 = (bf16[4,2,8,640]{3,2,0,1:T(8,128)(2,1)S(1)}, bf16[4,2,8,640]{3,2,0,1:T(8,128)(2,1)S(1)}, u32[]{:S(2)}, u32[]{:S(2)}) collective-permute-start(bf16[4,2,8,640]{3,2,0,1:T(8,128)(2,1)S(1)} %pad_maximum_fusion.6), channel_id=1, source_target_pairs={{0,1},{1,0},{2,3},{3,2},{4,5},{5,4},{6,7},{7,6},{8,9},{9,8},{10,11... | collective-permute-start | bytes 245768 | tf_op jit(solution)/shard_map/ppermute | solution.py:295
  15.9 5.1 %collective-permute-start.4 = (bf16[4,2,8,768]{3,2,0,1:T(8,128)(2,1)S(1)}, bf16[4,2,8,768]{3,2,0,1:T(8,128)(2,1)S(1)}, u32[]{:S(2)}, u32[]{:S(2)}) collective-permute-start(bf16[4,2,8,768]{3,2,0,1:T(8,128)(2,1)S(1)} %pad_maximum_fusion.4), channel_id=1, source_target_pairs={{0,2},{1,3},{2,0},{3,1},{4,6},{5,7},{6,4},{7,5},{8,10},{9,11},{10,... | collective-permute-start | bytes 294920 | tf_op jit(solution)/shard_map/ppermute | solution.py:295
  17.7 5.4 %collective-permute-start.8 = (bf16[4,2,2,8,640]{4,3,0,1,2:T(8,128)(2,1)S(1)}, bf16[4,2,2,8,640]{4,3,0,1,2:T(8,128)(2,1)S(1)}, u32[]{:S(2)}, u32[]{:S(2)}) collective-permute-start(bf16[4,2,2,8,640]{4,3,0,1,2:T(8,128)(2,1)S(1)} %pad_maximum_fusion.3), channel_id=1, source_target_pairs={{0,2},{1,3},{2,0},{3,1},{4,6},{5,7},{6,4},{7,5},{8,10},{9,11},{10,... | collective-permute-start | bytes 491528 | tf_op jit(solution)/shard_map/ppermute | solution.py:295
  21.0 5.9 %collective-permute-start.5 = (bf16[4,2,2,8,768]{4,3,0,1,2:T(8,128)(2,1)S(1)}, bf16[4,2,2,8,768]{4,3,0,1,2:T(8,128)(2,1)S(1)}, u32[]{:S(2)}, u32[]{:S(2)}) collective-permute-start(bf16[4,2,2,8,768]{4,3,0,1,2:T(8,128)(2,1)S(1)} %pad_maximum_fusion.2), channel_id=1, source_target_pairs={{0,1},{1,0},{2,3},{3,2},{4,5},{5,4},{6,7},{7,6},{8,9},{9,8},{10,11... | collective-permute-start | bytes 589832 | tf_op jit(solution)/shard_map/ppermute | solution.py:295
  27.4 8.1 %collective-permute-start.9 = (f32[2,8,256]{2,1,0:T(8,128)S(1)}, f32[2,8,256]{2,1,0:T(8,128)S(1)}, u32[]{:S(2)}, u32[]{:S(2)}) collective-permute-start(f32[2,8,256]{2,1,0:T(8,128)S(1)} %stats.1.l_ref.own_ref), channel_id=1, source_target_pairs={{0,1},{1,0},{2,3},{3,2},{4,5},{5,4},{6,7},{7,6},{8,9},{9,8},{10,11... | collective-permute-start | bytes 49160 | tf_op jit(solution)/shard_map/ppermute | solution.py:295
  31.3 22.0 %all-to-all-start = ((bf16[32,8,768]{2,1,0:T(8,128)(2,1)}), bf16[32,8,768]{2,1,0:T(8,128)(2,1)S(1)}, u32[]{:S(2)}, u32[]{:S(2)}) async-start(bf16[32,8,768]{2,1,0:T(8,128)(2,1)} %bitcast.46), calls=%async_computation | async-start | bytes 786432 | tf_op jit(solution)/shard_map/all_to_all | solution.py:331
  35.6 12.8 %collective-permute-start.10 = (f32[2,8,256]{2,1,0:T(8,128)S(1)}, f32[2,8,256]{2,1,0:T(8,128)S(1)}, u32[]{:S(2)}, u32[]{:S(2)}) collective-permute-start(f32[2,8,256]{2,1,0:T(8,128)S(1)} %pad_maximum_fusion.8), channel_id=1, source_target_pairs={{0,4},{1,5},{2,6},{3,7},{4,0},{5,1},{6,2},{7,3},{8,12},{9,13},{10,... | collective-permute-start | bytes 49160 | tf_op jit(solution)/shard_map/ppermute | solution.py:295
  48.4 3.8 %collective-permute-start.11 = (f32[2,8,256]{2,1,0:T(8,128)S(1)}, f32[2,8,256]{2,1,0:T(8,128)S(1)}, u32[]{:S(2)}, u32[]{:S(2)}) collective-permute-start(f32[2,8,256]{2,1,0:T(8,128)S(1)} %pad_maximum_fusion.9), channel_id=1, source_target_pairs={{0,2},{1,3},{2,0},{3,1},{4,6},{5,7},{6,4},{7,5},{8,10},{9,11},{10,... | collective-permute-start | bytes 49160 | tf_op jit(solution)/shard_map/ppermute | solution.py:295
